TPU v7x, 32 devices: a whole 2x2x4 slice. The times are simulated.
32 devices in a mesh: dp: 8 (over z, x), tensor: 4 (over y, core).
Axes of the slice: x: 2, y: 2, z: 4, core: 2. Of those that a mesh axis runs over, the one named last changes fastest.
Arguments:
- inputs: bfloat16 [1500, 8, 1024], P('tensor', 'dp'), may hold values from -6 to 6
- segments: int32 [8, 1500], P('dp'), may hold values from 0 to 3, never falling along the last dimension, each value on 1 to 750 neighbouring positions
- cotangent: bfloat16 [1500, 8, 1024], P('tensor', 'dp'), may hold values from -6 to 6
- gain_one: float32 [1024], replicated, may hold values from 0.1 to 1.9
- first_in: bfloat16 [1024, 4096], P(None, 'tensor'), may hold values from -0.1875 to 0.1875
- first_out: bfloat16 [4096, 1024], P('tensor'), may hold values from -0.1875 to 0.1875
- gain_two: float32 [1024], replicated, may hold values from 0.1 to 1.9
- w_query: bfloat16 [1024, 1024], P(None, 'tensor'), may hold values from -0.1875 to 0.1875
- w_key: bfloat16 [1024, 1024], P(None, 'tensor'), may hold values from -0.1875 to 0.1875
- w_value: bfloat16 [1024, 1024], P(None, 'tensor'), may hold values from -0.1875 to 0.1875
- w_output: bfloat16 [1024, 1024], P('tensor'), may hold values from -0.75 to 0.75
- rel_table: float32 [16, 257], P('tensor'), may hold values from -4 to 4
- gain_three: float32 [1024], replicated, may hold values from 0.1 to 1.9
- w_glu: bfloat16 [1024, 2, 1024], P(None, None, 'tensor'), may hold values from -0.1875 to 0.1875
- kernel: float32 [31, 1024], P(None, 'tensor'), may hold values from -1 to 1
- w_back: bfloat16 [1024, 1024], P('tensor'), may hold values from -0.5 to 0.5
- gain_four: float32 [1024], replicated, may hold values from 0.1 to 1.9
- second_in: bfloat16 [1024, 4096], P(None, 'tensor'), may hold values from -0.1875 to 0.1875
- second_out: bfloat16 [4096, 1024], P('tensor'), may hold values from -0.1875 to 0.1875
- gain_five: float32 [1024], replicated, may hold values from 0.1 to 1.9
Outputs:
- output: bfloat16 [1500, 8, 1024], P('tensor', 'dp')
- grad_inputs: float32 [1500, 8, 1024], P('tensor', 'dp')
- grad_gain_one: float32 [1024], replicated
- grad_first_in: float32 [1024, 4096], P('dp', 'tensor')
- grad_first_out: float32 [4096, 1024], P('tensor', 'dp')
- grad_gain_two: float32 [1024], replicated
- grad_w_query: float32 [1024, 1024], P('dp', 'tensor')
- grad_w_key: float32 [1024, 1024], P('dp', 'tensor')
- grad_w_value: float32 [1024, 1024], P('dp', 'tensor')
- grad_w_output: float32 [1024, 1024], P('tensor', 'dp')
- grad_rel_table: float32 [16, 257], P('tensor')
- grad_gain_three: float32 [1024], replicated
- grad_w_glu: float32 [1024, 2, 1024], P('dp', None, 'tensor')
- grad_kernel: float32 [31, 1024], P(None, 'tensor')
- grad_w_back: float32 [1024, 1024], P('tensor', 'dp')
- grad_gain_four: float32 [1024], replicated
- grad_second_in: float32 [1024, 4096], P('dp', 'tensor')
- grad_second_out: float32 [4096, 1024], P('tensor', 'dp')
- grad_gain_five: float32 [1024], replicated
Inputs may be any that keep to these rules, and one draw needn't show every extreme that they name: `segments`: within each row of 1500 frames the segment numbers start at 0 and never fall; each of the 4 utterances holds 1 to 750 frames, and one holds exactly 750.
All inputs are finite; a program needn't handle non-finite values.
Results may differ from a plain program's by a relative error of at most 0.03.
Values may be sent and summed in bfloat16 or wider, within the bound.
No kernel may reach another device: no remote copies, remote signals or barrier semaphores. Data moves between devices by JAX's collectives and lax.ppermute only.
A program may use at most 256 MiB of HBM per device.

v0:
```python
import jax
import jax.numpy as jnp
from jax import lax
from jax.sharding import PartitionSpec as P

masked_score = -1e30


def normed(residual, gain_vec):
    row_mean = jnp.mean(residual, axis=-1, keepdims=True)
    centred = residual - row_mean
    variance = jnp.mean(centred * centred, axis=-1, keepdims=True)
    return centred * lax.rsqrt(variance + 1e-05) * gain_vec


def depthwise(values, kernel, labels):
    kernel_len = kernel.shape[0]
    half_width = kernel_len // 2
    frames = values.shape[0]
    padded = jnp.pad(values, ((half_width, half_width),) + ((0, 0),) * (values.ndim - 1))
    padded_labels = jnp.pad(
        labels, ((half_width, half_width),) + ((0, 0),) * (labels.ndim - 1), constant_values=-1
    )
    summed = jnp.zeros_like(values)
    for offset in range(kernel_len):
        same_seg = (padded_labels[offset : offset + frames] == labels)[..., None]
        summed = summed + jnp.where(
            same_seg, padded[offset : offset + frames] * kernel[offset], 0.0
        )
    return summed


def rel_band(table_row, frames):
    reach_max = table_row.shape[0] // 2
    distance = jnp.arange(2 * frames, dtype=jnp.int32) - (frames - 1)
    column = jnp.clip(distance, -reach_max, reach_max) + reach_max
    onehot = (column[None, :] == jnp.arange(table_row.shape[0], dtype=jnp.int32)[:, None]).astype(
        jnp.float32
    )
    diagonal_vals = jnp.dot(
        table_row, onehot, precision=lax.Precision.HIGHEST, preferred_element_type=jnp.float32
    )
    tiled = jnp.tile(diagonal_vals, frames)[: frames * (2 * frames - 1)]
    return tiled.reshape(frames, 2 * frames - 1)[:, frames - 1 :]


def gated_conv(glu_input, kernel, labels):
    channels = kernel.shape[1]
    gated = glu_input[..., :channels] * jax.nn.sigmoid(glu_input[..., channels:])
    return jax.nn.silu(depthwise(gated, kernel, labels))


def share_frames(local_rows):
    return lax.all_gather(local_rows, "tensor", axis=0, tiled=True)


def share_grads(local_rows):
    return lax.all_gather(local_rows, "tensor", axis=0, tiled=True)


def products(operands, transposed):
    summed = 0.0
    for operand, weight in operands:
        if transposed:
            summed = summed + jnp.einsum(
                "src,dc->srd", operand, weight, preferred_element_type=jnp.float32
            )
        else:
            summed = summed + jnp.einsum(
                "src,cd->srd", operand, weight, preferred_element_type=jnp.float32
            )
    return summed


def forward_sum(operands):
    return lax.psum_scatter(
        products(operands, False).astype(jnp.bfloat16), "tensor", scatter_dimension=0, tiled=True
    ).astype(jnp.float32)


def backward_sum(operands):
    return lax.psum_scatter(
        products(operands, True).astype(jnp.bfloat16), "tensor", scatter_dimension=0, tiled=True
    ).astype(jnp.float32)


def settle(grad_in, grad_out):
    return (
        lax.psum_scatter(grad_in, "dp", scatter_dimension=0, tiled=True),
        lax.psum_scatter(grad_out, "dp", scatter_dimension=1, tiled=True),
    )


def per_head(array, row_count, head_count):
    frames = array.shape[0]
    head_width = array.shape[2] // head_count
    return (
        array.reshape(frames, row_count, head_count, head_width)
        .transpose(1, 2, 0, 3)
        .reshape(row_count * head_count, frames, head_width)
    )


def per_frame(array, row_count, head_count):
    entries, frames, head_width = array.shape
    return (
        array.reshape(row_count, head_count, frames, head_width)
        .transpose(2, 0, 1, 3)
        .reshape(frames, row_count, head_count * head_width)
    )


def head_scores(query_head, key_head, rel_bias, label_row):
    score_scale = query_head.shape[-1] ** (-0.5)
    raw_scores = (
        jnp.einsum("qd,kd->qk", query_head, key_head, preferred_element_type=jnp.float32)
        * score_scale
        + rel_bias
    )
    allowed = label_row[:, None] == label_row[None, :]
    return jnp.where(allowed, raw_scores, masked_score)


def feed_forward(residual, gain_vec, w_in, w_out):
    local_rows = normed(residual, gain_vec).astype(jnp.bfloat16)
    gathered = share_frames(local_rows)
    hidden = jnp.einsum("srd,df->srf", gathered, w_in, preferred_element_type=jnp.float32)
    active = jax.nn.silu(hidden).astype(jnp.bfloat16)
    branch = forward_sum(((active, w_out),))
    return (residual + 0.5 * branch, (gathered, hidden, active))


def feed_back(incoming, residual, gain_vec, w_in, w_out, state):
    stored, hidden, active = state
    grad_branch = share_grads((0.5 * incoming).astype(jnp.bfloat16))
    grad_w_out = jnp.einsum("srf,srd->fd", active, grad_branch, preferred_element_type=jnp.float32)
    grad_active = jnp.einsum("srd,fd->srf", grad_branch, w_out, preferred_element_type=jnp.float32)
    sigmoid_vals = jax.nn.sigmoid(hidden)
    grad_hidden = (grad_active * sigmoid_vals * (1.0 + hidden * (1.0 - sigmoid_vals))).astype(
        jnp.bfloat16
    )
    grad_w_in = jnp.einsum("srd,srf->df", stored, grad_hidden, preferred_element_type=jnp.float32)
    grad_normed = backward_sum(((grad_hidden, w_in),))
    norm_value, norm_pull = jax.vjp(normed, residual, gain_vec)
    grad_residual, grad_gain = norm_pull(grad_normed)
    return (incoming + grad_residual, grad_gain, grad_w_in, grad_w_out)


def attention(residual, gain_vec, w_query, w_key, w_value, w_output, rel_table, segments):
    local_rows = normed(residual, gain_vec).astype(jnp.bfloat16)
    gathered = share_frames(local_rows)
    frames, row_count = (gathered.shape[0], gathered.shape[1])
    head_count = rel_table.shape[0]

    def project(weight):
        projected = jnp.einsum("srd,dc->src", gathered, weight, preferred_element_type=jnp.float32)
        return per_head(projected.astype(jnp.bfloat16), row_count, head_count)

    query_rows, key_rows, value_rows = (project(w_query), project(w_key), project(w_value))
    tables = jnp.tile(rel_table, (row_count, 1))
    labels = jnp.repeat(segments, head_count, axis=0)

    def one_head(record):
        query_head, key_head, value_head, table_row, label_row = record
        scores = head_scores(query_head, key_head, rel_band(table_row, frames), label_row)
        row_max = jnp.max(scores, axis=-1, keepdims=True)
        log_total = row_max + jnp.log(jnp.sum(jnp.exp(scores - row_max), axis=-1, keepdims=True))
        attend = jnp.exp(scores - log_total).astype(jnp.bfloat16)
        mixed = jnp.einsum("qk,kd->qd", attend, value_head, preferred_element_type=jnp.float32)
        return (mixed.astype(jnp.bfloat16), log_total[:, 0])

    attended, log_totals = lax.map(one_head, (query_rows, key_rows, value_rows, tables, labels))
    attended = per_frame(attended, row_count, head_count)
    branch = forward_sum(((attended, w_output),))
    return (residual + branch, (gathered, query_rows, key_rows, value_rows, attended, log_totals))


def attention_back(
    incoming, residual, gain_vec, w_query, w_key, w_value, w_output, rel_table, segments, state
):
    stored, query_rows, key_rows, value_rows, attended, log_totals = state
    frames, row_count = (stored.shape[0], stored.shape[1])
    head_count = rel_table.shape[0]
    grad_branch = share_grads(incoming.astype(jnp.bfloat16))
    grad_w_output = jnp.einsum(
        "src,srd->cd", attended, grad_branch, preferred_element_type=jnp.float32
    )
    grad_mixed = jnp.einsum(
        "srd,cd->src", grad_branch, w_output, preferred_element_type=jnp.float32
    )
    grad_mixed = per_head(grad_mixed.astype(jnp.bfloat16), row_count, head_count)
    tables = jnp.tile(rel_table, (row_count, 1))
    labels = jnp.repeat(segments, head_count, axis=0)

    def one_head(record):
        query_head, key_head, value_head, table_row, label_row, log_total, grad_head = record
        score_scale = query_head.shape[-1] ** (-0.5)
        rel_bias, band_pull = jax.vjp(lambda table_vals: rel_band(table_vals, frames), table_row)
        scores = head_scores(query_head, key_head, rel_bias, label_row)
        attend = jnp.exp(scores - log_total[:, None])
        grad_value = jnp.einsum(
            "qk,qd->kd", attend.astype(jnp.bfloat16), grad_head, preferred_element_type=jnp.float32
        )
        grad_attend = jnp.einsum(
            "qd,kd->qk", grad_head, value_head, preferred_element_type=jnp.float32
        )
        grad_scores = attend * (grad_attend - jnp.sum(attend * grad_attend, axis=-1, keepdims=True))
        grad_scores = grad_scores.astype(jnp.bfloat16)
        grad_query = (
            jnp.einsum("qk,kd->qd", grad_scores, key_head, preferred_element_type=jnp.float32)
            * score_scale
        )
        grad_key = (
            jnp.einsum("qk,qd->kd", grad_scores, query_head, preferred_element_type=jnp.float32)
            * score_scale
        )
        grad_table = band_pull(grad_scores.astype(jnp.float32))[0]
        return (
            grad_query.astype(jnp.bfloat16),
            grad_key.astype(jnp.bfloat16),
            grad_value.astype(jnp.bfloat16),
            grad_table,
        )

    grad_queries, grad_keys, grad_values, grad_tables = lax.map(
        one_head, (query_rows, key_rows, value_rows, tables, labels, log_totals, grad_mixed)
    )
    grad_queries = per_frame(grad_queries, row_count, head_count)
    grad_keys = per_frame(grad_keys, row_count, head_count)
    grad_values = per_frame(grad_values, row_count, head_count)
    grad_table = jnp.sum(grad_tables.reshape(row_count, head_count, grad_tables.shape[-1]), axis=0)
    stacked = jnp.stack([grad_queries, grad_keys, grad_values], axis=2)
    grad_projections = jnp.einsum(
        "srd,srtc->dtc", stored, stacked, preferred_element_type=jnp.float32
    )
    grad_normed = backward_sum(
        ((grad_queries, w_query), (grad_keys, w_key), (grad_values, w_value))
    )
    norm_value, norm_pull = jax.vjp(normed, residual, gain_vec)
    grad_residual, grad_gain = norm_pull(grad_normed)
    return (incoming + grad_residual, grad_gain, grad_table, grad_projections, grad_w_output)


def convolution(residual, gain_vec, w_glu, kernel, w_back, labels):
    local_rows = normed(residual, gain_vec).astype(jnp.bfloat16)
    gathered = share_frames(local_rows)
    channels = kernel.shape[1]
    glu_input = jnp.einsum(
        "srd,dc->src",
        gathered,
        w_glu.reshape(w_glu.shape[0], 2 * channels),
        preferred_element_type=jnp.float32,
    )
    active = gated_conv(glu_input, kernel, labels).astype(jnp.bfloat16)
    branch = forward_sum(((active, w_back),))
    return (residual + branch, (gathered, glu_input))


def convolution_back(incoming, residual, gain_vec, w_glu, kernel, w_back, labels, state):
    stored, glu_input = state
    channels = kernel.shape[1]
    width = w_glu.shape[0]
    glu_matrix = w_glu.reshape(width, 2 * channels)
    grad_branch = share_grads(incoming.astype(jnp.bfloat16))
    conv_value, conv_pull = jax.vjp(
        lambda glu_vals, taps: gated_conv(glu_vals, taps, labels), glu_input, kernel
    )
    active = conv_value.astype(jnp.bfloat16)
    grad_w_back = jnp.einsum("src,srd->cd", active, grad_branch, preferred_element_type=jnp.float32)
    grad_active = jnp.einsum("srd,cd->src", grad_branch, w_back, preferred_element_type=jnp.float32)
    grad_glu_input, grad_kernel = conv_pull(grad_active)
    grad_glu_input = grad_glu_input.astype(jnp.bfloat16)
    grad_w_glu = jnp.einsum(
        "srd,src->dc", stored, grad_glu_input, preferred_element_type=jnp.float32
    ).reshape(width, 2, channels)
    grad_normed = backward_sum(((grad_glu_input, glu_matrix),))
    norm_value, norm_pull = jax.vjp(normed, residual, gain_vec)
    grad_residual, grad_gain = norm_pull(grad_normed)
    return (incoming + grad_residual, grad_gain, grad_kernel, grad_w_glu, grad_w_back)


def shards(
    inputs,
    segments,
    cotangent,
    gain_one,
    first_in,
    first_out,
    gain_two,
    w_query,
    w_key,
    w_value,
    w_output,
    rel_table,
    gain_three,
    w_glu,
    kernel,
    w_back,
    gain_four,
    second_in,
    second_out,
    gain_five,
):
    frame_labels = segments.T
    start_frames = inputs.astype(jnp.float32)
    after_one, state_one = feed_forward(start_frames, gain_one, first_in, first_out)
    after_two, state_two = attention(
        after_one, gain_two, w_query, w_key, w_value, w_output, rel_table, segments
    )
    after_three, state_three = convolution(
        after_two, gain_three, w_glu, kernel, w_back, frame_labels
    )
    after_four, state_four = feed_forward(after_three, gain_four, second_in, second_out)
    final_rows, final_pull = jax.vjp(normed, after_four, gain_five)
    output = final_rows.astype(jnp.bfloat16)
    incoming, grad_five = final_pull(cotangent.astype(jnp.float32))
    incoming, grad_four, grad_second_in, grad_second_out = feed_back(
        incoming, after_three, gain_four, second_in, second_out, state_four
    )
    grad_second_in, grad_second_out = settle(grad_second_in, grad_second_out)
    incoming, grad_three, grad_kernel, grad_w_glu, grad_w_back = convolution_back(
        incoming, after_two, gain_three, w_glu, kernel, w_back, frame_labels, state_three
    )
    grad_w_glu, grad_w_back = settle(grad_w_glu, grad_w_back)
    incoming, grad_two, grad_table, grad_projections, grad_w_output = attention_back(
        incoming,
        after_one,
        gain_two,
        w_query,
        w_key,
        w_value,
        w_output,
        rel_table,
        segments,
        state_two,
    )
    grad_projections, grad_w_output = settle(grad_projections, grad_w_output)
    incoming, grad_one, grad_first_in, grad_first_out = feed_back(
        incoming, start_frames, gain_one, first_in, first_out, state_one
    )
    grad_first_in, grad_first_out = settle(grad_first_in, grad_first_out)
    grad_table, grad_kernel = lax.psum((grad_table, grad_kernel), "dp")
    grad_one, grad_two, grad_three, grad_four, grad_five = lax.psum(
        (grad_one, grad_two, grad_three, grad_four, grad_five), ("dp", "tensor")
    )
    return (
        output,
        incoming,
        grad_one,
        grad_first_in,
        grad_first_out,
        grad_two,
        grad_projections[:, 0],
        grad_projections[:, 1],
        grad_projections[:, 2],
        grad_w_output,
        grad_table,
        grad_three,
        grad_w_glu,
        grad_kernel,
        grad_w_back,
        grad_four,
        grad_second_in,
        grad_second_out,
        grad_five,
    )


def solution(mesh):
    in_specs = (
        P("tensor", "dp", None),
        P("dp", None),
        P("tensor", "dp", None),
        P(),
        P(None, "tensor"),
        P("tensor", None),
        P(),
        P(None, "tensor"),
        P(None, "tensor"),
        P(None, "tensor"),
        P("tensor", None),
        P("tensor", None),
        P(),
        P(None, None, "tensor"),
        P(None, "tensor"),
        P("tensor", None),
        P(),
        P(None, "tensor"),
        P("tensor", None),
        P(),
    )
    out_specs = (
        P("tensor", "dp", None),
        P("tensor", "dp", None),
        P(),
        P("dp", "tensor"),
        P("tensor", "dp"),
        P(),
        P("dp", "tensor"),
        P("dp", "tensor"),
        P("dp", "tensor"),
        P("tensor", "dp"),
        P("tensor", None),
        P(),
        P("dp", None, "tensor"),
        P(None, "tensor"),
        P("tensor", "dp"),
        P(),
        P("dp", "tensor"),
        P("tensor", "dp"),
        P(),
    )
    return jax.shard_map(shards, mesh=mesh, in_specs=in_specs, out_specs=out_specs, check_vma=False)
```

profile of v0, /device:TPU:0, one launch (start us, length us, event | category | flops | bytes accessed | tf_op | source)
XLA Modules:
  0.0 2913.9 jit_solution(12028822160477935282)
XLA Ops:
  20.7 48.4 %all-gather.9.cloned.1.call-done = bf16[1500,1,1024]{2,1,0:T(2,128)(2,1)} async-done(((bf16[375,1,1024]{2,1,0:T(2,128)(2,1)}), bf16[1500,1,1024]{2,1,0:T(2,128)(2,1)}) %all-gather.9.cloned.1.call-update) | async-done | bytes 3072016 | tf_op jit(solution)/shard_map/all_gather | solution.py:54
  83.4 30.9 %fusion = bf16[376,1024]{1,0:T(8,128)(2,1)S(1)} fusion(bf16[1500,1,1024]{2,0,1:T(8,128)(2,1)} %fusion.77), kind=kCustom, calls=%all-reduce-scatter | all-reduce-scatter fusion | flops 1540097 | bytes 3842560
  141.4 48.1 %all-gather.11.cloned.1.call-done = bf16[1500,1,1024]{2,1,0:T(2,128)(2,1)} async-done(((bf16[375,1,1024]{2,1,0:T(2,128)(2,1)}), bf16[1500,1,1024]{2,1,0:T(2,128)(2,1)}) %all-gather.11.cloned.1.call-update) | async-done | bytes 3072016 | tf_op jit(solution)/shard_map/all_gather | solution.py:54
  213.3 417.3 %while.32 = (s32[]{:T(128)}, bf16[4,1500,64]{1,2,0:T(8,128)(2,1)S(1)}, f32[4,1500]{1,0:T(4,128)S(1)}, s32[4,1500]{1,0:T(4,128)S(1)}, bf16[4,1500,64]{2,1,0:T(8,1...) while((s32[]{:T(128)}, ...), condition=%wide.region_8.9_spmd, body=%wide.region_5.8_spmd.sunk | while | flops 606376448 | bytes 199957408 | solution.py:172
  635.3 30.8 %fusion.1 = bf16[376,1024]{1,0:T(8,128)(2,1)S(1)} fusion(bf16[1500,1,1024]{2,0,1:T(8,128)(2,1)} %fusion.74), kind=kCustom, calls=%all-reduce-scatter.1 | all-reduce-scatter fusion | flops 1540097 | bytes 3842560
  689.4 46.0 %all-gather.13.cloned.1.call-done = bf16[1500,1,1024]{2,1,0:T(2,128)(2,1)} async-done(((bf16[375,1,1024]{2,1,0:T(2,128)(2,1)}), bf16[1500,1,1024]{2,1,0:T(2,128)(2,1)}) %all-gather.13.cloned.1.call-update) | async-done | bytes 3072016 | tf_op jit(solution)/shard_map/all_gather | solution.py:54
  757.6 31.5 %fusion.2 = bf16[376,1024]{1,0:T(8,128)(2,1)} fusion(bf16[1500,1,1024]{2,0,1:T(8,128)(2,1)} %fusion.75), kind=kCustom, calls=%all-reduce-scatter.2 | all-reduce-scatter fusion | flops 1540097 | bytes 3842560
  815.9 49.6 %all-gather.15.cloned.1.call-done = bf16[1500,1,1024]{2,1,0:T(2,128)(2,1)} async-done(((bf16[375,1,1024]{2,1,0:T(2,128)(2,1)}), bf16[1500,1,1024]{2,1,0:T(2,128)(2,1)}) %all-gather.15.cloned.1.call-update) | async-done | bytes 3072016 | tf_op jit(solution)/shard_map/all_gather | solution.py:54
  880.0 30.8 %fusion.3 = bf16[376,1024]{1,0:T(8,128)(2,1)S(1)} fusion(bf16[1500,1,1024]{2,0,1:T(8,128)(2,1)} %fusion.78), kind=kCustom, calls=%all-reduce-scatter.3 | all-reduce-scatter fusion | flops 1540097 | bytes 3842560
  945.4 49.6 %all-gather.17.cloned.1.call-done = bf16[1500,1,1024]{2,1,0:T(2,128)(2,1)} async-done(((bf16[375,1,1024]{2,1,0:T(2,128)(2,1)}), bf16[1500,1,1024]{2,1,0:T(2,128)(2,1)}) %all-gather.17.cloned.1.call-update) | async-done | bytes 3072016 | tf_op jit(solution)/shard_map/all_gather | solution.py:58
  1010.9 30.8 %fusion.4 = bf16[376,1024]{1,0:T(8,128)(2,1)S(1)} fusion(bf16[1500,1,1024]{2,0,1:T(8,128)(2,1)} %fusion.79), kind=kCustom, calls=%all-reduce-scatter.4 | all-reduce-scatter fusion | flops 1540097 | bytes 3842560
  1067.4 49.6 %all-gather.19.cloned.1.call-done = bf16[1500,1,1024]{2,1,0:T(2,128)(2,1)} async-done(((bf16[375,1,1024]{2,1,0:T(2,128)(2,1)}), bf16[1500,1,1024]{2,1,0:T(2,128)(2,1)}) %all-gather.19.cloned.1.call-update) | async-done | bytes 3072016 | tf_op jit(solution)/shard_map/all_gather | solution.py:58
  1185.5 30.8 %fusion.5 = bf16[376,1024]{1,0:T(8,128)(2,1)S(1)} fusion(bf16[1500,1,1024]{2,0,1:T(8,128)(2,1)} %fusion.73), kind=kCustom, calls=%all-reduce-scatter.5 | all-reduce-scatter fusion | flops 1540097 | bytes 3842560
  1242.2 49.6 %all-gather.21.cloned.1.call-done = bf16[1500,1,1024]{2,1,0:T(2,128)(2,1)} async-done(((bf16[375,1,1024]{2,1,0:T(2,128)(2,1)}), bf16[1500,1,1024]{2,1,0:T(2,128)(2,1)}) %all-gather.21.cloned.1.call-update) | async-done | bytes 3072016 | tf_op jit(solution)/shard_map/all_gather | solution.py:58
  1298.9 841.6 %while.33 = (s32[]{:T(128)}, bf16[4,1500,64]{1,2,0:T(8,128)(2,1)}, bf16[4,1500,64]{1,2,0:T(8,128)(2,1)}, bf16[4,1500,64]{1,2,0:T(8,128)(2,1)}, f32[4,257]{1,0:T(...) while((s32[]{:T(128)}, bf16[4,1500,64]{1,2,0:T(8,128)(2,1)}, ...), condition=%wide.region_29.30_spmd, body=%wide.region_26.29_spmd.sunk | while | flops 1494280448 | bytes 381868960 | solution.py:225
  2147.9 30.8 %fusion.6 = bf16[376,1024]{1,0:T(8,128)(2,1)S(1)} fusion(bf16[1500,1,1024]{2,0,1:T(8,128)(2,1)} %fusion.76), kind=kCustom, calls=%all-reduce-scatter.6 | all-reduce-scatter fusion | flops 1540097 | bytes 3842560
  2321.6 33.9 %fusion.7 = bf16[376,1024]{1,0:T(8,128)(2,1)S(1)} fusion(bf16[1500,1,1024]{2,0,1:T(8,128)(2,1)} %fusion.80), kind=kCustom, calls=%all-reduce-scatter.7 | all-reduce-scatter fusion | flops 1540097 | bytes 3842560
  2359.0 38.5 %all-reduce.85 = (f32[4,257]{1,0:T(4,128)}, f32[31,256]{1,0:T(8,128)}) all-reduce(f32[4,257]{1,0:T(4,128)S(1)} %get-tuple-element.278, f32[31,256]{1,0:T(8,128)S(1)} %pad_add_fusion.7), channel_id=1, replica_groups=mesh['dp'=8,'tensor'=4] {'dp'}, use_global_device_ids=true, to_apply=%region_44.45 | all-reduce | flops 8964 | bytes 71712 | tf_op jit(solution)/shard_map/psum | solution.py:342
  2410.1 39.0 %all-reduce.84 = (f32[1024]{0:T(1024)}, f32[1024]{0:T(1024)}, f32[1024]{0:T(1024)}, f32[1024]{0:T(1024)}, f32[1024]{0:T(1024)}) all-reduce(f32[1024]{0:T(1024)S(1)} %get-tuple-element.454, f32[1024]{0:T(1024)S(1)} %get-tuple-element.452, f32[1024]{0:T(1024)S(1)} %copy-done.103, ...), channel_id=1, replica_groups=mesh['dp'=8,'tensor'=4] {'dp','tensor'}, use_global_device_ids=true, to_apply=%region_37.38 | all-reduce | flops 5120 | bytes 40960 | tf_op jit(solution)/shard_map/psum | solution.py:343
  2471.6 91.5 %reduce-scatter.45.cloned.1.call-done = f32[128,1024]{1,0:T(8,128)} async-done(((f32[1024,1024]{1,0:T(8,128)}), f32[128,1024]{1,0:T(8,128)}) %reduce-scatter.45.cloned.1.call-update) | async-done | bytes 524304 | tf_op jit(solution)/shard_map/reduce_scatter | solution.py:89
  2563.1 92.5 %reduce-scatter.47.cloned.1.call-done = f32[1024,128]{1,0:T(8,128)} async-done(((f32[1024,1024]{1,0:T(8,128)}), f32[1024,128]{1,0:T(8,128)}) %reduce-scatter.47.cloned.1.call-update) | async-done | bytes 524304 | tf_op jit(solution)/shard_map/reduce_scatter | solution.py:90
  2655.6 67.8 %reduce-scatter.39.cloned.1.call-done = f32[256,128]{1,0:T(8,128)} async-done(((f32[256,1024]{1,0:T(8,128)}), f32[256,128]{1,0:T(8,128)}) %reduce-scatter.39.cloned.1.call-update) | async-done | bytes 131088 | tf_op jit(solution)/shard_map/reduce_scatter | solution.py:90
  2723.4 91.0 %reduce-scatter.33.cloned.1.call-done = f32[128,1024]{1,0:T(8,128)} async-done(((f32[1024,1024]{1,0:T(8,128)}), f32[128,1024]{1,0:T(8,128)}) %reduce-scatter.33.cloned.1.call-update) | async-done | bytes 524304 | tf_op jit(solution)/shard_map/reduce_scatter | solution.py:89
  2814.4 92.8 %reduce-scatter.35.cloned.1.call-done = f32[1024,128]{1,0:T(8,128)} async-done(((f32[1024,1024]{1,0:T(8,128)}), f32[1024,128]{1,0:T(8,128)}) %reduce-scatter.35.cloned.1.call-update) | async-done | bytes 524304 | tf_op jit(solution)/shard_map/reduce_scatter | solution.py:90
  (619 shorter events, 1767.6 us)
Async XLA Ops:
  7.2 61.8 %all-gather.9.cloned.1.call-start = ((), (), s32[]{:S(2)}) async-start(), calls=%async_computation.8 | async-start | bytes 7680000 | tf_op jit(solution)/shard_map/all_gather | solution.py:54
  20.6 168.9 %all-gather.11.cloned.1.call-start = ((), (), s32[]{:S(2)}) async-start(), calls=%async_computation.9 | async-start | bytes 7680000 | tf_op jit(solution)/shard_map/all_gather | solution.py:54
  114.4 2.9 collective-permute-start
  140.7 594.7 %all-gather.13.cloned.1.call-start = ((), (), s32[]{:S(2)}) async-start(), calls=%async_computation.10 | async-start | bytes 7680000 | tf_op jit(solution)/shard_map/all_gather | solution.py:54
  666.1 2.1 collective-permute-start.1
  685.8 179.7 %all-gather.15.cloned.1.call-start = ((), (), s32[]{:S(2)}) async-start(), calls=%async_computation.11 | async-start | bytes 7680000 | tf_op jit(solution)/shard_map/all_gather | solution.py:54
  789.9 2.1 collective-permute-start.2
  815.9 179.2 %all-gather.17.cloned.1.call-start = ((), (), s32[]{:S(2)}) async-start(), calls=%async_computation.12 | async-start | bytes 7680000 | tf_op jit(solution)/shard_map/all_gather | solution.py:58
  910.9 2.1 collective-permute-start.3
  945.4 171.6 %all-gather.19.cloned.1.call-start = ((), (), s32[]{:S(2)}) async-start(), calls=%async_computation.13 | async-start | bytes 7680000 | tf_op jit(solution)/shard_map/all_gather | solution.py:58
  1041.8 2.2 collective-permute-start.4
  1067.4 224.4 %all-gather.21.cloned.1.call-start = ((), (), s32[]{:S(2)}) async-start(), calls=%async_computation.14 | async-start | bytes 7680000 | tf_op jit(solution)/shard_map/all_gather | solution.py:58
  1216.4 2.2 collective-permute-start.5
  1242.2 1020.0 %all-gather.23.cloned.1.call-start = ((), (), s32[]{:S(2)}) async-start(), calls=%async_computation.15 | async-start | bytes 7680000 | tf_op jit(solution)/shard_map/all_gather | solution.py:58
  2179.6 2.2 collective-permute-start.6
  2205.8 151.3 %reduce-scatter.41.cloned.1.call-start = ((), (), s32[]{:S(2)}) async-start(), calls=%async_computation.20 | async-start | bytes 2359296 | tf_op jit(solution)/shard_map/reduce_scatter | solution.py:89
  2219.8 238.4 %reduce-scatter.37.cloned.1.call-start = ((), (), s32[]{:S(2)}) async-start(), calls=%async_computation.18 | async-start | bytes 3538944 | tf_op jit(solution)/shard_map/reduce_scatter | solution.py:89
  2229.2 242.4 %reduce-scatter.43.cloned.1.call-start = ((), (), s32[]{:S(2)}) async-start(), calls=%async_computation.21 | async-start | bytes 1179648 | tf_op jit(solution)/shard_map/reduce_scatter | solution.py:90
  2235.9 327.3 %reduce-scatter.45.cloned.1.call-start = ((), (), s32[]{:S(2)}) async-start(), calls=%async_computation.22 | async-start | bytes 4718592 | tf_op jit(solution)/shard_map/reduce_scatter | solution.py:89
  2245.6 410.0 %reduce-scatter.47.cloned.1.call-start = ((), (), s32[]{:S(2)}) async-start(), calls=%async_computation.23 | async-start | bytes 4718592 | tf_op jit(solution)/shard_map/reduce_scatter | solution.py:90
  2256.1 467.3 %reduce-scatter.39.cloned.1.call-start = ((), (), s32[]{:S(2)}) async-start(), calls=%async_computation.19 | async-start | bytes 1179648 | tf_op jit(solution)/shard_map/reduce_scatter | solution.py:90
  2262.1 552.3 %reduce-scatter.33.cloned.1.call-start = ((), (), s32[]{:S(2)}) async-start(), calls=%async_computation.16 | async-start | bytes 4718592 | tf_op jit(solution)/shard_map/reduce_scatter | solution.py:89
  2282.0 625.2 %reduce-scatter.35.cloned.1.call-start = ((), (), s32[]{:S(2)}) async-start(), calls=%async_computation.17 | async-start | bytes 4718592 | tf_op jit(solution)/shard_map/reduce_scatter | solution.py:90
  2355.6 41.9 %collective-permute-start.7 = (bf16[3,1024]{1,0:T(4,128)(2,1)S(1)}, bf16[3,1024]{1,0:T(4,128)(2,1)S(1)}, u32[]{:S(2)}, u32[]{:S(2)}) collective-permute-start(bf16[3,1024]{1,0:T(4,128)(2,1)S(1)} %slice.522), channel_id=1, source_target_pairs={{0,1},{1,2},{2,3},{4,5},{5,6},{6,7},{8,9},{9,10},{10,11},{12,13},{... | collective-permute-start | bytes 18440
  (133 other events, 11711.0 us)
Sparse Core Ops, SparseCore 0:
  20.7 48.2 all-gather.8
  140.9 48.6 all-gather.10
  686.0 49.4 all-gather.12
  816.0 49.4 all-gather.14
  945.5 49.4 all-gather.16
  1067.5 49.4 all-gather.18
  1242.3 49.4 all-gather.20
  2205.9 49.4 all-gather.22
  2258.9 67.8 reduce-scatter.40
  2330.3 74.2 reduce-scatter.36
  2408.6 62.9 reduce-scatter.42
  2476.1 86.9 reduce-scatter.44
  2567.3 88.2 reduce-scatter.46
  2659.8 63.5 reduce-scatter.38
  2727.5 86.9 reduce-scatter.32
  2818.9 88.2 reduce-scatter.34
where the time goes:
time: 2930 us; the launch traced here: 2910 us
  local copies, waits for them, and re-layouts  1070 us (37%)
  waiting for transfers between devices  793 us (27%)
  other arithmetic  347 us (12%)
  blocking collectives  328 us (11%)
  matrix products  324 us (11%)
    reshape x12, local copies, waits for them, and re-layouts, rel_band(): return tiled.reshape(frames, 2 * frames - 1)[:, frames - 1:]  311 us
    reduce_scatter x4, waiting for transfers between devices, settle(): lax.psum_scatter(grad_out, 'dp', scatter_dimension=1, tiled=True)  265 us
    unnamed x8, blocking collectives  250 us
    another operation x16, local copies, waits for them, and re-layouts, rel_band(): tiled = jnp.tile(diagonal_vals, frames)[:frames * (2 * frames - 1)]  229 us
    all_gather x4, waiting for transfers between devices, share_frames(): return lax.all_gather(local_rows, 'tensor', axis=0, tiled=True)  192 us
    reduce_scatter x4, waiting for transfers between devices, settle(): lax.psum_scatter(grad_in, 'dp', scatter_dimension=0, tiled=True)  183 us
    all_gather x4, waiting for transfers between devices, share_grads(): return lax.all_gather(local_rows, 'tensor', axis=0, tiled=True)  149 us
    slice x8, local copies, waits for them, and re-layouts, rel_band(): tiled = jnp.tile(diagonal_vals, frames)[:frames * (2 * frames - 1)]  112 us
  transfers between devices with their start and end apart: 24, of which 19 were waited for; matrix products, arithmetic and copies ran while one was open for 6% of the time, Pallas kernels for 0%

commit v1 on v0

v1 whole, which is shorter than its diff:
```python
import functools

import jax
import jax.numpy as jnp
import numpy as np
from jax import lax
from jax.experimental import pallas as pl
from jax.experimental.pallas import tpu as pltpu
from jax.sharding import PartitionSpec as P

TILE = 128
MASKED = -1e30
F32 = jnp.float32
BF16 = jnp.bfloat16


def pad_up(size, unit):
    return -(-size // unit) * unit


def dot(a, b, ca, cb):
    return lax.dot_general(a, b, (((ca,), (cb,)), ((), ())), preferred_element_type=F32)


def tile_offsets(blocks, block_frames, per_block):
    starts = np.array([b * block_frames + t * TILE for b in range(blocks) for t in range(per_block)])
    return starts[None, :] - starts[:, None]


def bias_types(offsets, reach):
    near = sorted({int(d) for d in offsets.ravel() if abs(int(d)) < reach + TILE - 1})
    far = 4 * TILE + reach
    kinds = near + [-far, far]
    index = {d: i for i, d in enumerate(near)}
    table = np.array(
        [
            [index.get(int(d), len(near) + (1 if d > 0 else 0)) for d in row]
            for row in offsets
        ],
        np.int32,
    )
    return kinds, table


def column_onehot(kinds, reach):
    lane = lax.broadcasted_iota(jnp.int32, (len(kinds), 2 * TILE), 1)
    signed = jnp.where(lane < TILE, lane, lane - 2 * TILE)
    base = jnp.array(kinds, jnp.int32)[:, None]
    column = jnp.clip(base - signed, -reach, reach) + reach
    width = 2 * reach + 1
    flat = column.reshape(-1)
    return (flat[None, :] == jnp.arange(width, dtype=jnp.int32)[:, None]).astype(F32)


def bias_body(row_ref, out_ref):
    for head in range(2):
        line = jnp.broadcast_to(row_ref[0, 0, head : head + 1, :], (TILE, 2 * TILE))
        skewed = pltpu.roll(line, 0, 1, stride=1, stride_axis=0)
        out_ref[0, 0, :, head * TILE : (head + 1) * TILE] = skewed[:, :TILE]


def bias_tiles(rel_table, onehot, kinds):
    heads = rel_table.shape[0]
    pairs = heads // 2
    count = len(kinds)
    rows = jnp.dot(rel_table, onehot, precision=lax.Precision.HIGHEST, preferred_element_type=F32)
    rows = rows.reshape(pairs, 2, count, 2 * TILE).transpose(0, 2, 1, 3)
    return pl.pallas_call(
        bias_body,
        grid=(pairs, count),
        in_specs=[pl.BlockSpec((1, 1, 2, 2 * TILE), lambda p, c: (p, c, 0, 0))],
        out_specs=pl.BlockSpec((1, 1, TILE, 2 * TILE), lambda p, c: (p, c, 0, 0)),
        out_shape=jax.ShapeDtypeStruct((pairs, count, TILE, 2 * TILE), F32),
        name="distance_bias",
    )(rows)


def stacked_heads(pair):
    low_half = lax.broadcasted_iota(jnp.int32, pair.shape, 1) < pair.shape[1] // 2
    zero = jnp.zeros_like(pair)
    return jnp.concatenate([jnp.where(low_half, pair, zero), jnp.where(low_half, zero, pair)], 0)


def own_quadrants(wide):
    half = lax.broadcasted_iota(jnp.int32, (TILE, TILE), 0) < TILE // 2
    return jnp.where(half, wide[:, :TILE], wide[:, TILE:])


def fold(values):
    return values.reshape(values.shape[0] // 8, 8, values.shape[1])


def attend_body(
    place_ref, start_ref, count_ref, kind_ref,
    qkv_ref, bias_ref, lab_ref, labrow_ref,
    out_ref, lse_ref,
    score_ref, turned_ref, acc_ref,
    *, tiles, pairs, scale,
):
    step = pl.program_id(0)
    width = pairs * TILE

    @pl.when(step == 0)
    def _():
        for tile in range(tiles):
            turned_ref[tile] = qkv_ref[place_ref[tile], :, 2 * width :].T

    mine = qkv_ref[place_ref[step]]
    queries = [
        stacked_heads(mine[:, p * TILE : (p + 1) * TILE] * scale) for p in range(pairs)
    ]
    own_label = labrow_ref[step]
    begin = start_ref[step]
    trips = count_ref[step]

    def scores(trip, best):
        for sub in range(2):
            tile = begin + 2 * trip + sub
            kind = kind_ref[step * tiles + tile]
            keys = qkv_ref[place_ref[tile], :, width : 2 * width]
            allowed = lab_ref[tile] == own_label
            parts = []
            for p in range(pairs):
                raw = dot(keys[:, p * TILE : (p + 1) * TILE], queries[p], 1, 1)
                raw = raw + bias_ref[p, kind]
                for h in range(2):
                    part = jnp.where(allowed, raw[:, h * TILE : (h + 1) * TILE], MASKED)
                    score_ref[tile, :, (2 * p + h) * TILE : (2 * p + h + 1) * TILE] = part
                    parts.append(jnp.max(fold(part), axis=0))
            best = jnp.maximum(best, jnp.concatenate(parts, 1))
        return best

    best = lax.fori_loop(0, trips, scores, jnp.full((8, 2 * width), MASKED, F32))
    top = jnp.max(best, axis=0, keepdims=True)
    acc_ref[...] = jnp.zeros_like(acc_ref)

    def mix(trip, total):
        first = begin + 2 * trip
        probs = []
        for sub in range(2):
            value = jnp.exp(score_ref[first + sub] - top)
            total = total + jnp.sum(fold(value), axis=0)
            probs.append(value.astype(BF16))
        both = jnp.concatenate(probs, 0)
        for p in range(pairs):
            turned = jnp.concatenate(
                [turned_ref[first + sub, p * TILE : (p + 1) * TILE, :] for sub in range(2)], 1
            )
            acc_ref[p] += dot(turned, both[:, 2 * p * TILE : 2 * (p + 1) * TILE], 1, 0)
        return total

    total = lax.fori_loop(0, trips, mix, jnp.zeros((8, 2 * width), F32))
    total = jnp.sum(total, axis=0, keepdims=True)
    inverse = 1.0 / total
    log_total = top + jnp.log(total)
    for p in range(pairs):
        wide = acc_ref[p] * inverse[:, 2 * p * TILE : 2 * (p + 1) * TILE]
        out_ref[0, :, p * TILE : (p + 1) * TILE] = own_quadrants(wide).T.astype(BF16)
    for h in range(2 * pairs):
        lse_ref[0, h : h + 1, :] = log_total[:, h * TILE : (h + 1) * TILE]


def attend(qkv, bias, plan):
    tiles, pairs = qkv.shape[0], bias.shape[0]
    width = pairs * TILE
    whole = lambda *shape: pl.BlockSpec(shape, lambda i, *_: (0,) * len(shape))
    return pl.pallas_call(
        functools.partial(attend_body, tiles=tiles, pairs=pairs, scale=plan["scale"]),
        grid_spec=pltpu.PrefetchScalarGridSpec(
            num_scalar_prefetch=4,
            grid=(tiles,),
            in_specs=[
                whole(*qkv.shape),
                whole(*bias.shape),
                whole(tiles, TILE, TILE),
                whole(tiles, 1, TILE),
            ],
            out_specs=[
                pl.BlockSpec((1, TILE, width), lambda i, place, *_: (place[i], 0, 0)),
                pl.BlockSpec((1, 2 * pairs, TILE), lambda i, *_: (i, 0, 0)),
            ],
            scratch_shapes=[
                pltpu.VMEM((tiles, TILE, 2 * width), F32),
                pltpu.VMEM((tiles, width, TILE), BF16),
                pltpu.VMEM((pairs, TILE, 2 * TILE), F32),
            ],
        ),
        out_shape=[
            jax.ShapeDtypeStruct((tiles, TILE, width), BF16),
            jax.ShapeDtypeStruct((tiles, 2 * pairs, TILE), F32),
        ],
        compiler_params=pltpu.CompilerParams(vmem_limit_bytes=48 * 2**20),
        name="attend",
    )(plan["place"], plan["start2"], plan["count2"], plan["kind"], qkv, bias, plan["lab"], plan["labrow"])


def unskew(values):
    wide = jnp.concatenate([values, jnp.zeros_like(values)], 1)
    rows = TILE
    while rows > 8:
        rows //= 2
        wide = wide[:rows] + pltpu.roll(wide[rows:], 2 * TILE - rows, 1)
    row = lax.broadcasted_iota(jnp.int32, wide.shape, 0)
    for bit in (4, 2, 1):
        wide = jnp.where((row & bit) != 0, pltpu.roll(wide, 2 * TILE - bit, 1), wide)
    return jnp.sum(wide, axis=0, keepdims=True)


def attend_back_body(
    place_ref, start_ref, count_ref, kind_ref,
    qkv_ref, bias_ref, lab_ref, labrow_ref, out_ref, grad_ref, lse_ref,
    dqkv_ref, table_ref,
    turned_ref, dk_ref, dv_ref, dq_ref, sums_ref,
    *, tiles, pairs, scale, kinds,
):
    step = pl.program_id(0)
    width = pairs * TILE

    @pl.when(step == 0)
    def _():
        for tile in range(tiles):
            turned_ref[tile] = qkv_ref[place_ref[tile], :, width : 2 * width].T
        dk_ref[...] = jnp.zeros_like(dk_ref)
        dv_ref[...] = jnp.zeros_like(dv_ref)
        sums_ref[...] = jnp.zeros_like(sums_ref)

    here = place_ref[step]
    queries, grads, deltas, logs = [], [], [], []
    for p in range(pairs):
        span = slice(p * TILE, (p + 1) * TILE)
        queries.append(stacked_heads(qkv_ref[here, :, span] * scale))
        grad = grad_ref[here, :, span]
        grads.append(stacked_heads(grad))
        product = (grad.astype(F32) * out_ref[here, :, span].astype(F32)).T
        half = TILE // 2
        deltas.append(
            jnp.concatenate(
                [
                    jnp.sum(product[:half], axis=0, keepdims=True),
                    jnp.sum(product[half:], axis=0, keepdims=True),
                ],
                1,
            )
        )
        logs.append(jnp.concatenate([lse_ref[step, 2 * p + h : 2 * p + h + 1, :] for h in range(2)], 1))
    own_label = labrow_ref[step]
    begin = start_ref[step]
    dq_ref[...] = jnp.zeros_like(dq_ref)

    def visit(trip, carry):
        tile = begin + trip
        kind = kind_ref[step * tiles + tile]
        there = place_ref[tile]
        allowed = lab_ref[tile] == own_label
        allowed = jnp.concatenate([allowed, allowed], 1)
        for p in range(pairs):
            span = slice(p * TILE, (p + 1) * TILE)
            keys = qkv_ref[there, :, width + p * TILE : width + (p + 1) * TILE]
            vals = qkv_ref[there, :, 2 * width + p * TILE : 2 * width + (p + 1) * TILE]
            raw = dot(keys, queries[p], 1, 1) + bias_ref[p, kind]
            prob = jnp.exp(jnp.where(allowed, raw - logs[p], MASKED))
            lift = dot(vals, grads[p], 1, 1)
            slope = prob * (lift - deltas[p])
            sums_ref[p, kind] += slope
            slope = slope.astype(BF16)
            dv_ref[tile, :, span] += dot(prob.astype(BF16), grads[p], 1, 0)
            dk_ref[tile, :, span] += dot(slope, queries[p], 1, 0)
            dq_ref[p] += dot(turned_ref[tile, span, :], slope, 1, 0)
        return carry

    lax.fori_loop(0, count_ref[step], visit, 0)
    for p in range(pairs):
        span = slice(p * TILE, (p + 1) * TILE)
        dqkv_ref[here, :, span] = (own_quadrants(dq_ref[p]).T * scale).astype(BF16)

    @pl.when(step == tiles - 1)
    def _():
        for tile in range(tiles):
            there = place_ref[tile]
            dqkv_ref[there, :, width : 2 * width] = dk_ref[tile].astype(BF16)
            dqkv_ref[there, :, 2 * width :] = dv_ref[tile].astype(BF16)
        for p in range(pairs):
            for kind in range(kinds):
                for h in range(2):
                    table_ref[2 * p + h, kind : kind + 1, :] = unskew(
                        sums_ref[p, kind, :, h * TILE : (h + 1) * TILE]
                    )


def attend_back(qkv, bias, plan, out, grad, lse):
    tiles, pairs, kinds = qkv.shape[0], bias.shape[0], bias.shape[1]
    width = pairs * TILE
    whole = lambda *shape: pl.BlockSpec(shape, lambda i, *_: (0,) * len(shape))
    return pl.pallas_call(
        functools.partial(
            attend_back_body, tiles=tiles, pairs=pairs, scale=plan["scale"], kinds=kinds
        ),
        grid_spec=pltpu.PrefetchScalarGridSpec(
            num_scalar_prefetch=4,
            grid=(tiles,),
            in_specs=[
                whole(*qkv.shape),
                whole(*bias.shape),
                whole(tiles, TILE, TILE),
                whole(tiles, 1, TILE),
                whole(tiles, TILE, width),
                whole(tiles, TILE, width),
                whole(tiles, 2 * pairs, TILE),
            ],
            out_specs=[
                whole(tiles, TILE, 3 * width),
                whole(2 * pairs, kinds, 2 * TILE),
            ],
            scratch_shapes=[
                pltpu.VMEM((tiles, width, TILE), BF16),
                pltpu.VMEM((tiles, TILE, width), F32),
                pltpu.VMEM((tiles, TILE, width), F32),
                pltpu.VMEM((pairs, TILE, 2 * TILE), F32),
                pltpu.VMEM((pairs, kinds, TILE, 2 * TILE), F32),
            ],
        ),
        out_shape=[
            jax.ShapeDtypeStruct((tiles, TILE, 3 * width), BF16),
            jax.ShapeDtypeStruct((2 * pairs, kinds, 2 * TILE), F32),
        ],
        compiler_params=pltpu.CompilerParams(vmem_limit_bytes=48 * 2**20),
        name="attend_back",
    )(
        plan["place"], plan["start1"], plan["count1"], plan["kind"],
        qkv, bias, plan["lab"], plan["labrow"], out, grad, lse,
    )


EDGE = 16


def sigmoid(values):
    return 1.0 / (1.0 + jnp.exp(-values))


def conv_body(
    order_ref, low_ref, high_ref,
    glu_ref, taps_ref, lab_ref,
    act_ref, gated_ref, mixed_ref,
    window_ref, pad_ref, out_pad_ref,
    *, blocks, frames, chunks, lanes, taps,
):
    size = glu_ref.shape[1]
    channels = lanes * TILE
    half = taps // 2
    span = TILE + 2 * EDGE
    for lane in range(lanes):
        pad_ref[lane, :EDGE, :] = jnp.zeros((EDGE, TILE), F32)
    for block in range(blocks):
        where = order_ref[block]
        for lane in range(lanes):
            value = glu_ref[where, :, lane * TILE : (lane + 1) * TILE]
            gate = glu_ref[where, :, channels + lane * TILE : channels + (lane + 1) * TILE]
            first = EDGE + block * frames
            pad_ref[lane, first : first + size, :] = value * sigmoid(gate)
    rest = EDGE + (blocks - 1) * frames + size
    for lane in range(lanes):
        tail = pad_ref.shape[1] - rest
        pad_ref[lane, rest:, :] = jnp.zeros((tail, TILE), F32)

    def chunk(index, carry):
        base = pl.multiple_of(index * TILE, TILE)
        labels = lab_ref[pl.ds(base, span), :]
        center = labels[EDGE : EDGE + TILE]
        for lane in range(lanes):
            values = pad_ref[lane, pl.ds(base, span), :]
            gated_ref[pl.ds(base, TILE), lane * TILE : (lane + 1) * TILE] = values[
                EDGE : EDGE + TILE
            ]

            def segment(label, total):
                window_ref[...] = jnp.where(labels == label, values, 0.0)
                acc = jnp.zeros((TILE, TILE), F32)
                for tap in range(taps):
                    first = EDGE + tap - half
                    acc = acc + window_ref[first : first + TILE, :] * taps_ref[
                        tap : tap + 1, lane * TILE : (lane + 1) * TILE
                    ]
                return jnp.where(center == label, acc, total)

            total = lax.fori_loop(
                low_ref[index], high_ref[index] + 1, segment, jnp.zeros((TILE, TILE), F32)
            )
            mixed_ref[pl.ds(base, TILE), lane * TILE : (lane + 1) * TILE] = total
            out_pad_ref[lane, pl.ds(base, TILE), :] = total * sigmoid(total)
        return carry

    lax.fori_loop(0, chunks, chunk, 0)
    valid = lax.broadcasted_iota(jnp.int32, (size, TILE), 0) < frames
    for block in range(blocks):
        where = order_ref[block]
        for lane in range(lanes):
            rows = out_pad_ref[lane, block * frames : block * frames + size, :]
            act_ref[where, :, lane * TILE : (lane + 1) * TILE] = jnp.where(valid, rows, 0.0).astype(
                BF16
            )


def conv_forward(glu, taps, plan):
    blocks, size, double = glu.shape
    channels = double // 2
    frames, chunks = plan["frames"], plan["chunks"]
    rows = chunks * TILE
    return pl.pallas_call(
        functools.partial(
            conv_body, blocks=blocks, frames=frames, chunks=chunks,
            lanes=channels // TILE, taps=taps.shape[0],
        ),
        grid_spec=pltpu.PrefetchScalarGridSpec(
            num_scalar_prefetch=3,
            grid=(1,),
            in_specs=[
                pl.BlockSpec(glu.shape, lambda i, *_: (0, 0, 0)),
                pl.BlockSpec(taps.shape, lambda i, *_: (0, 0)),
                pl.BlockSpec(plan["flat_lab"].shape, lambda i, *_: (0, 0)),
            ],
            out_specs=[
                pl.BlockSpec((blocks, size, channels), lambda i, *_: (0, 0, 0)),
                pl.BlockSpec((rows, channels), lambda i, *_: (0, 0)),
                pl.BlockSpec((rows, channels), lambda i, *_: (0, 0)),
            ],
            scratch_shapes=[
                pltpu.VMEM((TILE + 2 * EDGE, TILE), F32),
                pltpu.VMEM((channels // TILE, rows + 2 * EDGE, TILE), F32),
                pltpu.VMEM((channels // TILE, rows, TILE), F32),
            ],
        ),
        out_shape=[
            jax.ShapeDtypeStruct((blocks, size, channels), BF16),
            jax.ShapeDtypeStruct((rows, channels), F32),
            jax.ShapeDtypeStruct((rows, channels), F32),
        ],
        compiler_params=pltpu.CompilerParams(vmem_limit_bytes=48 * 2**20),
        name="conv_forward",
    )(plan["order"], plan["low"], plan["high"], glu, taps, plan["flat_lab"])


def conv_back_body(
    order_ref, low_ref, high_ref,
    glu_ref, taps_ref, lab_ref, gated_ref, mixed_ref, grad_ref,
    dglu_ref, dtaps_ref,
    window_ref, source_ref, slope_ref, dgate_ref, sums_ref,
    *, blocks, frames, chunks, lanes, taps,
):
    size = glu_ref.shape[1]
    channels = lanes * TILE
    half = taps // 2
    span = TILE + 2 * EDGE
    rows = chunks * TILE
    for block in range(blocks):
        where = order_ref[block]
        for lane in range(lanes):
            first = EDGE + block * frames
            slope_ref[lane, first : first + size, :] = grad_ref[
                where, :, lane * TILE : (lane + 1) * TILE
            ]
    rest = EDGE + (blocks - 1) * frames + size
    for lane in range(lanes):
        slope_ref[lane, :EDGE, :] = jnp.zeros((EDGE, TILE), F32)
        slope_ref[lane, rest:, :] = jnp.zeros((slope_ref.shape[1] - rest, TILE), F32)
        mixed = mixed_ref[:, lane * TILE : (lane + 1) * TILE]
        gate = sigmoid(mixed)
        slope_ref[lane, EDGE : EDGE + rows, :] = slope_ref[lane, EDGE : EDGE + rows, :] * (
            gate * (1.0 + mixed * (1.0 - gate))
        )
        source_ref[lane, :EDGE, :] = jnp.zeros((EDGE, TILE), F32)
        source_ref[lane, EDGE : EDGE + rows, :] = gated_ref[:, lane * TILE : (lane + 1) * TILE]
        source_ref[lane, EDGE + rows :, :] = jnp.zeros((EDGE, TILE), F32)
        dgate_ref[lane, rows:, :] = jnp.zeros((dgate_ref.shape[1] - rows, TILE), F32)
    sums_ref[...] = jnp.zeros_like(sums_ref)

    def chunk(index, carry):
        base = pl.multiple_of(index * TILE, TILE)
        labels = lab_ref[pl.ds(base, span), :]
        center = labels[EDGE : EDGE + TILE]
        for lane in range(lanes):
            slopes = slope_ref[lane, pl.ds(base, span), :]
            sources = source_ref[lane, pl.ds(base, span), :]

            def segment(label, total):
                window_ref[0] = jnp.where(labels == label, slopes, 0.0)
                window_ref[1] = jnp.where(labels == label, sources, 0.0)
                inner = window_ref[0, EDGE : EDGE + TILE, :]
                acc = jnp.zeros((TILE, TILE), F32)
                for tap in range(taps):
                    first = EDGE - tap + half
                    acc = acc + window_ref[0, first : first + TILE, :] * taps_ref[
                        tap : tap + 1, lane * TILE : (lane + 1) * TILE
                    ]
                    first = EDGE + tap - half
                    part = fold(inner * window_ref[1, first : first + TILE, :])
                    sums_ref[lane, tap] += jnp.sum(part, axis=0)
                return jnp.where(center == label, acc, total)

            dgate_ref[lane, pl.ds(base, TILE), :] = lax.fori_loop(
                low_ref[index], high_ref[index] + 1, segment, jnp.zeros((TILE, TILE), F32)
            )
        return carry

    lax.fori_loop(0, chunks, chunk, 0)
    for lane in range(lanes):
        dtaps_ref[:, lane * TILE : (lane + 1) * TILE] = jnp.sum(sums_ref[lane], axis=1)
    valid = lax.broadcasted_iota(jnp.int32, (size, TILE), 0) < frames
    for block in range(blocks):
        where = order_ref[block]
        for lane in range(lanes):
            lead = slice(lane * TILE, (lane + 1) * TILE)
            follow = slice(channels + lane * TILE, channels + (lane + 1) * TILE)
            rows_in = dgate_ref[lane, block * frames : block * frames + size, :]
            rows_in = jnp.where(valid, rows_in, 0.0)
            value = glu_ref[where, :, lead]
            gate = sigmoid(glu_ref[where, :, follow])
            dglu_ref[where, :, lead] = (rows_in * gate).astype(BF16)
            dglu_ref[where, :, follow] = (rows_in * value * gate * (1.0 - gate)).astype(BF16)


def conv_backward(glu, taps, plan, gated, mixed, grad):
    blocks, size, double = glu.shape
    channels = double // 2
    frames, chunks = plan["frames"], plan["chunks"]
    rows = chunks * TILE
    lanes = channels // TILE
    whole = lambda *shape: pl.BlockSpec(shape, lambda i, *_: (0,) * len(shape))
    return pl.pallas_call(
        functools.partial(
            conv_back_body, blocks=blocks, frames=frames, chunks=chunks,
            lanes=lanes, taps=taps.shape[0],
        ),
        grid_spec=pltpu.PrefetchScalarGridSpec(
            num_scalar_prefetch=3,
            grid=(1,),
            in_specs=[
                whole(*glu.shape),
                whole(*taps.shape),
                whole(*plan["flat_lab"].shape),
                whole(rows, channels),
                whole(rows, channels),
                whole(blocks, size, channels),
            ],
            out_specs=[whole(*glu.shape), whole(*taps.shape)],
            scratch_shapes=[
                pltpu.VMEM((2, TILE + 2 * EDGE, TILE), F32),
                pltpu.VMEM((lanes, rows + 2 * EDGE, TILE), F32),
                pltpu.VMEM((lanes, rows + 2 * EDGE, TILE), F32),
                pltpu.VMEM((lanes, rows + EDGE, TILE), F32),
                pltpu.VMEM((lanes, taps.shape[0], 8, TILE), F32),
            ],
        ),
        out_shape=[
            jax.ShapeDtypeStruct(glu.shape, BF16),
            jax.ShapeDtypeStruct(taps.shape, F32),
        ],
        compiler_params=pltpu.CompilerParams(vmem_limit_bytes=56 * 2**20),
        name="conv_backward",
    )(
        plan["order"], plan["low"], plan["high"],
        glu, taps, plan["flat_lab"], gated, mixed, grad,
    )


def swap(values, bit, axis="tensor"):
    count = lax.axis_size(axis)
    return lax.ppermute(values, axis, [(i, i ^ bit) for i in range(count)])


def gather(mine):
    beside = swap(mine, 1)
    across = swap(mine, 2)
    return [mine, beside, across, swap(across, 1)]


def scatter(parts):
    own, beside, across, diagonal = parts
    outgoing = (across + swap(diagonal.astype(BF16), 1).astype(F32)).astype(BF16)
    far = swap(outgoing, 2)
    return own + swap(beside.astype(BF16), 1).astype(F32) + far.astype(F32)


def sum_bits(values, axis):
    bit = 1
    while bit < lax.axis_size(axis):
        values = values + swap(values, bit, axis)
        bit *= 2
    return values


def settle(grad):
    return lax.psum_scatter(
        grad.astype(BF16), "dp", scatter_dimension=0, tiled=True
    ).astype(F32)


def norm_parts(rows):
    mean = jnp.mean(rows, axis=-1, keepdims=True)
    centred = rows - mean
    rstd = lax.rsqrt(jnp.mean(centred * centred, axis=-1, keepdims=True) + 1e-05)
    return centred * rstd, rstd


def normed(rows, gain):
    return norm_parts(rows)[0] * gain


def norm_back(rows, gain, grad):
    unit, rstd = norm_parts(rows)
    scaled = grad * gain
    first = jnp.mean(scaled, axis=-1, keepdims=True)
    second = jnp.mean(scaled * unit, axis=-1, keepdims=True)
    return rstd * (scaled - first - unit * second), jnp.sum(grad * unit, axis=0)


def pile(blocks):
    return jnp.concatenate(blocks, 0)


def feed_forward(rows, gain, w_in, w_out):
    blocks = gather(normed(rows, gain).astype(BF16))
    hidden, active, parts = [], [], []
    for block in blocks:
        a = dot(block, w_in, 1, 0)
        z = (a * jax.nn.sigmoid(a)).astype(BF16)
        hidden.append(a.astype(BF16))
        active.append(z)
        parts.append(dot(z, w_out, 1, 0))
    return rows + 0.5 * scatter(parts), (blocks, hidden, active)


def feed_back(incoming, rows, gain, w_in, w_out, state):
    blocks, hidden, active = state
    grads = gather((0.5 * incoming).astype(BF16))
    inner, parts = [], []
    for grad, a in zip(grads, hidden):
        ez = dot(grad, w_out, 1, 1)
        a = a.astype(F32)
        s = jax.nn.sigmoid(a)
        ea = (ez * s * (1.0 + a * (1.0 - s))).astype(BF16)
        inner.append(ea)
        parts.append(dot(ea, w_in, 1, 1))
    grad_w_out = settle(dot(pile(grads), pile(active), 0, 0)).T
    grad_w_in = settle(dot(pile(blocks), pile(inner), 0, 0))
    passed, grad_gain = norm_back(rows, gain, scatter(parts))
    return incoming + passed, grad_gain, grad_w_in, grad_w_out


def make_plan(segments, frames, reach, head_width):
    blocks = lax.axis_size("tensor")
    here = lax.axis_index("tensor").astype(jnp.int32)
    size = pad_up(frames, TILE)
    per_block = size // TILE
    tiles = blocks * per_block
    offsets = tile_offsets(blocks, frames, per_block)
    kinds, table = bias_types(offsets, reach)
    flat = segments.reshape(-1).astype(jnp.int32)
    lab = jnp.pad(flat.reshape(blocks, frames), ((0, 0), (0, size - frames)), constant_values=-1)
    lab = lab.reshape(tiles, TILE)
    high = jnp.max(lab, axis=1)
    low = jnp.min(jnp.where(lab < 0, 1 << 20, lab), axis=1)
    seen = (low[:, None] <= high[None, :]) & (low[None, :] <= high[:, None])
    position = jnp.arange(tiles, dtype=jnp.int32)
    first = jnp.min(jnp.where(seen, position[None, :], tiles), axis=1)
    last = jnp.max(jnp.where(seen, position[None, :], -1), axis=1)
    count1 = last - first + 1
    count2 = (count1 + 1) // 2
    start2 = jnp.minimum(first, tiles - 2 * count2)
    order = jnp.arange(blocks, dtype=jnp.int32) ^ here
    place = (order[:, None] * per_block + jnp.arange(per_block, dtype=jnp.int32)[None, :]).reshape(-1)
    total = blocks * frames
    chunks = pad_up(total, TILE) // TILE
    padded = jnp.pad(flat, (EDGE, chunks * TILE - total + EDGE), constant_values=-1)
    body = padded[EDGE : EDGE + chunks * TILE].reshape(chunks, TILE)
    return dict(
        kinds=kinds,
        kind=jnp.asarray(table.reshape(-1)),
        place=place,
        start1=first,
        count1=count1,
        start2=start2,
        count2=count2,
        lab=jnp.broadcast_to(lab[:, :, None], (tiles, TILE, TILE)),
        labrow=lab[:, None, :],
        scale=float(head_width) ** -0.5,
        frames=frames,
        chunks=chunks,
        order=order,
        low=jnp.min(jnp.where(body < 0, 1 << 20, body), axis=1),
        high=jnp.max(body, axis=1),
        flat_lab=jnp.broadcast_to(padded[:, None], (padded.shape[0], TILE)),
    )


def attention(rows, gain, w_qkv, w_output, bias, plan):
    blocks = gather(normed(rows, gain).astype(BF16))
    size = rows.shape[0]
    qkv = jnp.stack([dot(block, w_qkv, 1, 0).astype(BF16) for block in blocks])
    qkv = qkv.reshape(-1, TILE, w_qkv.shape[1])
    out, lse = attend(qkv, bias, plan)
    flat = out.reshape(len(blocks), size, -1)
    parts = [dot(flat[i], w_output, 1, 0) for i in range(len(blocks))]
    return rows + scatter(parts), (blocks, qkv, out, lse)


def attention_back(incoming, rows, gain, w_qkv, w_output, bias, plan, state):
    blocks, qkv, out, lse = state
    size = rows.shape[0]
    grads = gather(incoming.astype(BF16))
    eo = jnp.stack([dot(grad, w_output, 1, 1).astype(BF16) for grad in grads])
    dqkv, sums = attend_back(qkv, bias, plan, out, eo.reshape(out.shape), lse)
    flat = dqkv.reshape(len(blocks), size, -1)
    parts = [dot(flat[i], w_qkv, 1, 1) for i in range(len(blocks))]
    grad_w_output = settle(dot(pile(grads), out.reshape(-1, out.shape[-1]), 0, 0)).T
    grad_w_qkv = settle(dot(pile(blocks), flat.reshape(-1, flat.shape[-1]), 0, 0))
    passed, grad_gain = norm_back(rows, gain, scatter(parts))
    return incoming + passed, grad_gain, sums, grad_w_qkv, grad_w_output


def convolution(rows, gain, w_glu, taps, w_back, plan):
    blocks = gather(normed(rows, gain).astype(BF16))
    glu = jnp.stack([dot(block, w_glu, 1, 0) for block in blocks])
    act, gated, mixed = conv_forward(glu, taps, plan)
    parts = [dot(act[i], w_back, 1, 0) for i in range(len(blocks))]
    return rows + scatter(parts), (blocks, glu, act, gated, mixed)


def convolution_back(incoming, rows, gain, w_glu, taps, w_back, plan, state):
    blocks, glu, act, gated, mixed = state
    grads = gather(incoming.astype(BF16))
    ew = jnp.stack([dot(grad, w_back, 1, 1) for grad in grads])
    dglu, dtaps = conv_backward(glu, taps, plan, gated, mixed, ew)
    parts = [dot(dglu[i], w_glu, 1, 1) for i in range(len(blocks))]
    grad_w_back = settle(dot(pile(grads), act.reshape(-1, act.shape[-1]), 0, 0)).T
    grad_w_glu = settle(dot(pile(blocks), dglu.reshape(-1, dglu.shape[-1]), 0, 0))
    passed, grad_gain = norm_back(rows, gain, scatter(parts))
    return incoming + passed, grad_gain, dtaps, grad_w_glu, grad_w_back


def shards(
    inputs, segments, cotangent, gain_one, first_in, first_out, gain_two, w_query, w_key, w_value,
    w_output, rel_table, gain_three, w_glu, kernel, w_back, gain_four, second_in, second_out,
    gain_five,
):
    frames, _, width = inputs.shape
    size = pad_up(frames, TILE)
    heads = rel_table.shape[0]
    reach = rel_table.shape[1] // 2
    head_width = w_query.shape[1] // heads

    def padded(values):
        return jnp.pad(values.reshape(frames, width).astype(F32), ((0, size - frames), (0, 0)))

    plan = make_plan(segments, frames, reach, head_width)
    onehot = column_onehot(plan["kinds"], reach)
    bias = bias_tiles(rel_table, onehot, plan["kinds"])
    w_qkv = jnp.concatenate([w_query, w_key, w_value], 1)
    channels = kernel.shape[1]
    glu_matrix = w_glu.reshape(width, 2 * channels)

    start = padded(inputs)
    one, state_one = feed_forward(start, gain_one, first_in, first_out)
    two, state_two = attention(one, gain_two, w_qkv, w_output, bias, plan)
    three, state_three = convolution(two, gain_three, glu_matrix, kernel, w_back, plan)
    four, state_four = feed_forward(three, gain_four, second_in, second_out)
    output = normed(four, gain_five).astype(BF16)
    e4, grad_five = norm_back(four, gain_five, padded(cotangent))
    e3, grad_four, grad_second_in, grad_second_out = feed_back(
        e4, three, gain_four, second_in, second_out, state_four
    )
    e2, grad_three, grad_kernel, grad_w_glu, grad_w_back = convolution_back(
        e3, two, gain_three, glu_matrix, kernel, w_back, plan, state_three
    )
    e1, grad_two, sums, grad_w_qkv, grad_w_output = attention_back(
        e2, one, gain_two, w_qkv, w_output, bias, plan, state_two
    )
    e0, grad_one, grad_first_in, grad_first_out = feed_back(
        e1, start, gain_one, first_in, first_out, state_one
    )
    grad_table = lax.dot_general(
        sums.reshape(heads, -1), onehot, (((1,), (1,)), ((), ())),
        precision=lax.Precision.HIGHEST, preferred_element_type=F32,
    )
    gains = sum_bits(jnp.concatenate([grad_one, grad_two, grad_three, grad_four, grad_five]), "tensor")
    small = jnp.concatenate([gains, grad_table.reshape(-1), grad_kernel.reshape(-1)])
    small = sum_bits(small, "dp")
    grad_gains = [small[i * width : (i + 1) * width] for i in range(5)]
    rest = small[5 * width :]
    grad_table = rest[: grad_table.size].reshape(grad_table.shape)
    grad_kernel = rest[grad_table.size :].reshape(grad_kernel.shape)
    cut = w_query.shape[1]
    return (
        output[:frames].reshape(inputs.shape),
        e0[:frames].reshape(inputs.shape),
        grad_gains[0],
        grad_first_in,
        grad_first_out,
        grad_gains[1],
        grad_w_qkv[:, :cut],
        grad_w_qkv[:, cut : 2 * cut],
        grad_w_qkv[:, 2 * cut :],
        grad_w_output,
        grad_table,
        grad_gains[2],
        grad_w_glu.reshape(grad_w_glu.shape[0], 2, channels),
        grad_kernel,
        grad_w_back,
        grad_gains[3],
        grad_second_in,
        grad_second_out,
        grad_gains[4],
    )


def solution(mesh):
    in_specs = (
        P("tensor", "dp", None), P("dp", None), P("tensor", "dp", None), P(),
        P(None, "tensor"), P("tensor", None), P(), P(None, "tensor"), P(None, "tensor"),
        P(None, "tensor"), P("tensor", None), P("tensor", None), P(), P(None, None, "tensor"),
        P(None, "tensor"), P("tensor", None), P(), P(None, "tensor"), P("tensor", None), P(),
    )
    out_specs = (
        P("tensor", "dp", None), P("tensor", "dp", None), P(), P("dp", "tensor"),
        P("tensor", "dp"), P(), P("dp", "tensor"), P("dp", "tensor"), P("dp", "tensor"),
        P("tensor", "dp"), P("tensor", None), P(), P("dp", None, "tensor"), P(None, "tensor"),
        P("tensor", "dp"), P(), P("dp", "tensor"), P("tensor", "dp"), P(),
    )
    return jax.shard_map(shards, mesh=mesh, in_specs=in_specs, out_specs=out_specs, check_vma=False)
```

time: 2930 us -> 853 us (0.29)
  local copies, waits for them, and re-layouts: 1070 us -> 28.8 us
  blocking collectives: 328 us -> 0 us
  waiting for transfers between devices: 793 us -> 479 us
  other arithmetic: 347 us -> 37.6 us
  matrix products: 324 us -> 139 us
  Pallas kernels: 0 us -> 102 us
    reshape x17 -> x8, local copies, waits for them, and re-layouts: 392 us -> 3.84 us  [the longest x1 1.77 us: shards(): grad_w_glu.reshape(grad_w_glu.shape[0], 2, channels)]
    all_gather x8 -> x0, waiting for transfers between devices: 341 us -> none  [the longest x4 192 us: share_frames(): return lax.all_gather(local_rows, 'tensor', axis=0, tiled=True)]
    ppermute x0 -> x53, waiting for transfers between devices: none -> 256 us  [swap(): return lax.ppermute(values, axis, [(i, i ^ bit) for i in range(count)])]
    unnamed x8 -> x0, blocking collectives: 250 us -> none
    another operation x23 -> x2, local copies, waits for them, and re-layouts: 235 us -> 0.1 us  [the longest x1 0.08 us: make_plan(): flat.reshape(blocks, frames)]
    reduce_scatter x8, waiting for transfers between devices: 447 us -> 222 us  [settle(): lax.psum_scatter(grad.astype(BF16), 'dp', scatter_dimension=0, tiled=True)]
    slice x18 -> x6, local copies, waits for them, and re-layouts: 191 us -> 3.38 us  [the longest x1 1.65 us: shards(): grad_w_qkv[:, 2 * cut:]]
    dot_general x68 -> x74, matrix products: 324 us -> 139 us  [the longest x72 137 us: dot(): lax.dot_general(a, b, (((ca,), (cb,)), ((), ())), preferred_element_type=...]
  transfers between devices with their start and end apart: 24 -> 61, of which waited for: 19 -> 27; matrix products, arithmetic and copies ran while one was open for 6% -> 20% of each run, Pallas kernels for 0% -> 9%
where the time goes in v1:
time: 853 us; the launch traced here: 844 us
  waiting for transfers between devices  479 us (56%)
  matrix products  139 us (16%)
  Pallas kernels  102 us (12%)
  starting transfers between devices  41.4 us (5%)
  other arithmetic  37.6 us (4%)
  local copies, waits for them, and re-layouts  28.8 us (3%)
  between operations  16.5 us (2%)
    ppermute x53, waiting for transfers between devices, swap(): return lax.ppermute(values, axis, [(i, i ^ bit) for i in range(count)])  256 us
    reduce_scatter x8, waiting for transfers between devices, settle(): lax.psum_scatter(grad.astype(BF16), 'dp', scatter_dimension=0, tiled=True)  222 us
    dot_general x72, matrix products, dot(): lax.dot_general(a, b, (((ca,), (cb,)), ((), ())), preferred_element_type=...  137 us
    pallas_call x1, Pallas kernels, attend_back(): pl.pallas_call(functools.partial(attend_back_body, tiles=tiles, pairs=pai...  47.4 us
    ppermute x53, starting transfers between devices, swap(): return lax.ppermute(values, axis, [(i, i ^ bit) for i in range(count)])  40 us
    unnamed x241, local copies, waits for them, and re-layouts  19.8 us
    pallas_call x1, Pallas kernels, attend(): pl.pallas_call(functools.partial(attend_body, tiles=tiles, pairs=pairs, s...  18.9 us
    pallas_call x1, Pallas kernels, conv_backward(): pl.pallas_call(functools.partial(conv_back_body, blocks=blocks, frames=fr...  17.1 us
  transfers between devices with their start and end apart: 61, of which 27 were waited for; matrix products, arithmetic and copies ran while one was open for 20% of the time, Pallas kernels for 9%

profile of v1, /device:TPU:0, one launch (start us, length us, event | category | flops | bytes accessed | tf_op | source)
XLA Modules:
  0.0 843.7 jit_solution(12502962849693328544)
XLA Ops:
  16.4 16.6 %collective-permute-done.2 = bf16[384,1024]{1,0:T(8,128)(2,1)} collective-permute-done((bf16[384,1024]{1,0:T(8,128)(2,1)}, bf16[384,1024]{1,0:T(8,128)(2,1)}, u32[]{:S(2)}, u32[]{:S(2)}) %collective-permute-start.2) | collective-permute-done | bytes 786464 | tf_op jit(solution)/shard_map/ppermute | solution.py:568
  54.5 15.1 %collective-permute-done.5 = bf16[384,1024]{1,0:T(8,128)(2,1)S(1)} collective-permute-done((bf16[384,1024]{1,0:T(8,128)(2,1)S(1)}, bf16[384,1024]{1,0:T(8,128)(2,1)S(1)}, u32[]{:S(2)}, u32[]{:S(2)}) %collective-permute-start.5) | collective-permute-done | bytes 786464 | tf_op jit(solution)/shard_map/ppermute | solution.py:568
  74.9 9.9 %distance_bias.1.bias_ref = f32[2,9,128,256]{3,2,1,0:T(8,128)} custom-call(f32[2,9,2,256]{3,2,1,0:T(2,128)} %bitcast.262), custom_call_target="tpu_custom_call" | custom-call | tf_op jit(solution)/shard_map/distance_bias/pallas_call | solution.py:68
  101.4 18.9 %attend.1 = (bf16[12,128,256]{2,1,0:T(8,128)(2,1)S(1)}, f32[12,4,128]{2,1,0:T(4,128)S(1)}) custom-call(s32[12]{0:T(128)S(1)} %add.304.place_ref, s32[12]{0:T(128)S(1)} %get-tuple-element.134.start_ref, s32[12]{0:T(128)S(1)} %get-tuple-element.135.count_ref, s32[144]{0:T(256)S(1)} %copy-done.15, bf16[12,128,768]{2,1,0:T(8,128)(2,1)S(1)} %bitcast.228, ...), custom_call_target="tpu_custom_call" | custom-call | tf_op jit(solution)/shard_map/attend/pallas_call | solution.py:167
  127.1 17.7 %collective-permute-done.11 = bf16[384,1024]{1,0:T(8,128)(2,1)S(1)} collective-permute-done((bf16[384,1024]{1,0:T(8,128)(2,1)S(1)}, bf16[384,1024]{1,0:T(8,128)(2,1)S(1)}, u32[]{:S(2)}, u32[]{:S(2)}) %collective-permute-start.11) | collective-permute-done | bytes 786464 | tf_op jit(solution)/shard_map/ppermute | solution.py:568
  148.0 17.3 %collective-permute-done.13 = bf16[384,1024]{1,0:T(8,128)(2,1)S(1)} collective-permute-done((bf16[384,1024]{1,0:T(8,128)(2,1)S(1)}, bf16[384,1024]{1,0:T(8,128)(2,1)S(1)}, u32[]{:S(2)}, u32[]{:S(2)}) %collective-permute-start.13) | collective-permute-done | bytes 786464 | tf_op jit(solution)/shard_map/ppermute | solution.py:568
  170.5 8.8 %conv_forward.1 = (bf16[4,384,256]{2,1,0:T(8,128)(2,1)S(1)}, f32[1536,256]{1,0:T(8,128)S(1)}, f32[1536,256]{1,0:T(8,128)S(1)}) custom-call(s32[4]{0:T(128)S(1)} %iota_xor_fusion.order_ref, s32[12]{0:T(128)S(1)} %get-tuple-element.110.low_ref, s32[12]{0:T(128)S(1)} %get-tuple-element.109.high_ref, f32[4,384,512]{2,1,0:T(8,128)} %pad_maximum_fusion.glu_ref, ...), custom_call_target="tpu_custom_call" | custom-call | tf_op jit(solution)/shard_map/conv_forward/pallas_call | solution.py:409
  184.8 17.7 %collective-permute-done.17 = bf16[384,1024]{1,0:T(8,128)(2,1)S(1)} collective-permute-done((bf16[384,1024]{1,0:T(8,128)(2,1)S(1)}, bf16[384,1024]{1,0:T(8,128)(2,1)S(1)}, u32[]{:S(2)}, u32[]{:S(2)}) %collective-permute-start.17) | collective-permute-done | bytes 786464 | tf_op jit(solution)/shard_map/ppermute | solution.py:568
  205.7 17.3 %collective-permute-done.20 = bf16[384,1024]{1,0:T(8,128)(2,1)S(1)} collective-permute-done((bf16[384,1024]{1,0:T(8,128)(2,1)S(1)}, bf16[384,1024]{1,0:T(8,128)(2,1)S(1)}, u32[]{:S(2)}, u32[]{:S(2)}) %collective-permute-start.20) | collective-permute-done | bytes 786464 | tf_op jit(solution)/shard_map/ppermute | solution.py:568
  236.8 14.9 %collective-permute-done.23 = bf16[384,1024]{1,0:T(8,128)(2,1)S(1)} collective-permute-done((bf16[384,1024]{1,0:T(8,128)(2,1)S(1)}, bf16[384,1024]{1,0:T(8,128)(2,1)S(1)}, u32[]{:S(2)}, u32[]{:S(2)}) %collective-permute-start.23) | collective-permute-done | bytes 786464 | tf_op jit(solution)/shard_map/ppermute | solution.py:568
  257.5 17.0 %collective-permute-done.26 = bf16[384,1024]{1,0:T(8,128)(2,1)S(1)} collective-permute-done((bf16[384,1024]{1,0:T(8,128)(2,1)S(1)}, bf16[384,1024]{1,0:T(8,128)(2,1)S(1)}, u32[]{:S(2)}, u32[]{:S(2)}) %collective-permute-start.26) | collective-permute-done | bytes 786464 | tf_op jit(solution)/shard_map/ppermute | solution.py:568
  296.7 15.8 %collective-permute-done.29 = bf16[384,1024]{1,0:T(8,128)(2,1)S(1)} collective-permute-done((bf16[384,1024]{1,0:T(8,128)(2,1)S(1)}, bf16[384,1024]{1,0:T(8,128)(2,1)S(1)}, u32[]{:S(2)}, u32[]{:S(2)}) %collective-permute-start.29) | collective-permute-done | bytes 786464 | tf_op jit(solution)/shard_map/ppermute | solution.py:568
  318.3 17.8 %collective-permute-done.31 = bf16[384,1024]{1,0:T(8,128)(2,1)} collective-permute-done((bf16[384,1024]{1,0:T(8,128)(2,1)}, bf16[384,1024]{1,0:T(8,128)(2,1)}, u32[]{:S(2)}, u32[]{:S(2)}) %collective-permute-start.31) | collective-permute-done | bytes 786464 | tf_op jit(solution)/shard_map/ppermute | solution.py:568
  349.6 17.1 %conv_backward.1 = (bf16[4,384,512]{2,1,0:T(8,128)(2,1)}, f32[31,256]{1,0:T(8,128)}) custom-call(s32[4]{0:T(128)} %copy-done.16, s32[12]{0:T(128)} %copy-done.14, s32[12]{0:T(128)} %copy-done.13, f32[4,384,512]{2,1,0:T(8,128)} %pad_maximum_fusion.glu_ref, f32[31,256]{1,0:T(8,128)} %taps_ref.3, s32[1568,128]{1,0:T(8,128)} %copy-done.3, ...), custom_call_target="tpu_custom_call" | custom-call | tf_op jit(solution)/shard_map/conv_backward/pallas_call | solution.py:529
  374.0 17.4 %collective-permute-done.35 = bf16[384,1024]{1,0:T(8,128)(2,1)S(1)} collective-permute-done((bf16[384,1024]{1,0:T(8,128)(2,1)S(1)}, bf16[384,1024]{1,0:T(8,128)(2,1)S(1)}, u32[]{:S(2)}, u32[]{:S(2)}) %collective-permute-start.35) | collective-permute-done | bytes 786464 | tf_op jit(solution)/shard_map/ppermute | solution.py:568
  399.8 13.5 %collective-permute-done.37 = bf16[384,1024]{1,0:T(8,128)(2,1)S(1)} collective-permute-done((bf16[384,1024]{1,0:T(8,128)(2,1)S(1)}, bf16[384,1024]{1,0:T(8,128)(2,1)S(1)}, u32[]{:S(2)}, u32[]{:S(2)}) %collective-permute-start.37) | collective-permute-done | bytes 786464 | tf_op jit(solution)/shard_map/ppermute | solution.py:568
  423.0 47.4 %attend_back.1 = (bf16[12,128,768]{2,1,0:T(8,128)(2,1)S(1)}, f32[4,9,256]{2,1,0:T(8,128)S(1)}) custom-call(s32[12]{0:T(128)S(1)} %add.304.place_ref, s32[12]{0:T(128)S(1)} %get-tuple-element.114.start_ref, s32[12]{0:T(128)S(1)} %get-tuple-element.153.count_ref, s32[144]{0:T(256)S(1)} %copy-done.15, bf16[12,128,768]{2,1,0:T(8,128)(2,1)} %bitcast.229, ...), custom_call_target="tpu_custom_call" | custom-call | tf_op jit(solution)/shard_map/attend_back/pallas_call | solution.py:294
  494.6 10.6 %collective-permute-done.41 = bf16[384,1024]{1,0:T(8,128)(2,1)} collective-permute-done((bf16[384,1024]{1,0:T(8,128)(2,1)}, bf16[384,1024]{1,0:T(8,128)(2,1)}, u32[]{:S(2)}, u32[]{:S(2)}) %collective-permute-start.41) | collective-permute-done | bytes 786464 | tf_op jit(solution)/shard_map/ppermute | solution.py:568
  511.0 17.2 %collective-permute-done.44 = bf16[384,1024]{1,0:T(8,128)(2,1)S(1)} collective-permute-done((bf16[384,1024]{1,0:T(8,128)(2,1)S(1)}, bf16[384,1024]{1,0:T(8,128)(2,1)S(1)}, u32[]{:S(2)}, u32[]{:S(2)}) %collective-permute-start.44) | collective-permute-done | bytes 786464 | tf_op jit(solution)/shard_map/ppermute | solution.py:568
  575.5 11.0 %collective-permute-done.47 = bf16[384,1024]{1,0:T(8,128)(2,1)} collective-permute-done((bf16[384,1024]{1,0:T(8,128)(2,1)}, bf16[384,1024]{1,0:T(8,128)(2,1)}, u32[]{:S(2)}, u32[]{:S(2)}) %collective-permute-start.47) | collective-permute-done | bytes 786464 | tf_op jit(solution)/shard_map/ppermute | solution.py:568
  588.9 37.6 %reduce-scatter.15.cloned.1.call-done = bf16[128,256]{1,0:T(8,128)(2,1)} async-done(((bf16[1024,256]{1,0:T(8,128)(2,1)}), bf16[128,256]{1,0:T(8,128)(2,1)}) %reduce-scatter.15.cloned.1.call-update) | async-done | bytes 65552 | tf_op jit(solution)/shard_map/reduce_scatter | solution.py:593
  629.6 64.4 %reduce-scatter.13.cloned.1.call-done = bf16[128,768]{1,0:T(8,128)(2,1)} async-done(((bf16[1024,768]{1,0:T(8,128)(2,1)}), bf16[128,768]{1,0:T(8,128)(2,1)}) %reduce-scatter.13.cloned.1.call-update) | async-done | bytes 196624 | tf_op jit(solution)/shard_map/reduce_scatter | solution.py:593
  712.6 51.9 %reduce-scatter.11.cloned.1.call-done = bf16[128,1024]{1,0:T(8,128)(2,1)} async-done(((bf16[1024,1024]{1,0:T(8,128)(2,1)}), bf16[128,1024]{1,0:T(8,128)(2,1)}) %reduce-scatter.11.cloned.1.call-update) | async-done | bytes 262160 | tf_op jit(solution)/shard_map/reduce_scatter | solution.py:593
  766.4 68.2 %reduce-scatter.9.cloned.1.call-done = bf16[128,1024]{1,0:T(8,128)(2,1)} async-done(((bf16[1024,1024]{1,0:T(8,128)(2,1)}), bf16[128,1024]{1,0:T(8,128)(2,1)}) %reduce-scatter.9.cloned.1.call-update) | async-done | bytes 262160 | tf_op jit(solution)/shard_map/reduce_scatter | solution.py:593
  (521 shorter events, 266.2 us)
Async XLA Ops:
  7.2 548.2 %reduce-scatter.23.cloned.1.call-start = ((), (), s32[]{:S(2)}) async-start(), calls=%async_computation.15 | async-start | bytes 2359296 | tf_op jit(solution)/shard_map/reduce_scatter | solution.py:593
  12.2 20.8 %collective-permute-start.2 = (bf16[384,1024]{1,0:T(8,128)(2,1)}, bf16[384,1024]{1,0:T(8,128)(2,1)}, u32[]{:S(2)}, u32[]{:S(2)}) collective-permute-start(bf16[384,1024]{1,0:T(8,128)(2,1)} %multiply_convert_fusion.13), channel_id=1, source_target_pairs={{0,2},{1,3},{2,0},{3,1},{4,6},{5,7},{6,4},{7,5},{8,10},{9,11},{10,... | collective-permute-start | bytes 2359304 | tf_op jit(solution)/shard_map/ppermute | solution.py:568
  15.1 20.7 %collective-permute-start = (bf16[384,1024]{1,0:T(8,128)(2,1)}, bf16[384,1024]{1,0:T(8,128)(2,1)}, u32[]{:S(2)}, u32[]{:S(2)}) collective-permute-start(bf16[384,1024]{1,0:T(8,128)(2,1)} %multiply_convert_fusion.13), channel_id=1, source_target_pairs={{0,1},{1,0},{2,3},{3,2},{4,5},{5,4},{6,7},{7,6},{8,9},{9,8},{10,11... | collective-permute-start | bytes 2359304 | tf_op jit(solution)/shard_map/ppermute | solution.py:568
  49.6 20.0 %collective-permute-start.5 = (bf16[384,1024]{1,0:T(8,128)(2,1)S(1)}, bf16[384,1024]{1,0:T(8,128)(2,1)S(1)}, u32[]{:S(2)}, u32[]{:S(2)}) collective-permute-start(bf16[384,1024]{1,0:T(8,128)(2,1)S(1)} %add_convert_fusion.7), channel_id=1, source_target_pairs={{0,2},{1,3},{2,0},{3,1},{4,6},{5,7},{6,4},{7,5},{8,10},{9,11},{10,... | collective-permute-start | bytes 2359304 | tf_op jit(solution)/shard_map/ppermute | solution.py:568
  74.0 21.2 %collective-permute-start.6 = (bf16[384,1024]{1,0:T(8,128)(2,1)S(1)}, bf16[384,1024]{1,0:T(8,128)(2,1)}, u32[]{:S(2)}, u32[]{:S(2)}) collective-permute-start(bf16[384,1024]{1,0:T(8,128)(2,1)S(1)} %multiply_convert_fusion.8), channel_id=1, source_target_pairs={{0,1},{1,0},{2,3},{3,2},{4,5},{5,4},{6,7},{7,6},{8,9},{9,8},{10,11... | collective-permute-start | bytes 2359304 | tf_op jit(solution)/shard_map/ppermute | solution.py:568
  124.9 19.9 %collective-permute-start.11 = (bf16[384,1024]{1,0:T(8,128)(2,1)S(1)}, bf16[384,1024]{1,0:T(8,128)(2,1)S(1)}, u32[]{:S(2)}, u32[]{:S(2)}) collective-permute-start(bf16[384,1024]{1,0:T(8,128)(2,1)S(1)} %add_convert_fusion.6), channel_id=1, source_target_pairs={{0,2},{1,3},{2,0},{3,1},{4,6},{5,7},{6,4},{7,5},{8,10},{9,11},{10,... | collective-permute-start | bytes 2359304 | tf_op jit(solution)/shard_map/ppermute | solution.py:568
  182.6 19.9 %collective-permute-start.17 = (bf16[384,1024]{1,0:T(8,128)(2,1)S(1)}, bf16[384,1024]{1,0:T(8,128)(2,1)S(1)}, u32[]{:S(2)}, u32[]{:S(2)}) collective-permute-start(bf16[384,1024]{1,0:T(8,128)(2,1)S(1)} %add_convert_fusion.5), channel_id=1, source_target_pairs={{0,2},{1,3},{2,0},{3,1},{4,6},{5,7},{6,4},{7,5},{8,10},{9,11},{10,... | collective-permute-start | bytes 2359304 | tf_op jit(solution)/shard_map/ppermute | solution.py:568
  232.0 19.6 %collective-permute-start.23 = (bf16[384,1024]{1,0:T(8,128)(2,1)S(1)}, bf16[384,1024]{1,0:T(8,128)(2,1)S(1)}, u32[]{:S(2)}, u32[]{:S(2)}) collective-permute-start(bf16[384,1024]{1,0:T(8,128)(2,1)S(1)} %add_convert_fusion.4), channel_id=1, source_target_pairs={{0,2},{1,3},{2,0},{3,1},{4,6},{5,7},{6,4},{7,5},{8,10},{9,11},{10,... | collective-permute-start | bytes 2359304 | tf_op jit(solution)/shard_map/ppermute | solution.py:568
  286.6 270.8 %reduce-scatter.21.cloned.1.call-start = ((), (), s32[]{:S(2)}) async-start(), calls=%async_computation.14 | async-start | bytes 2359296 | tf_op jit(solution)/shard_map/reduce_scatter | solution.py:593
  292.6 20.0 %collective-permute-start.29 = (bf16[384,1024]{1,0:T(8,128)(2,1)S(1)}, bf16[384,1024]{1,0:T(8,128)(2,1)S(1)}, u32[]{:S(2)}, u32[]{:S(2)}) collective-permute-start(bf16[384,1024]{1,0:T(8,128)(2,1)S(1)} %add_convert_fusion.3), channel_id=1, source_target_pairs={{0,2},{1,3},{2,0},{3,1},{4,6},{5,7},{6,4},{7,5},{8,10},{9,11},{10,... | collective-permute-start | bytes 2359304 | tf_op jit(solution)/shard_map/ppermute | solution.py:568
  316.5 19.6 %collective-permute-start.31 = (bf16[384,1024]{1,0:T(8,128)(2,1)}, bf16[384,1024]{1,0:T(8,128)(2,1)}, u32[]{:S(2)}, u32[]{:S(2)}) collective-permute-start(bf16[384,1024]{1,0:T(8,128)(2,1)} %get-tuple-element.122), channel_id=1, source_target_pairs={{0,2},{1,3},{2,0},{3,1},{4,6},{5,7},{6,4},{7,5},{8,10},{9,11},{10,... | collective-permute-start | bytes 2359304 | tf_op jit(solution)/shard_map/ppermute | solution.py:568
  318.3 27.0 %collective-permute-start.30 = (bf16[384,1024]{1,0:T(8,128)(2,1)}, bf16[384,1024]{1,0:T(8,128)(2,1)}, u32[]{:S(2)}, u32[]{:S(2)}) collective-permute-start(bf16[384,1024]{1,0:T(8,128)(2,1)} %get-tuple-element.122), channel_id=1, source_target_pairs={{0,1},{1,0},{2,3},{3,2},{4,5},{5,4},{6,7},{7,6},{8,9},{9,8},{10,11... | collective-permute-start | bytes 2359304 | tf_op jit(solution)/shard_map/ppermute | solution.py:568
  341.1 227.1 %reduce-scatter.19.cloned.1.call-start = ((), (), s32[]{:S(2)}) async-start(), calls=%async_computation.13 | async-start | bytes 589824 | tf_op jit(solution)/shard_map/reduce_scatter | solution.py:593
  371.6 19.9 %collective-permute-start.35 = (bf16[384,1024]{1,0:T(8,128)(2,1)S(1)}, bf16[384,1024]{1,0:T(8,128)(2,1)S(1)}, u32[]{:S(2)}, u32[]{:S(2)}) collective-permute-start(bf16[384,1024]{1,0:T(8,128)(2,1)S(1)} %add_convert_fusion.2), channel_id=1, source_target_pairs={{0,2},{1,3},{2,0},{3,1},{4,6},{5,7},{6,4},{7,5},{8,10},{9,11},{10,... | collective-permute-start | bytes 2359304 | tf_op jit(solution)/shard_map/ppermute | solution.py:568
  399.7 170.2 %reduce-scatter.17.cloned.1.call-start = ((), (), s32[]{:S(2)}) async-start(), calls=%async_computation.12 | async-start | bytes 1179648 | tf_op jit(solution)/shard_map/reduce_scatter | solution.py:593
  399.7 19.9 %collective-permute-start.36 = (bf16[384,1024]{1,0:T(8,128)(2,1)S(1)}, bf16[384,1024]{1,0:T(8,128)(2,1)}, u32[]{:S(2)}, u32[]{:S(2)}) collective-permute-start(bf16[384,1024]{1,0:T(8,128)(2,1)S(1)} %get-tuple-element.119), channel_id=1, source_target_pairs={{0,1},{1,0},{2,3},{3,2},{4,5},{5,4},{6,7},{7,6},{8,9},{9,8},{10,11... | collective-permute-start | bytes 2359304 | tf_op jit(solution)/shard_map/ppermute | solution.py:568
  418.5 207.9 %reduce-scatter.15.cloned.1.call-start = ((), (), s32[]{:S(2)}) async-start(), calls=%async_computation.11 | async-start | bytes 589824 | tf_op jit(solution)/shard_map/reduce_scatter | solution.py:593
  481.5 212.6 %reduce-scatter.13.cloned.1.call-start = ((), (), s32[]{:S(2)}) async-start(), calls=%async_computation.10 | async-start | bytes 1769472 | tf_op jit(solution)/shard_map/reduce_scatter | solution.py:593
  485.2 20.0 %collective-permute-start.41 = (bf16[384,1024]{1,0:T(8,128)(2,1)}, bf16[384,1024]{1,0:T(8,128)(2,1)}, u32[]{:S(2)}, u32[]{:S(2)}) collective-permute-start(bf16[384,1024]{1,0:T(8,128)(2,1)} %add_convert_fusion.1), channel_id=1, source_target_pairs={{0,2},{1,3},{2,0},{3,1},{4,6},{5,7},{6,4},{7,5},{8,10},{9,11},{10,... | collective-permute-start | bytes 2359304 | tf_op jit(solution)/shard_map/ppermute | solution.py:568
  492.2 272.2 %reduce-scatter.11.cloned.1.call-start = ((), (), s32[]{:S(2)}) async-start(), calls=%async_computation.9 | async-start | bytes 2359296 | tf_op jit(solution)/shard_map/reduce_scatter | solution.py:593
  536.4 298.2 %reduce-scatter.9.cloned.1.call-start = ((), (), s32[]{:S(2)}) async-start(), calls=%async_computation.8 | async-start | bytes 2359296 | tf_op jit(solution)/shard_map/reduce_scatter | solution.py:593
  566.5 19.9 %collective-permute-start.47 = (bf16[384,1024]{1,0:T(8,128)(2,1)}, bf16[384,1024]{1,0:T(8,128)(2,1)}, u32[]{:S(2)}, u32[]{:S(2)}) collective-permute-start(bf16[384,1024]{1,0:T(8,128)(2,1)} %add_convert_fusion), channel_id=1, source_target_pairs={{0,2},{1,3},{2,0},{3,1},{4,6},{5,7},{6,4},{7,5},{8,10},{9,11},{10,... | collective-permute-start | bytes 2359304 | tf_op jit(solution)/shard_map/ppermute | solution.py:568
  588.8 39.3 %collective-permute-start.48 = (f32[5120]{0:T(1024)S(1)}, f32[5120]{0:T(1024)S(1)}, u32[]{:S(2)}, u32[]{:S(2)}) collective-permute-start(f32[5120]{0:T(1024)S(1)} %constant_dynamic-update-slice_fusion.4), channel_id=1, source_target_pairs={{0,1},{1,0},{2,3},{3,2},{4,5},{5,4},{6,7},{7,6},{8,9},{9,8},{10,11... | collective-permute-start | bytes 61448 | tf_op jit(solution)/shard_map/ppermute | solution.py:568
  628.1 67.7 %collective-permute-start.49 = (f32[5120]{0:T(1024)S(1)}, f32[5120]{0:T(1024)S(1)}, u32[]{:S(2)}, u32[]{:S(2)}) collective-permute-start(f32[5120]{0:T(1024)S(1)} %add.362), channel_id=1, source_target_pairs={{0,2},{1,3},{2,0},{3,1},{4,6},{5,7},{6,4},{7,5},{8,10},{9,11},{10,... | collective-permute-start | bytes 61448 | tf_op jit(solution)/shard_map/ppermute | solution.py:568
  (151 other events, 1839.7 us)
Sparse Core Ops, SparseCore 0:
  286.8 73.0 reduce-scatter.22
  363.4 66.4 reduce-scatter.20
  433.9 61.2 reduce-scatter.18
  499.3 62.3 reduce-scatter.16
  565.5 60.9 reduce-scatter.14
  630.1 63.9 reduce-scatter.12
  697.6 66.7 reduce-scatter.10
  768.0 66.6 reduce-scatter.8

commit v2 on v1

v2 whole, which is shorter than its diff:
```python
import functools

import jax
import jax.numpy as jnp
import numpy as np
from jax import lax
from jax.experimental import pallas as pl
from jax.experimental.pallas import tpu as pltpu
from jax.sharding import PartitionSpec as P

TILE = 128
MASKED = -1e30
F32 = jnp.float32
BF16 = jnp.bfloat16


def pad_up(size, unit):
    return -(-size // unit) * unit


CHUNKS = 2


def dot(a, b, ca, cb):
    return lax.dot_general(a, b, (((ca,), (cb,)), ((), ())), preferred_element_type=F32)


def sigmoid(values):
    return 0.5 * jnp.tanh(0.5 * values) + 0.5


def fixed(*shape):
    return pl.BlockSpec(shape, lambda *_: (0,) * len(shape))


def shaped(shape, kind):
    return jax.ShapeDtypeStruct(tuple(shape), kind)


BUDGET = dict(
    distance_bias=(3, 12), enter=(1, 8), join=(2, 8), turn=(3, 12), join_back=(3, 12),
    ff_rows=(4, 28), ff_back_rows=(4, 28), project=(2, 20), expand=(2, 16),
    weight_grads=(5, 40), attend=(24, 40), attend_back=(43, 48),
    conv_forward=(11, 40), conv_backward=(17, 48),
)
COST_SCALE = 1.0


def call(body, name, out_shape, cost=1.0, **options):
    time, limit = BUDGET[name]
    time = time * cost * COST_SCALE
    return pl.pallas_call(
        body,
        out_shape=out_shape,
        compiler_params=pltpu.CompilerParams(vmem_limit_bytes=limit * 2**20),
        cost_estimate=pl.CostEstimate(
            flops=int(time * 1e9), bytes_accessed=int(time * 3.5e6), transcendentals=0
        ),
        name=name,
        **options,
    )


def tile_offsets(blocks, block_frames, per_block):
    starts = np.array([b * block_frames + t * TILE for b in range(blocks) for t in range(per_block)])
    return starts[None, :] - starts[:, None]


def bias_types(offsets, reach):
    near = sorted({int(d) for d in offsets.ravel() if abs(int(d)) < reach + TILE - 1})
    far = 4 * TILE + reach
    kinds = near + [-far, far]
    index = {d: i for i, d in enumerate(near)}
    table = np.array(
        [
            [index.get(int(d), len(near) + (1 if d > 0 else 0)) for d in row]
            for row in offsets
        ],
        np.int32,
    )
    return kinds, table


def column_onehot(kinds, reach):
    lane = lax.broadcasted_iota(jnp.int32, (len(kinds), 2 * TILE), 1)
    signed = jnp.where(lane < TILE, lane, lane - 2 * TILE)
    base = jnp.array(kinds, jnp.int32)[:, None]
    column = jnp.clip(base - signed, -reach, reach) + reach
    width = 2 * reach + 1
    flat = column.reshape(-1)
    return (flat[None, :] == jnp.arange(width, dtype=jnp.int32)[:, None]).astype(F32)


def bias_body(row_ref, out_ref, *, pairs, count):
    for p in range(pairs):
        for kind in range(count):
            for head in range(2):
                line = jnp.broadcast_to(row_ref[2 * p + head, kind : kind + 1, :], (TILE, 2 * TILE))
                skewed = pltpu.roll(line, 0, 1, stride=1, stride_axis=0)
                out_ref[p, kind, :, head * TILE : (head + 1) * TILE] = skewed[:, :TILE]


def bias_tiles(rel_table, onehot, kinds):
    heads = rel_table.shape[0]
    pairs = heads // 2
    count = len(kinds)
    rows = jnp.dot(rel_table, onehot, precision=lax.Precision.HIGHEST, preferred_element_type=F32)
    return call(
        functools.partial(bias_body, pairs=pairs, count=count),
        "distance_bias",
        shaped((pairs, count, TILE, 2 * TILE), F32),
    )(rows.reshape(heads, count, 2 * TILE))


SLAB = 16


def unit_rows(rows):
    mean = jnp.mean(rows, axis=-1, keepdims=True)
    centred = rows - mean
    rstd = lax.rsqrt(jnp.mean(centred * centred, axis=-1, keepdims=True) + 1e-05)
    return centred * rstd, rstd


def pull_back(unit, rstd, scaled):
    first = jnp.mean(scaled, axis=-1, keepdims=True)
    second = jnp.mean(scaled * unit, axis=-1, keepdims=True)
    return rstd * (scaled - first - unit * second)


def fold(values):
    return values.reshape(values.shape[0] // 8, 8, values.shape[1])


def slabs(rows, body):
    def step(i, carry):
        body(pl.ds(pl.multiple_of(i * SLAB, SLAB), SLAB))
        return carry

    lax.fori_loop(0, rows // SLAB, step, 0, unroll=2)


def enter(rows, gain):
    def body(r_ref, g_ref, h_ref):
        def slab(at):
            unit, _ = unit_rows(r_ref[at, :].astype(F32))
            h_ref[at, :] = (unit * g_ref[...]).astype(BF16)

        slabs(r_ref.shape[0], slab)

    return call(body, "enter", shaped(rows.shape, BF16))(rows, gain[None, :])


def received(at, refs):
    return refs[0][at, :].astype(F32) + refs[1][at, :].astype(F32) + refs[2][at, :].astype(F32)


def by_chunks(body, name, arrays, gain, kinds, sums=0):
    some = next(x for x in arrays if not isinstance(x, list))
    size, width = some.shape
    cut = int(size // CHUNKS)
    lone = fixed(cut, width)
    filled, lists = None, [[] for _ in kinds[1:]]
    for chunk in range(CHUNKS):
        piece = pl.BlockSpec((cut, width), lambda i, chunk=chunk: (chunk, 0))
        inputs = [x[chunk] if isinstance(x, list) else x for x in arrays]
        specs = [lone if isinstance(x, list) else piece for x in arrays]
        inputs.append(gain[None, :])
        specs.append(fixed(1, width))
        aliases = {}
        run = body
        if filled is not None:
            aliases = {len(inputs): 0}
            inputs.append(filled)
            specs.append(pl.BlockSpec(memory_space=pl.ANY))
            count = len(inputs)
            run = lambda *refs, count=count: body(*refs[: count - 1], *refs[count:])
        shapes = [shaped((size, width), kinds[0])]
        outs = [piece]
        for i, kind in enumerate(kinds[1:]):
            is_sum = i >= len(kinds) - 1 - sums
            shape = (8, width) if is_sum else (cut, width)
            shapes.append(shaped(shape, kind))
            outs.append(fixed(*shape))
        filled, *others = call(
            run, name, shapes, grid=(1,), in_specs=specs, out_specs=outs,
            input_output_aliases=aliases,
        )(*inputs)
        for place, other in zip(lists, others):
            place.append(other)
    return filled, *lists


def join(rows, parts, gain, factor):
    def body(r_ref, p1_ref, p2_ref, p3_ref, g_ref, h_ref, out_ref):
        def slab(at):
            total = r_ref[at, :].astype(F32) + factor * received(at, (p1_ref, p2_ref, p3_ref))
            out_ref[at, :] = total
            unit, _ = unit_rows(total)
            h_ref[at, :] = (unit * g_ref[...]).astype(BF16)

        slabs(r_ref.shape[0], slab)

    return by_chunks(body, "join", [rows, *parts], gain, [BF16, F32])


def turn(rows, parts, gain, cotangent, factor, onward):
    def body(r_ref, p1_ref, p2_ref, p3_ref, c_ref, g_ref, next_ref, out_ref, e_ref, sum_ref):
        sum_ref[...] = jnp.zeros_like(sum_ref)

        def slab(at):
            total = r_ref[at, :].astype(F32) + factor * received(at, (p1_ref, p2_ref, p3_ref))
            unit, rstd = unit_rows(total)
            out_ref[at, :] = (unit * g_ref[...]).astype(BF16)
            grad = c_ref[at, :].astype(F32)
            sum_ref[...] += jnp.sum(fold(grad * unit), axis=0)
            e = pull_back(unit, rstd, grad * g_ref[...])
            e_ref[at, :] = e
            next_ref[at, :] = (onward * e).astype(BF16)

        slabs(r_ref.shape[0], slab)

    return by_chunks(
        body, "turn", [rows, *parts, cotangent], gain, [BF16, BF16, F32, F32], sums=1
    )


def join_back(incoming, rows, parts, gain, onward):
    def body(e_ref, r_ref, p1_ref, p2_ref, p3_ref, g_ref, next_ref, *more):
        out_ref, sum_ref = more if onward else (next_ref, more[0])
        sum_ref[...] = jnp.zeros_like(sum_ref)

        def slab(at):
            unit, rstd = unit_rows(r_ref[at, :].astype(F32))
            grad = received(at, (p1_ref, p2_ref, p3_ref))
            sum_ref[...] += jnp.sum(fold(grad * unit), axis=0)
            e = e_ref[at, :] + pull_back(unit, rstd, grad * g_ref[...])
            out_ref[at, :] = e
            if onward:
                next_ref[at, :] = (onward * e).astype(BF16)

        slabs(r_ref.shape[0], slab)

    kinds = [BF16, F32, F32] if onward else [F32, F32]
    return by_chunks(body, "join_back", [incoming, rows, *parts], gain, kinds, sums=1)


def pieces_of(arrays):
    specs, plain = [], []
    for entry in arrays:
        array, i, n = entry if isinstance(entry, tuple) else (entry, 0, 1)
        shape = (array.shape[0] // n, array.shape[1])
        specs.append(pl.BlockSpec(shape, lambda *_, i=i: (i, 0)))
        plain.append(array)
    return specs, plain


def ff_rows(x1, x2, w_in, w_out):
    specs, plain = pieces_of([x1, x2])
    rows, width = specs[0].block_shape

    def body(x1_ref, x2_ref, w_in_ref, w_out_ref, a_ref, z_ref, u1_ref, u2_ref):
        for x_ref, u_ref, at in ((x1_ref, u1_ref, 0), (x2_ref, u2_ref, rows)):
            a = dot(x_ref[...], w_in_ref[...], 1, 0)
            z = (a * sigmoid(a)).astype(BF16)
            a_ref[at : at + rows, :] = a.astype(BF16)
            z_ref[at : at + rows, :] = z
            u_ref[...] = dot(z, w_out_ref[...], 1, 0).astype(BF16)

    wide = (2 * rows, w_in.shape[1])
    return call(
        body, "ff_rows", [shaped(wide, BF16)] * 2 + [shaped((rows, width), BF16)] * 2, grid=(1,),
        in_specs=specs + [fixed(*w_in.shape), fixed(*w_out.shape)],
        out_specs=[fixed(*wide)] * 2 + [fixed(rows, width)] * 2,
    )(*plain, w_in, w_out)


def ff_back_rows(g1, g2, a, w_out, w_in):
    specs, plain = pieces_of([g1, g2])
    rows, width = specs[0].block_shape

    def body(g1_ref, g2_ref, a_ref, w_out_ref, w_in_ref, ea_ref, p1_ref, p2_ref):
        for g_ref, p_ref, at in ((g1_ref, p1_ref, 0), (g2_ref, p2_ref, rows)):
            ez = dot(g_ref[...], w_out_ref[...], 1, 1)
            a = a_ref[at : at + rows, :].astype(F32)
            s = sigmoid(a)
            ea = (ez * s * (1.0 + a * (1.0 - s))).astype(BF16)
            ea_ref[at : at + rows, :] = ea
            p_ref[...] = dot(ea, w_in_ref[...], 1, 1).astype(BF16)

    return call(
        body, "ff_back_rows", [shaped(a.shape, BF16)] + [shaped((rows, width), BF16)] * 2,
        grid=(1,),
        in_specs=specs + [fixed(*a.shape), fixed(*w_out.shape), fixed(*w_in.shape)],
        out_specs=[fixed(*a.shape)] + [fixed(rows, width)] * 2,
    )(*plain, a, w_out, w_in)


def project(x1, x2, weight, side, kind):
    def body(x1_ref, x2_ref, w_ref, y_ref):
        rows = x1_ref.shape[0]
        y_ref[:rows, :] = dot(x1_ref[...], w_ref[...], 1, side).astype(kind)
        y_ref[rows:, :] = dot(x2_ref[...], w_ref[...], 1, side).astype(kind)

    shape = (2 * x1.shape[0], weight.shape[1 - side])
    return call(body, "project", shaped(shape, kind))(x1, x2, weight)


def expand(x1, x2, weight, side):
    specs, plain = pieces_of([x1, x2])

    def body(x1_ref, x2_ref, w_ref, y1_ref, y2_ref):
        y1_ref[...] = dot(x1_ref[...], w_ref[...], 1, side).astype(BF16)
        y2_ref[...] = dot(x2_ref[...], w_ref[...], 1, side).astype(BF16)

    shape = (specs[0].block_shape[0], weight.shape[1 - side])
    return call(
        body, "expand", [shaped(shape, BF16)] * 2, grid=(1,),
        in_specs=specs + [fixed(*weight.shape)],
        out_specs=[fixed(*shape)] * 2,
    )(*plain, weight)


def weight_grads(products, pieces=1):
    entries, spans, at, column = [], [], 0, 0
    for left, right in products:
        entries += left + right
        first = right[0][0] if isinstance(right[0], tuple) else right[0]
        spans.append((at, at + len(left), at + len(left) + len(right), column))
        at += len(left) + len(right)
        column += first.shape[1]
    specs, plain = pieces_of(entries)
    height = specs[0].block_shape[1]
    cut = column // pieces

    def body(*refs):
        out_refs = refs[at:]
        for first, middle, last, column in spans:
            left = jnp.concatenate([ref[...] for ref in refs[first:middle]], 0)
            right = jnp.concatenate([ref[...] for ref in refs[middle:last]], 0)
            value = dot(left, right, 0, 0).astype(BF16)
            if pieces == 1:
                out_refs[0][:, column : column + right.shape[1]] = value
            else:
                for i, out_ref in enumerate(out_refs):
                    out_ref[...] = value[:, i * cut : (i + 1) * cut]

    return call(
        body, "weight_grads", [shaped((height, cut), BF16)] * pieces, grid=(1,),
        in_specs=specs, out_specs=[fixed(height, cut)] * pieces,
    )(*plain)


def stacked_heads(pair):
    low_half = lax.broadcasted_iota(jnp.int32, pair.shape, 1) < pair.shape[1] // 2
    zero = jnp.zeros_like(pair)
    return jnp.concatenate([jnp.where(low_half, pair, zero), jnp.where(low_half, zero, pair)], 0)


def own_quadrants(wide):
    half = lax.broadcasted_iota(jnp.int32, (TILE, TILE), 0) < TILE // 2
    return jnp.where(half, wide[:, :TILE], wide[:, TILE:])


def assemble(target_ref, piece_refs):
    rows = piece_refs[0].shape[0]
    for i, ref in enumerate(piece_refs):
        target_ref[i * rows : (i + 1) * rows, :] = ref[...]


def tile_rows(index):
    return pl.ds(pl.multiple_of(index * TILE, TILE), TILE)


def attend_body(
    place_ref, start_ref, count_ref, kind_ref, *refs, tiles, pairs, scale,
):
    pieces, refs = refs[:2], refs[2:]
    bias_ref, lab_ref, labrow_ref, out_ref, lse_ref, qkv_ref, score_ref, turned_ref, acc_ref = refs
    step = pl.program_id(0)
    width = pairs * TILE

    @pl.when(step == 0)
    def _():
        assemble(qkv_ref, pieces)
        for tile in range(tiles):
            turned_ref[tile] = qkv_ref[tile_rows(place_ref[tile]), 2 * width :].T

    mine = qkv_ref[tile_rows(place_ref[step]), :]
    queries = [
        stacked_heads(mine[:, p * TILE : (p + 1) * TILE] * scale) for p in range(pairs)
    ]
    own_label = labrow_ref[step]
    begin = start_ref[step]
    trips = count_ref[step]

    def scores(trip, best):
        couple = [begin + 2 * trip + sub for sub in range(2)]
        kinds = [kind_ref[step * tiles + tile] for tile in couple]
        allowed = [lab_ref[tile] == own_label for tile in couple]
        keys = jnp.concatenate(
            [qkv_ref[tile_rows(place_ref[tile]), width : 2 * width] for tile in couple], 0
        )
        parts = []
        for p in range(pairs):
            both = dot(keys[:, p * TILE : (p + 1) * TILE], queries[p], 1, 1)
            highs = []
            for sub in range(2):
                raw = both[sub * TILE : (sub + 1) * TILE] + bias_ref[p, kinds[sub]]
                pair_high = []
                for h in range(2):
                    part = jnp.where(allowed[sub], raw[:, h * TILE : (h + 1) * TILE], MASKED)
                    span = slice((2 * p + h) * TILE, (2 * p + h + 1) * TILE)
                    score_ref[couple[sub], :, span] = part
                    pair_high.append(jnp.max(fold(part), axis=0))
                highs.append(jnp.concatenate(pair_high, 1))
            parts.append(jnp.maximum(*highs))
        return jnp.maximum(best, jnp.concatenate(parts, 1))

    best = lax.fori_loop(0, trips, scores, jnp.full((8, 2 * width), MASKED, F32))
    top = jnp.max(best, axis=0, keepdims=True)
    acc_ref[...] = jnp.zeros_like(acc_ref)

    def mix(trip, total):
        first = begin + 2 * trip
        probs = []
        for sub in range(2):
            value = jnp.exp(score_ref[first + sub] - top)
            total = total + jnp.sum(fold(value), axis=0)
            probs.append(value.astype(BF16))
        both = jnp.concatenate(probs, 0)
        for p in range(pairs):
            turned = jnp.concatenate(
                [turned_ref[first + sub, p * TILE : (p + 1) * TILE, :] for sub in range(2)], 1
            )
            acc_ref[p] += dot(turned, both[:, 2 * p * TILE : 2 * (p + 1) * TILE], 1, 0)
        return total

    total = lax.fori_loop(0, trips, mix, jnp.zeros((8, 2 * width), F32))
    total = jnp.sum(total, axis=0, keepdims=True)
    inverse = 1.0 / total
    log_total = top + jnp.log(total)
    for p in range(pairs):
        wide = acc_ref[p] * inverse[:, 2 * p * TILE : 2 * (p + 1) * TILE]
        out_ref[:, p * TILE : (p + 1) * TILE] = own_quadrants(wide).T.astype(BF16)
    for h in range(2 * pairs):
        lse_ref[0, h : h + 1, :] = log_total[:, h * TILE : (h + 1) * TILE]


def attend(pieces, bias, plan):
    pairs = bias.shape[0]
    width = pairs * TILE
    tiles = plan["tiles"]
    rows = tiles * TILE
    return call(
        functools.partial(attend_body, tiles=tiles, pairs=pairs, scale=plan["scale"]),
        "attend",
        [
            shaped((rows, width), BF16),
            shaped((tiles, 2 * pairs, TILE), F32),
            shaped((rows, 3 * width), BF16),
        ],
        grid_spec=pltpu.PrefetchScalarGridSpec(
            num_scalar_prefetch=4,
            grid=(tiles,),
            in_specs=[fixed(*piece.shape) for piece in pieces]
            + [fixed(*bias.shape), fixed(tiles, TILE, TILE), fixed(tiles, 1, TILE)],
            out_specs=[
                pl.BlockSpec((TILE, width), lambda i, place, *_: (place[i], 0)),
                pl.BlockSpec((1, 2 * pairs, TILE), lambda i, *_: (i, 0, 0)),
                fixed(rows, 3 * width),
            ],
            scratch_shapes=[
                pltpu.VMEM((tiles, TILE, 2 * width), F32),
                pltpu.VMEM((tiles, width, TILE), BF16),
                pltpu.VMEM((pairs, TILE, 2 * TILE), F32),
            ],
        ),
    )(
        plan["place"], plan["start"], plan["count"], plan["kind"],
        *pieces, bias, plan["lab"], plan["labrow"],
    )


def unskew(values):
    wide = jnp.concatenate([values, jnp.zeros_like(values)], 1)
    rows = TILE
    while rows > 8:
        rows //= 2
        wide = wide[:rows] + pltpu.roll(wide[rows:], 2 * TILE - rows, 1)
    row = lax.broadcasted_iota(jnp.int32, wide.shape, 0)
    for bit in (4, 2, 1):
        wide = jnp.where((row & bit) != 0, pltpu.roll(wide, 2 * TILE - bit, 1), wide)
    return jnp.sum(wide, axis=0, keepdims=True)


def attend_back_body(
    place_ref, start_ref, count_ref, kind_ref, *refs, tiles, pairs, scale, kinds,
):
    pieces, refs = refs[:2], refs[2:]
    (
        qkv_ref, bias_ref, lab_ref, labrow_ref, out_ref, lse_ref,
        dqkv_ref, table_ref,
        grad_ref, turned_ref, dk_ref, dv_ref, dq_ref, sums_ref,
    ) = refs
    step = pl.program_id(0)
    width = pairs * TILE

    @pl.when(step == 0)
    def _():
        assemble(grad_ref, pieces)
        for tile in range(tiles):
            turned_ref[tile] = qkv_ref[tile_rows(place_ref[tile]), width : 2 * width].T
        dk_ref[...] = jnp.zeros_like(dk_ref)
        dv_ref[...] = jnp.zeros_like(dv_ref)
        sums_ref[...] = jnp.zeros_like(sums_ref)

    here = tile_rows(place_ref[step])
    queries, grads, deltas, logs = [], [], [], []
    for p in range(pairs):
        span = slice(p * TILE, (p + 1) * TILE)
        queries.append(stacked_heads(qkv_ref[here, span] * scale))
        grad = grad_ref[here, span]
        grads.append(stacked_heads(grad))
        product = (grad.astype(F32) * out_ref[here, span].astype(F32)).T
        half = TILE // 2
        deltas.append(
            jnp.concatenate(
                [
                    jnp.sum(product[:half], axis=0, keepdims=True),
                    jnp.sum(product[half:], axis=0, keepdims=True),
                ],
                1,
            )
        )
        logs.append(jnp.concatenate([lse_ref[step, 2 * p + h : 2 * p + h + 1, :] for h in range(2)], 1))
    own_label = labrow_ref[step]
    begin = start_ref[step]
    dq_ref[...] = jnp.zeros_like(dq_ref)

    def visit(trip, carry):
        couple = [begin + 2 * trip + sub for sub in range(2)]
        kind = [kind_ref[step * tiles + tile] for tile in couple]
        there = [tile_rows(place_ref[tile]) for tile in couple]
        allowed = jnp.concatenate([lab_ref[tile] == own_label for tile in couple], 0)
        allowed = jnp.concatenate([allowed, allowed], 1)
        for p in range(pairs):
            span = slice(p * TILE, (p + 1) * TILE)
            key_span = slice(width + p * TILE, width + (p + 1) * TILE)
            value_span = slice(2 * width + p * TILE, 2 * width + (p + 1) * TILE)
            keys = jnp.concatenate([qkv_ref[at, key_span] for at in there], 0)
            vals = jnp.concatenate([qkv_ref[at, value_span] for at in there], 0)
            bias = jnp.concatenate([bias_ref[p, k] for k in kind], 0)
            raw = dot(keys, queries[p], 1, 1) + bias
            prob = jnp.exp(jnp.where(allowed, raw - logs[p], MASKED))
            lift = dot(vals, grads[p], 1, 1)
            slope = prob * (lift - deltas[p])
            low = slope.astype(BF16)
            dv = dot(prob.astype(BF16), grads[p], 1, 0)
            dk = dot(low, queries[p], 1, 0)
            for sub in range(2):
                part = slice(sub * TILE, (sub + 1) * TILE)
                sums_ref[p, kind[sub]] += slope[part]
                dv_ref[couple[sub], :, span] += dv[part]
                dk_ref[couple[sub], :, span] += dk[part]
            turned = jnp.concatenate([turned_ref[tile, span, :] for tile in couple], 1)
            dq_ref[p] += dot(turned, low, 1, 0)
        return carry

    lax.fori_loop(0, count_ref[step], visit, 0)
    for p in range(pairs):
        span = slice(p * TILE, (p + 1) * TILE)
        dqkv_ref[here, span] = (own_quadrants(dq_ref[p]).T * scale).astype(BF16)

    @pl.when(step == tiles - 1)
    def _():
        for tile in range(tiles):
            there = tile_rows(place_ref[tile])
            dqkv_ref[there, width : 2 * width] = dk_ref[tile].astype(BF16)
            dqkv_ref[there, 2 * width :] = dv_ref[tile].astype(BF16)
        for p in range(pairs):
            for kind in range(kinds):
                for h in range(2):
                    table_ref[2 * p + h, kind : kind + 1, :] = unskew(
                        sums_ref[p, kind, :, h * TILE : (h + 1) * TILE]
                    )


def attend_back(pieces, qkv, bias, plan, out, lse):
    tiles, pairs, kinds = plan["tiles"], bias.shape[0], bias.shape[1]
    width = pairs * TILE
    rows = tiles * TILE
    return call(
        functools.partial(
            attend_back_body, tiles=tiles, pairs=pairs, scale=plan["scale"], kinds=kinds
        ),
        "attend_back",
        [shaped((rows, 3 * width), BF16), shaped((2 * pairs, kinds, 2 * TILE), F32)],
        grid_spec=pltpu.PrefetchScalarGridSpec(
            num_scalar_prefetch=4,
            grid=(tiles,),
            in_specs=[fixed(*piece.shape) for piece in pieces]
            + [
                fixed(*qkv.shape), fixed(*bias.shape), fixed(tiles, TILE, TILE),
                fixed(tiles, 1, TILE), fixed(*out.shape), fixed(*lse.shape),
            ],
            out_specs=[fixed(rows, 3 * width), fixed(2 * pairs, kinds, 2 * TILE)],
            scratch_shapes=[
                pltpu.VMEM((rows, width), BF16),
                pltpu.VMEM((tiles, width, TILE), BF16),
                pltpu.VMEM((tiles, TILE, width), F32),
                pltpu.VMEM((tiles, TILE, width), F32),
                pltpu.VMEM((pairs, TILE, 2 * TILE), F32),
                pltpu.VMEM((pairs, kinds, TILE, 2 * TILE), F32),
            ],
        ),
    )(
        plan["place"], plan["start"], plan["count"], plan["kind"],
        *pieces, qkv, bias, plan["lab"], plan["labrow"], out, lse,
    )


EDGE = 16


def conv_body(
    order_ref, low_ref, high_ref, *refs, blocks, frames, chunks, lanes, taps,
):
    pieces, refs = refs[:2], refs[2:]
    taps_ref, lab_ref, act_ref, gated_ref, mixed_ref, glu_ref, window_ref, pad_ref, out_pad_ref = refs
    size = glu_ref.shape[0] // blocks
    assemble(glu_ref, pieces)
    channels = lanes * TILE
    half = taps // 2
    span = TILE + 2 * EDGE
    for lane in range(lanes):
        pad_ref[lane, :EDGE, :] = jnp.zeros((EDGE, TILE), F32)
    for block in range(blocks):
        here = pl.ds(pl.multiple_of(order_ref[block] * size, TILE), size)
        for lane in range(lanes):
            value = glu_ref[here, lane * TILE : (lane + 1) * TILE]
            gate = glu_ref[here, channels + lane * TILE : channels + (lane + 1) * TILE]
            first = EDGE + block * frames
            pad_ref[lane, first : first + size, :] = value * sigmoid(gate)
    rest = EDGE + (blocks - 1) * frames + size
    for lane in range(lanes):
        tail = pad_ref.shape[1] - rest
        pad_ref[lane, rest:, :] = jnp.zeros((tail, TILE), F32)

    def chunk(index, carry):
        base = pl.multiple_of(index * TILE, TILE)
        labels = lab_ref[pl.ds(base, span), :]
        center = labels[EDGE : EDGE + TILE]
        for lane in range(lanes):
            values = pad_ref[lane, pl.ds(base, span), :]
            gated_ref[pl.ds(base, TILE), lane * TILE : (lane + 1) * TILE] = values[
                EDGE : EDGE + TILE
            ]

            def segment(label, total):
                window_ref[...] = jnp.where(labels == label, values, 0.0)
                acc = jnp.zeros((TILE, TILE), F32)
                for tap in range(taps):
                    first = EDGE + tap - half
                    acc = acc + window_ref[first : first + TILE, :] * taps_ref[
                        tap : tap + 1, lane * TILE : (lane + 1) * TILE
                    ]
                return jnp.where(center == label, acc, total)

            total = lax.fori_loop(
                low_ref[index], high_ref[index] + 1, segment, jnp.zeros((TILE, TILE), F32)
            )
            mixed_ref[pl.ds(base, TILE), lane * TILE : (lane + 1) * TILE] = total
            out_pad_ref[lane, pl.ds(base, TILE), :] = total * sigmoid(total)
        return carry

    lax.fori_loop(0, chunks, chunk, 0)
    valid = lax.broadcasted_iota(jnp.int32, (size, TILE), 0) < frames
    for block in range(blocks):
        here = pl.ds(pl.multiple_of(order_ref[block] * size, TILE), size)
        for lane in range(lanes):
            rows = out_pad_ref[lane, block * frames : block * frames + size, :]
            act_ref[here, lane * TILE : (lane + 1) * TILE] = jnp.where(valid, rows, 0.0).astype(BF16)


def conv_forward(pieces, taps, plan):
    channels = pieces[0].shape[1] // 2
    blocks, frames, chunks = 4, plan["frames"], plan["chunks"]
    total = plan["tiles"] * TILE
    rows = chunks * TILE
    lanes = channels // TILE
    return call(
        functools.partial(
            conv_body, blocks=blocks, frames=frames, chunks=chunks, lanes=lanes, taps=taps.shape[0]
        ),
        "conv_forward",
        [
            shaped((total, channels), BF16),
            shaped((rows, channels), F32),
            shaped((rows, channels), F32),
            shaped((total, 2 * channels), F32),
        ],
        grid_spec=pltpu.PrefetchScalarGridSpec(
            num_scalar_prefetch=3,
            grid=(1,),
            in_specs=[fixed(*piece.shape) for piece in pieces]
            + [fixed(*taps.shape), fixed(*plan["flat_lab"].shape)],
            out_specs=[
                fixed(total, channels), fixed(rows, channels), fixed(rows, channels),
                fixed(total, 2 * channels),
            ],
            scratch_shapes=[
                pltpu.VMEM((TILE + 2 * EDGE, TILE), F32),
                pltpu.VMEM((lanes, rows + 2 * EDGE, TILE), F32),
                pltpu.VMEM((lanes, rows, TILE), F32),
            ],
        ),
    )(plan["order"], plan["low"], plan["high"], *pieces, taps, plan["flat_lab"])


def conv_back_body(
    order_ref, low_ref, high_ref, *refs, blocks, frames, chunks, lanes, taps,
):
    pieces, refs = refs[:2], refs[2:]
    (
        glu_ref, taps_ref, lab_ref, gated_ref, mixed_ref,
        dglu_ref, dtaps_ref,
        grad_ref, window_ref, source_ref, slope_ref, dgate_ref, sums_ref,
    ) = refs
    size = glu_ref.shape[0] // blocks
    assemble(grad_ref, pieces)
    channels = lanes * TILE
    half = taps // 2
    span = TILE + 2 * EDGE
    rows = chunks * TILE
    for block in range(blocks):
        here = pl.ds(pl.multiple_of(order_ref[block] * size, TILE), size)
        for lane in range(lanes):
            first = EDGE + block * frames
            slope_ref[lane, first : first + size, :] = grad_ref[
                here, lane * TILE : (lane + 1) * TILE
            ]
    rest = EDGE + (blocks - 1) * frames + size
    for lane in range(lanes):
        slope_ref[lane, :EDGE, :] = jnp.zeros((EDGE, TILE), F32)
        slope_ref[lane, rest:, :] = jnp.zeros((slope_ref.shape[1] - rest, TILE), F32)
        mixed = mixed_ref[:, lane * TILE : (lane + 1) * TILE]
        gate = sigmoid(mixed)
        slope_ref[lane, EDGE : EDGE + rows, :] = slope_ref[lane, EDGE : EDGE + rows, :] * (
            gate * (1.0 + mixed * (1.0 - gate))
        )
        source_ref[lane, :EDGE, :] = jnp.zeros((EDGE, TILE), F32)
        source_ref[lane, EDGE : EDGE + rows, :] = gated_ref[:, lane * TILE : (lane + 1) * TILE]
        source_ref[lane, EDGE + rows :, :] = jnp.zeros((EDGE, TILE), F32)
        dgate_ref[lane, rows:, :] = jnp.zeros((dgate_ref.shape[1] - rows, TILE), F32)
    sums_ref[...] = jnp.zeros_like(sums_ref)

    def chunk(index, carry):
        base = pl.multiple_of(index * TILE, TILE)
        labels = lab_ref[pl.ds(base, span), :]
        center = labels[EDGE : EDGE + TILE]
        for lane in range(lanes):
            slopes = slope_ref[lane, pl.ds(base, span), :]
            sources = source_ref[lane, pl.ds(base, span), :]

            def segment(label, total):
                window_ref[0] = jnp.where(labels == label, slopes, 0.0)
                window_ref[1] = jnp.where(labels == label, sources, 0.0)
                inner = window_ref[0, EDGE : EDGE + TILE, :]
                acc = jnp.zeros((TILE, TILE), F32)
                for tap in range(taps):
                    first = EDGE - tap + half
                    acc = acc + window_ref[0, first : first + TILE, :] * taps_ref[
                        tap : tap + 1, lane * TILE : (lane + 1) * TILE
                    ]
                    first = EDGE + tap - half
                    part = fold(inner * window_ref[1, first : first + TILE, :])
                    sums_ref[lane, tap] += jnp.sum(part, axis=0)
                return jnp.where(center == label, acc, total)

            dgate_ref[lane, pl.ds(base, TILE), :] = lax.fori_loop(
                low_ref[index], high_ref[index] + 1, segment, jnp.zeros((TILE, TILE), F32)
            )
        return carry

    lax.fori_loop(0, chunks, chunk, 0)
    for lane in range(lanes):
        dtaps_ref[:, lane * TILE : (lane + 1) * TILE] = jnp.sum(sums_ref[lane], axis=1)
    valid = lax.broadcasted_iota(jnp.int32, (size, TILE), 0) < frames
    for block in range(blocks):
        here = pl.ds(pl.multiple_of(order_ref[block] * size, TILE), size)
        for lane in range(lanes):
            lead = slice(lane * TILE, (lane + 1) * TILE)
            follow = slice(channels + lane * TILE, channels + (lane + 1) * TILE)
            rows_in = dgate_ref[lane, block * frames : block * frames + size, :]
            rows_in = jnp.where(valid, rows_in, 0.0)
            value = glu_ref[here, lead]
            gate = sigmoid(glu_ref[here, follow])
            dglu_ref[here, lead] = (rows_in * gate).astype(BF16)
            dglu_ref[here, follow] = (rows_in * value * gate * (1.0 - gate)).astype(BF16)


def conv_backward(pieces, glu, taps, plan, gated, mixed):
    channels = glu.shape[1] // 2
    blocks, frames, chunks = 4, plan["frames"], plan["chunks"]
    rows = chunks * TILE
    lanes = channels // TILE
    return call(
        functools.partial(
            conv_back_body, blocks=blocks, frames=frames, chunks=chunks,
            lanes=lanes, taps=taps.shape[0],
        ),
        "conv_backward",
        [shaped(glu.shape, BF16), shaped(taps.shape, F32)],
        grid_spec=pltpu.PrefetchScalarGridSpec(
            num_scalar_prefetch=3,
            grid=(1,),
            in_specs=[fixed(*piece.shape) for piece in pieces]
            + [
                fixed(*glu.shape), fixed(*taps.shape), fixed(*plan["flat_lab"].shape),
                fixed(rows, channels), fixed(rows, channels),
            ],
            out_specs=[fixed(*glu.shape), fixed(*taps.shape)],
            scratch_shapes=[
                pltpu.VMEM((glu.shape[0], channels), F32),
                pltpu.VMEM((2, TILE + 2 * EDGE, TILE), F32),
                pltpu.VMEM((lanes, rows + 2 * EDGE, TILE), F32),
                pltpu.VMEM((lanes, rows + 2 * EDGE, TILE), F32),
                pltpu.VMEM((lanes, rows + EDGE, TILE), F32),
                pltpu.VMEM((lanes, taps.shape[0], 8, TILE), F32),
            ],
        ),
    )(
        plan["order"], plan["low"], plan["high"],
        *pieces, glu, taps, plan["flat_lab"], gated, mixed,
    )


def swap(values, bit, axis="tensor"):
    count = lax.axis_size(axis)
    return lax.ppermute(values, axis, [(i, i ^ bit) for i in range(count)])


def gather(mine):
    return [mine, swap(mine, 1), swap(mine, 2)]


def tie(value, other):
    return lax.optimization_barrier((value, other))


def complete(blocks, near):
    blocks[2], near[0] = tie(blocks[2], near[0])
    blocks.append(swap(blocks[2], 1))


def scatter(own, beside, far):
    arriving = []
    for across, diagonal in far:
        outgoing = (across.astype(F32) + swap(diagonal, 1).astype(F32)).astype(BF16)
        arriving.append(swap(outgoing, 2))
    return [own, swap(beside, 1), arriving]


def sum_bits(values, axis):
    bit = 1
    while bit < lax.axis_size(axis):
        values = values + swap(values, bit, axis)
        bit *= 2
    return values


def settle_halving(grad, first_bits):
    count = lax.axis_size("dp")
    bits = count.bit_length() - 1
    here = lax.axis_index("dp")
    values = grad.astype(BF16).reshape((2,) * bits + (grad.shape[0] // count, grad.shape[1]))
    left = list(range(bits - 1, -1, -1))
    order = [b for b in first_bits if b < bits] + [b for b in range(bits) if b not in first_bits]
    for bit in order:
        dim = left.index(bit)
        keep = (here >> bit) & 1
        sent = lax.dynamic_index_in_dim(values, 1 - keep, dim, keepdims=False)
        kept = lax.dynamic_index_in_dim(values, keep, dim, keepdims=False)
        values = kept.astype(F32) + swap(sent, 1 << bit, "dp").astype(F32)
        left.pop(dim)
        if left:
            values = values.astype(BF16)
    return values


def settle(grads):
    return lax.psum_scatter(grads, "dp", scatter_dimension=0, tiled=True).astype(F32)


PIECES = 2


def settle_split(grads):
    return jnp.concatenate([settle_halving(grad, (0, 1, 2)) for grad in grads], 1)


def halves(array):
    return [(array, c, CHUNKS) for c in range(CHUNKS)]


def feed_forward(blocks, w_in, w_out):
    near = list(ff_rows(blocks[0], blocks[1], w_in, w_out))
    complete(blocks, near)
    far = [ff_rows(x1, x2, w_in, w_out) for x1, x2 in zip(halves(blocks[2]), halves(blocks[3]))]
    state = ([near[0]] + [f[0] for f in far], [near[1]] + [f[1] for f in far])
    return scatter(near[2], near[3], [f[2:] for f in far]), state


def feed_back(blocks, state, w_in, w_out):
    hidden, _ = state
    near = list(ff_back_rows(blocks[0], blocks[1], hidden[0], w_out, w_in))
    complete(blocks, near)
    far = [
        ff_back_rows(g1, g2, a, w_out, w_in)
        for g1, g2, a in zip(halves(blocks[2]), halves(blocks[3]), hidden[1:])
    ]
    return scatter(near[1], near[2], [f[1:] for f in far]), [near[0]] + [f[0] for f in far]


def zigzag(blocks):
    far = [item for pair in zip(halves(blocks[2]), halves(blocks[3])) for item in pair]
    return [blocks[0], blocks[1]] + far


def spread(blocks, weight, side, kind):
    near = [project(blocks[0], blocks[1], weight, side, kind)]
    complete(blocks, near)
    return near[0], project(blocks[2], blocks[3], weight, side, kind)


def collect(flat, weight, side):
    count = 4 * CHUNKS
    far = [
        expand((flat, 2 * CHUNKS + c, count), (flat, 3 * CHUNKS + c, count), weight, side)
        for c in range(CHUNKS)
    ]
    own, beside = expand((flat, 0, 4), (flat, 1, 4), weight, side)
    return scatter(own, beside, far)


def delayed(parts, other):
    own, beside, (first, *rest) = parts
    first, other = tie(first, other)
    return [own, beside, [first, *rest]], other


def make_plan(segments, frames, reach, head_width):
    blocks = lax.axis_size("tensor")
    here = lax.axis_index("tensor").astype(jnp.int32)
    size = pad_up(frames, TILE)
    per_block = size // TILE
    tiles = blocks * per_block
    offsets = tile_offsets(blocks, frames, per_block)
    kinds, table = bias_types(offsets, reach)
    flat = segments.reshape(-1).astype(jnp.int32)
    lab = jnp.pad(flat.reshape(blocks, frames), ((0, 0), (0, size - frames)), constant_values=-1)
    lab = lab.reshape(tiles, TILE)
    high = jnp.max(lab, axis=1)
    low = jnp.min(jnp.where(lab < 0, 1 << 20, lab), axis=1)
    seen = (low[:, None] <= high[None, :]) & (low[None, :] <= high[:, None])
    position = jnp.arange(tiles, dtype=jnp.int32)
    first = jnp.min(jnp.where(seen, position[None, :], tiles), axis=1)
    last = jnp.max(jnp.where(seen, position[None, :], -1), axis=1)
    count1 = last - first + 1
    count = (count1 + 1) // 2
    start = jnp.minimum(first, tiles - 2 * count)
    order = jnp.arange(blocks, dtype=jnp.int32) ^ here
    place = (order[:, None] * per_block + jnp.arange(per_block, dtype=jnp.int32)[None, :]).reshape(-1)
    total = blocks * frames
    chunks = pad_up(total, TILE) // TILE
    padded = jnp.pad(flat, (EDGE, chunks * TILE - total + EDGE), constant_values=-1)
    body = padded[EDGE : EDGE + chunks * TILE].reshape(chunks, TILE)
    return dict(
        kinds=kinds,
        kind=jnp.asarray(table.reshape(-1)),
        place=place,
        tiles=tiles,
        start=start,
        count=count,
        lab=jnp.broadcast_to(lab[:, :, None], (tiles, TILE, TILE)),
        labrow=lab[:, None, :],
        scale=float(head_width) ** -0.5,
        frames=frames,
        chunks=chunks,
        order=order,
        low=jnp.min(jnp.where(body < 0, 1 << 20, body), axis=1),
        high=jnp.max(body, axis=1),
        flat_lab=jnp.broadcast_to(padded[:, None], (padded.shape[0], TILE)),
    )


def shards(
    inputs, segments, cotangent, gain_one, first_in, first_out, gain_two, w_query, w_key, w_value,
    w_output, rel_table, gain_three, w_glu, kernel, w_back, gain_four, second_in, second_out,
    gain_five,
):
    frames, _, width = inputs.shape
    size = pad_up(frames, TILE)
    heads = rel_table.shape[0]
    reach = rel_table.shape[1] // 2
    head_width = w_query.shape[1] // heads

    def padded(values):
        return jnp.pad(values.reshape(frames, width), ((0, size - frames), (0, 0)))

    def total(sums):
        return sum(jnp.sum(part, axis=0) for part in sums)

    plan = make_plan(segments, frames, reach, head_width)
    onehot = column_onehot(plan["kinds"], reach)
    bias = bias_tiles(rel_table, onehot, plan["kinds"])
    w_qkv = jnp.concatenate([w_query, w_key, w_value], 1)
    channels = kernel.shape[1]
    glu_matrix = w_glu.reshape(width, 2 * channels)

    start = padded(inputs)
    h_one = gather(enter(start, gain_one))
    parts, state_one = feed_forward(h_one, first_in, first_out)
    h_two, one = join(start, parts, gain_two, 0.5)
    h_two = gather(h_two)
    out, lse, qkv = attend(spread(h_two, w_qkv, 0, BF16), bias, plan)
    h_three, two = join(one, collect(out, w_output, 0), gain_three, 1.0)
    h_three = gather(h_three)
    act, gated, mixed, glu = conv_forward(spread(h_three, glu_matrix, 0, F32), kernel, plan)
    h_four, three = join(two, collect(act, w_back, 0), gain_four, 1.0)
    h_four = gather(h_four)
    parts, state_four = feed_forward(h_four, second_in, second_out)

    grads, output, e4, sums = turn(three, parts, gain_five, padded(cotangent), 0.5, 0.5)
    grad_five = total(sums)
    grads = gather(grads)
    parts, inner = feed_back(grads, state_four, second_in, second_out)
    parts, grad_w = delayed(
        parts, weight_grads([(zigzag(grads), state_four[1]), (zigzag(h_four), inner)])[0]
    )
    settled_four = settle(grad_w)
    grads, e3, sums = join_back(e4, three, parts, gain_four, 1.0)
    grad_four = total(sums)
    grads = gather(grads)
    dglu, grad_kernel = conv_backward(
        spread(grads, w_back, 1, F32), glu, kernel, plan, gated, mixed
    )
    parts, grad_w = delayed(
        collect(dglu, glu_matrix, 1), weight_grads([(grads, [act]), (h_three, [dglu])])[0]
    )
    settled_three = settle(grad_w)
    grads, e2, sums = join_back(e3, two, parts, gain_three, 1.0)
    grad_three = total(sums)
    grads = gather(grads)
    pulled = spread(grads, w_output, 1, BF16)
    dqkv, table_sums = attend_back(pulled, qkv, bias, plan, out, lse)
    dqkv, settled_four = tie(dqkv, settled_four)
    parts, grad_w = delayed(
        collect(dqkv, w_qkv, 1), weight_grads([(grads, [out]), (h_two, [dqkv])])[0]
    )
    settled_two = settle(grad_w)
    grads, e1, sums = join_back(e2, one, parts, gain_two, 0.5)
    grad_two = total(sums)
    grads = gather(grads)
    grads[0], settled_three = tie(grads[0], settled_three)
    parts, inner = feed_back(grads, state_one, first_in, first_out)
    grad_w, = weight_grads([(zigzag(grads), state_one[1])])
    parts, grad_first_in = delayed(parts, weight_grads([(zigzag(h_one), inner)], PIECES))
    parts, grad_w = delayed(parts, grad_w)
    grad_first_out = settle(grad_w)
    small, grad_first_in = tie(
        (table_sums, grad_kernel, grad_two, grad_three, grad_four, grad_five), grad_first_in
    )
    table_sums, grad_kernel, grad_two, grad_three, grad_four, grad_five = small
    grad_first_in = settle_split(grad_first_in)
    e0, sums = join_back(e1, start, parts, gain_one, 0.0)
    grad_one = total(sums)
    grad_table = lax.dot_general(
        table_sums.reshape(heads, -1), onehot, (((1,), (1,)), ((), ())),
        precision=lax.Precision.HIGHEST, preferred_element_type=F32,
    )
    gains = sum_bits(jnp.concatenate([grad_two, grad_three, grad_four, grad_five]), "tensor")
    small = jnp.concatenate([gains, grad_table.reshape(-1), grad_kernel.reshape(-1)])
    small = sum_bits(small, "dp")
    grad_one = sum_bits(sum_bits(grad_one, "tensor"), "dp")
    grad_gains = [grad_one] + [small[i * width : (i + 1) * width] for i in range(4)]
    rest = small[4 * width :]
    grad_table = rest[: grad_table.size].reshape(grad_table.shape)
    grad_kernel = rest[grad_table.size :].reshape(grad_kernel.shape)
    part, own = w_query.shape[1], w_output.shape[0]
    return (
        jnp.concatenate(output, 0)[:frames].reshape(inputs.shape),
        e0[:frames].reshape(inputs.shape),
        grad_gains[0],
        grad_first_in,
        grad_first_out.T,
        grad_gains[1],
        settled_two[:, own : own + part],
        settled_two[:, own + part : own + 2 * part],
        settled_two[:, own + 2 * part :],
        settled_two[:, :own].T,
        grad_table,
        grad_gains[2],
        settled_three[:, channels:].reshape(-1, 2, channels),
        grad_kernel,
        settled_three[:, :channels].T,
        grad_gains[3],
        settled_four[:, second_out.shape[0] :],
        settled_four[:, : second_out.shape[0]].T,
        grad_gains[4],
    )


def solution(mesh):
    in_specs = (
        P("tensor", "dp", None), P("dp", None), P("tensor", "dp", None), P(),
        P(None, "tensor"), P("tensor", None), P(), P(None, "tensor"), P(None, "tensor"),
        P(None, "tensor"), P("tensor", None), P("tensor", None), P(), P(None, None, "tensor"),
        P(None, "tensor"), P("tensor", None), P(), P(None, "tensor"), P("tensor", None), P(),
    )
    out_specs = (
        P("tensor", "dp", None), P("tensor", "dp", None), P(), P("dp", "tensor"),
        P("tensor", "dp"), P(), P("dp", "tensor"), P("dp", "tensor"), P("dp", "tensor"),
        P("tensor", "dp"), P("tensor", None), P(), P("dp", None, "tensor"), P(None, "tensor"),
        P("tensor", "dp"), P(), P("dp", "tensor"), P("tensor", "dp"), P(),
    )
    return jax.shard_map(shards, mesh=mesh, in_specs=in_specs, out_specs=out_specs, check_vma=False)
```

time: 853 us -> 652 us (0.76)
  waiting for transfers between devices: 479 us -> 255 us
  matrix products: 139 us -> 2.1 us
  Pallas kernels: 102 us -> 217 us
  local copies, waits for them, and re-layouts: 28.8 us -> 72.3 us
  starting transfers between devices: 41.4 us -> 61.8 us
  other arithmetic: 37.6 us -> 19.4 us
    reduce_scatter x8 -> x4, waiting for transfers between devices: 222 us -> 9.67 us  [settle(): lax.psum_scatter(grads, 'dp', scatter_dimension=0, tiled=True).astype(F32)]
    dot_general x73 -> x1, matrix products: 138 us -> 1.21 us  [shards(): lax.dot_general(table_sums.reshape(heads, -1), onehot, (((1,), (1,)), (()...]
    pallas_call x5 -> x59, Pallas kernels: 102 us -> 217 us  [the longest x1 43.9 us: attend_back(): call(functools.partial(attend_back_body, tiles=tiles, pairs=pairs, scale=...]
    unnamed x241 -> x330, local copies, waits for them, and re-layouts: 19.8 us -> 59.6 us
    ppermute x53 -> x80, starting transfers between devices: 40 us -> 61.5 us  [swap(): return lax.ppermute(values, axis, [(i, i ^ bit) for i in range(count)])]
    reduce_sum x15 -> x10, other arithmetic: 14.6 us -> 0.14 us  [total(): return sum((jnp.sum(part, axis=0) for part in sums))]
    ppermute x53 -> x80, waiting for transfers between devices: 256 us -> 246 us  [swap(): return lax.ppermute(values, axis, [(i, i ^ bit) for i in range(count)])]
  transfers between devices with their start and end apart: 61 -> 84, of which waited for: 27 -> 43; matrix products, arithmetic and copies ran while one was open for 20% -> 6% of each run, Pallas kernels for 9% -> 26%
where the time goes in v2:
time: 652 us; the launch traced here: 644 us
  waiting for transfers between devices  255 us (39%)
  Pallas kernels  217 us (33%)
  local copies, waits for them, and re-layouts  72.3 us (11%)
  starting transfers between devices  61.8 us (9%)
  other arithmetic  19.4 us (3%)
  between operations  16 us (2%)
    ppermute x80, waiting for transfers between devices, swap(): return lax.ppermute(values, axis, [(i, i ^ bit) for i in range(count)])  246 us
    ppermute x80, starting transfers between devices, swap(): return lax.ppermute(values, axis, [(i, i ^ bit) for i in range(count)])  61.5 us
    unnamed x330, local copies, waits for them, and re-layouts  59.6 us
    pallas_call x1, Pallas kernels, attend_back(): call(functools.partial(attend_back_body, tiles=tiles, pairs=pairs, scale=...  43.9 us
    pallas_call x16, Pallas kernels, by_chunks(): call(run, name, shapes, grid=(1,), in_specs=specs, out_specs=outs, input_...  35.5 us
    pallas_call x5, Pallas kernels, weight_grads(): call(body, 'weight_grads', [shaped((height, cut), BF16)] * pieces, grid=(...  29.1 us
    pallas_call x6, Pallas kernels, ff_back_rows(): call(body, 'ff_back_rows', [shaped(a.shape, BF16)] + [shaped((rows, width...  25 us
    pallas_call x1, Pallas kernels, attend(): call(functools.partial(attend_body, tiles=tiles, pairs=pairs, scale=plan[...  23.7 us
  transfers between devices with their start and end apart: 84, of which 43 were waited for; matrix products, arithmetic and copies ran while one was open for 6% of the time, Pallas kernels for 26%

profile of v2, /device:TPU:0, one launch (start us, length us, event | category | flops | bytes accessed | tf_op | source)
XLA Modules:
  0.0 644.2 jit_solution(10417358145829647727)
XLA Ops:
  19.5 13.4 %collective-permute-done.2.x1_ref.refs_2_.refs_4_ = bf16[384,1024]{1,0:T(8,128)(2,1)S(1)} collective-permute-done((bf16[384,1024]{1,0:T(8,128)(2,1)S(1)}, bf16[384,1024]{1,0:T(8,128)(2,1)S(1)}, u32[]{:S(2)}, u32[]{:S(2)}) %collective-permute-start.2) | collective-permute-done | bytes 786464 | tf_op jit(solution)/shard_map/ppermute | solution.py:841
  45.7 8.9 %collective-permute-done.5.p3_ref = bf16[192,1024]{1,0:T(8,128)(2,1)S(1)} collective-permute-done((bf16[192,1024]{1,0:T(8,128)(2,1)S(1)}, bf16[192,1024]{1,0:T(8,128)(2,1)S(1)}, u32[]{:S(2)}, u32[]{:S(2)}) %collective-permute-start.5) | collective-permute-done | bytes 393248 | tf_op jit(solution)/shard_map/ppermute | solution.py:841
  75.5 10.3 %collective-permute-done.8.x1_ref.refs_7_ = bf16[384,1024]{1,0:T(8,128)(2,1)S(1)} collective-permute-done((bf16[384,1024]{1,0:T(8,128)(2,1)}, bf16[384,1024]{1,0:T(8,128)(2,1)S(1)}, u32[]{:S(2)}, u32[]{:S(2)}) %collective-permute-start.8) | collective-permute-done | bytes 786464 | tf_op jit(solution)/shard_map/ppermute | solution.py:841
  92.0 23.7 %attend.1 = (bf16[1536,256]{1,0:T(8,128)(2,1)S(1)}, f32[12,4,128]{2,1,0:T(4,128)S(1)}, bf16[1536,768]{1,0:T(8,128)(2,1)S(1)}) custom-call(s32[12]{0:T(128)S(1)} %add.199.place_ref, s32[12]{0:T(128)S(1)} %get-tuple-element.402.start_ref, s32[12]{0:T(128)S(1)} %get-tuple-element.403.count_ref, s32[144]{0:T(256)S(1)} %copy-done.76, ...), custom_call_target="tpu_custom_call" | custom-call | flops 24000000000 | bytes 84000000 | tf_op jit(solution)/shard_map/attend/pallas_call | solution.py:455
  122.1 9.6 %collective-permute-done.13.p3_ref = bf16[192,1024]{1,0:T(8,128)(2,1)S(1)} collective-permute-done((bf16[192,1024]{1,0:T(8,128)(2,1)S(1)}, bf16[192,1024]{1,0:T(8,128)(2,1)S(1)}, u32[]{:S(2)}, u32[]{:S(2)}) %collective-permute-start.13) | collective-permute-done | bytes 393248 | tf_op jit(solution)/shard_map/ppermute | solution.py:841
  133.1 6.5 %collective-permute-done.15.refs_3_ = bf16[192,1024]{1,0:T(8,128)(2,1)S(1)} collective-permute-done((bf16[192,1024]{1,0:T(8,128)(2,1)S(1)}, bf16[192,1024]{1,0:T(8,128)(2,1)S(1)}, u32[]{:S(2)}, u32[]{:S(2)}) %collective-permute-start.15) | collective-permute-done | bytes 393248 | tf_op jit(solution)/shard_map/ppermute | solution.py:841
  144.2 16.7 %collective-permute-done.16.x1_ref.refs_7_ = bf16[384,1024]{1,0:T(8,128)(2,1)S(1)} collective-permute-done((bf16[384,1024]{1,0:T(8,128)(2,1)S(1)}, bf16[384,1024]{1,0:T(8,128)(2,1)S(1)}, u32[]{:S(2)}, u32[]{:S(2)}) %collective-permute-start.16) | collective-permute-done | bytes 786464 | tf_op jit(solution)/shard_map/ppermute | solution.py:841
  178.0 9.6 %collective-permute-done.21.p3_ref = bf16[192,1024]{1,0:T(8,128)(2,1)S(1)} collective-permute-done((bf16[192,1024]{1,0:T(8,128)(2,1)S(1)}, bf16[192,1024]{1,0:T(8,128)(2,1)S(1)}, u32[]{:S(2)}, u32[]{:S(2)}) %collective-permute-start.21) | collective-permute-done | bytes 393248 | tf_op jit(solution)/shard_map/ppermute | solution.py:841
  188.9 6.6 %collective-permute-done.23.refs_3_ = bf16[192,1024]{1,0:T(8,128)(2,1)S(1)} collective-permute-done((bf16[192,1024]{1,0:T(8,128)(2,1)S(1)}, bf16[192,1024]{1,0:T(8,128)(2,1)S(1)}, u32[]{:S(2)}, u32[]{:S(2)}) %collective-permute-start.23) | collective-permute-done | bytes 393248 | tf_op jit(solution)/shard_map/ppermute | solution.py:841
  202.7 14.1 %collective-permute-done.26.x1_ref.refs_11_.refs_13_ = bf16[384,1024]{1,0:T(8,128)(2,1)S(1)} collective-permute-done((bf16[384,1024]{1,0:T(8,128)(2,1)S(1)}, bf16[384,1024]{1,0:T(8,128)(2,1)S(1)}, u32[]{:S(2)}, u32[]{:S(2)}) %collective-permute-start.26) | collective-permute-done | bytes 786464 | tf_op jit(solution)/shard_map/ppermute | solution.py:841
  227.0 8.8 %collective-permute-done.29.p3_ref = bf16[192,1024]{1,0:T(8,128)(2,1)S(1)} collective-permute-done((bf16[192,1024]{1,0:T(8,128)(2,1)S(1)}, bf16[192,1024]{1,0:T(8,128)(2,1)S(1)}, u32[]{:S(2)}, u32[]{:S(2)}) %collective-permute-start.29) | collective-permute-done | bytes 393248 | tf_op jit(solution)/shard_map/ppermute | solution.py:841
  254.3 12.0 %collective-permute-done.34.g1_ref.refs_2_.refs_4_ = bf16[384,1024]{1,0:T(8,128)(2,1)S(1)} collective-permute-done((bf16[384,1024]{1,0:T(8,128)(2,1)S(1)}, bf16[384,1024]{1,0:T(8,128)(2,1)S(1)}, u32[]{:S(2)}, u32[]{:S(2)}) %collective-permute-start.34) | collective-permute-done | bytes 786464 | tf_op jit(solution)/shard_map/ppermute | solution.py:841
  279.6 8.8 %weight_grads.5 = bf16[1024,2048]{1,0:T(8,128)(2,1)} custom-call(bf16[384,1024]{1,0:T(8,128)(2,1)S(1)} %get-tuple-element.229.g1_ref.refs_0_, bf16[384,1024]{1,0:T(8,128)(2,1)S(1)} %collective-permute-done.32.g2_ref.refs_1_, bf16[384,1024]{1,0:T(8,128)(2,1)S(1)} %collective-permute-done.34.g1_ref.refs_2_.refs_4_, ...), custom_call_target="tpu_custom_call" | custom-call | flops 5000000000 | bytes 17500000 | tf_op jit(solution)/shard_map/weight_grads/pallas_call | solution.py:348
  308.8 17.0 %collective-permute-done.40.x1_ref.refs_2_ = bf16[384,1024]{1,0:T(8,128)(2,1)S(1)} collective-permute-done((bf16[384,1024]{1,0:T(8,128)(2,1)S(1)}, bf16[384,1024]{1,0:T(8,128)(2,1)S(1)}, u32[]{:S(2)}, u32[]{:S(2)}) %collective-permute-start.40) | collective-permute-done | bytes 786464 | tf_op jit(solution)/shard_map/ppermute | solution.py:841
  328.7 14.7 %conv_backward.1 = (bf16[1536,512]{1,0:T(8,128)(2,1)S(1)}, f32[31,256]{1,0:T(8,128)S(1)}) custom-call(s32[4]{0:T(128)S(1)} %copy-done.75, s32[12]{0:T(128)S(1)} %get-tuple-element.397.low_ref, s32[12]{0:T(128)S(1)} %get-tuple-element.396.high_ref, f32[768,256]{1,0:T(8,128)S(1)} %project.12.refs_0_, f32[768,256]{1,0:T(8,128)S(1)} %project.13.refs_1_, ...), custom_call_target="tpu_custom_call" | custom-call | flops 16999999488 | bytes 59500000 | tf_op jit(solution)/shard_map/conv_backward/pallas_call | solution.py:808
  354.9 13.3 %collective-permute-done.47.p3_ref = bf16[192,1024]{1,0:T(8,128)(2,1)} collective-permute-done((bf16[192,1024]{1,0:T(8,128)(2,1)}, bf16[192,1024]{1,0:T(8,128)(2,1)}, u32[]{:S(2)}, u32[]{:S(2)}) %collective-permute-start.47) | collective-permute-done | bytes 393248 | tf_op jit(solution)/shard_map/ppermute | solution.py:841
  382.3 16.1 %collective-permute-done.48.x1_ref.refs_2_ = bf16[384,1024]{1,0:T(8,128)(2,1)S(1)} collective-permute-done((bf16[384,1024]{1,0:T(8,128)(2,1)S(1)}, bf16[384,1024]{1,0:T(8,128)(2,1)S(1)}, u32[]{:S(2)}, u32[]{:S(2)}) %collective-permute-start.48) | collective-permute-done | bytes 786464 | tf_op jit(solution)/shard_map/ppermute | solution.py:841
  403.2 43.9 %attend_back.1 = (bf16[1536,768]{1,0:T(8,128)(2,1)S(1)}, f32[4,9,256]{2,1,0:T(8,128)S(1)}) custom-call(s32[12]{0:T(128)S(1)} %copy-done.15, s32[12]{0:T(128)S(1)} %get-tuple-element.402.start_ref, s32[12]{0:T(128)S(1)} %copy-done.17, s32[144]{0:T(256)S(1)} %copy-done.77, bf16[768,256]{1,0:T(8,128)(2,1)S(1)} %copy-done.127, ...), custom_call_target="tpu_custom_call" | custom-call | flops 43000000512 | bytes 150500000 | tf_op jit(solution)/shard_map/attend_back/pallas_call | solution.py:593
  462.9 6.4 weight_grads.7
  469.3 10.6 %collective-permute-done.55.p3_ref = bf16[192,1024]{1,0:T(8,128)(2,1)S(1)} collective-permute-done((bf16[192,1024]{1,0:T(8,128)(2,1)}, bf16[192,1024]{1,0:T(8,128)(2,1)S(1)}, u32[]{:S(2)}, u32[]{:S(2)}) %collective-permute-start.55) | collective-permute-done | bytes 393248 | tf_op jit(solution)/shard_map/ppermute | solution.py:841
  534.6 6.5 %weight_grads.9 = bf16[1024,1024]{1,0:T(8,128)(2,1)} custom-call(bf16[384,1024]{1,0:T(8,128)(2,1)} %get-tuple-element.288.g1_ref.refs_0_, bf16[384,1024]{1,0:T(8,128)(2,1)S(1)} %copy-done.45, bf16[384,1024]{1,0:T(8,128)(2,1)S(1)} %copy-done.47, bf16[384,1024]{1,0:T(8,128)(2,1)} %collective-permute-done.59.g2_ref.refs_3_.refs_5_, ...), custom_call_target="tpu_custom_call" | custom-call | flops 5000000000 | bytes 17500000 | tf_op jit(solution)/shard_map/weight_grads/pallas_call | solution.py:348
  541.1 10.5 %collective-permute-done.63.p3_ref = bf16[192,1024]{1,0:T(8,128)(2,1)} collective-permute-done((bf16[192,1024]{1,0:T(8,128)(2,1)}, bf16[192,1024]{1,0:T(8,128)(2,1)}, u32[]{:S(2)}, u32[]{:S(2)}) %collective-permute-start.63) | collective-permute-done | bytes 393248 | tf_op jit(solution)/shard_map/ppermute | solution.py:841
  595.5 9.5 %collective-permute-done.69 = bf16[2,2,128,512]{3,2,0,1:T(8,128)(2,1)S(1)} collective-permute-done((bf16[2,2,128,512]{3,2,0,1:T(8,128)(2,1)S(1)}, bf16[2,2,128,512]{3,2,0,1:T(8,128)(2,1)S(1)}, u32[]{:S(2)}, u32[]{:S(2)}) %collective-permute-start.69) | collective-permute-done | bytes 524320 | tf_op jit(solution)/shard_map/ppermute | solution.py:841
  625.8 9.6 %reduce-scatter.9.cloned.1.call-done = bf16[128,1024]{1,0:T(8,128)(2,1)} async-done(((bf16[1024,1024]{1,0:T(8,128)(2,1)}), bf16[128,1024]{1,0:T(8,128)(2,1)}) %reduce-scatter.9.cloned.1.call-update) | async-done | bytes 262160 | tf_op jit(solution)/shard_map/reduce_scatter | solution.py:893
  (640 shorter events, 320.8 us)
Async XLA Ops:
  7.2 441.4 %reduce-scatter.5.cloned.1.call-start = ((), (), s32[]{:S(2)}) async-start(), calls=%async_computation.4 | async-start | bytes 4718592 | tf_op jit(solution)/shard_map/reduce_scatter | solution.py:893
  12.2 20.7 %collective-permute-start.2 = (bf16[384,1024]{1,0:T(8,128)(2,1)S(1)}, bf16[384,1024]{1,0:T(8,128)(2,1)S(1)}, u32[]{:S(2)}, u32[]{:S(2)}) collective-permute-start(bf16[384,1024]{1,0:T(8,128)(2,1)S(1)} %enter.1.x1_ref.refs_0_), channel_id=1, source_target_pairs={{0,2},{1,3},{2,0},{3,1},{4,6},{5,7},{6,4},{7,5},{8,10},{9,11},{10,... | collective-permute-start | bytes 2359304 | tf_op jit(solution)/shard_map/ppermute | solution.py:841
  44.6 17.9 %collective-permute-start.7 = (bf16[192,1024]{1,0:T(8,128)(2,1)S(1)}, bf16[192,1024]{1,0:T(8,128)(2,1)S(1)}, u32[]{:S(2)}, u32[]{:S(2)}) collective-permute-start(bf16[192,1024]{1,0:T(8,128)(2,1)S(1)} %add_convert_fusion.14), channel_id=1, source_target_pairs={{0,2},{1,3},{2,0},{3,1},{4,6},{5,7},{6,4},{7,5},{8,10},{9,11},{10,... | collective-permute-start | bytes 1179656 | tf_op jit(solution)/shard_map/ppermute | solution.py:841
  65.6 20.2 %collective-permute-start.8 = (bf16[384,1024]{1,0:T(8,128)(2,1)}, bf16[384,1024]{1,0:T(8,128)(2,1)S(1)}, u32[]{:S(2)}, u32[]{:S(2)}) collective-permute-start(bf16[384,1024]{1,0:T(8,128)(2,1)} %get-tuple-element.189.x1_ref.refs_5_), channel_id=1, source_target_pairs={{0,2},{1,3},{2,0},{3,1},{4,6},{5,7},{6,4},{7,5},{8,10},{9,11},{10,... | collective-permute-start | bytes 2359304 | tf_op jit(solution)/shard_map/ppermute | solution.py:841
  121.7 17.8 %collective-permute-start.15 = (bf16[192,1024]{1,0:T(8,128)(2,1)S(1)}, bf16[192,1024]{1,0:T(8,128)(2,1)S(1)}, u32[]{:S(2)}, u32[]{:S(2)}) collective-permute-start(bf16[192,1024]{1,0:T(8,128)(2,1)S(1)} %add_convert_fusion.12), channel_id=1, source_target_pairs={{0,2},{1,3},{2,0},{3,1},{4,6},{5,7},{6,4},{7,5},{8,10},{9,11},{10,... | collective-permute-start | bytes 1179656 | tf_op jit(solution)/shard_map/ppermute | solution.py:841
  140.9 20.0 %collective-permute-start.16 = (bf16[384,1024]{1,0:T(8,128)(2,1)S(1)}, bf16[384,1024]{1,0:T(8,128)(2,1)S(1)}, u32[]{:S(2)}, u32[]{:S(2)}) collective-permute-start(bf16[384,1024]{1,0:T(8,128)(2,1)S(1)} %get-tuple-element.202.x1_ref.refs_5_), channel_id=1, source_target_pairs={{0,2},{1,3},{2,0},{3,1},{4,6},{5,7},{6,4},{7,5},{8,10},{9,11},{10,... | collective-permute-start | bytes 2359304 | tf_op jit(solution)/shard_map/ppermute | solution.py:841
  177.5 17.9 %collective-permute-start.23 = (bf16[192,1024]{1,0:T(8,128)(2,1)S(1)}, bf16[192,1024]{1,0:T(8,128)(2,1)S(1)}, u32[]{:S(2)}, u32[]{:S(2)}) collective-permute-start(bf16[192,1024]{1,0:T(8,128)(2,1)S(1)} %add_convert_fusion.10), channel_id=1, source_target_pairs={{0,2},{1,3},{2,0},{3,1},{4,6},{5,7},{6,4},{7,5},{8,10},{9,11},{10,... | collective-permute-start | bytes 1179656 | tf_op jit(solution)/shard_map/ppermute | solution.py:841
  196.8 20.0 %collective-permute-start.26 = (bf16[384,1024]{1,0:T(8,128)(2,1)S(1)}, bf16[384,1024]{1,0:T(8,128)(2,1)S(1)}, u32[]{:S(2)}, u32[]{:S(2)}) collective-permute-start(bf16[384,1024]{1,0:T(8,128)(2,1)S(1)} %get-tuple-element.215.x1_ref.refs_9_), channel_id=1, source_target_pairs={{0,2},{1,3},{2,0},{3,1},{4,6},{5,7},{6,4},{7,5},{8,10},{9,11},{10,... | collective-permute-start | bytes 2359304 | tf_op jit(solution)/shard_map/ppermute | solution.py:841
  225.7 17.7 %collective-permute-start.31 = (bf16[192,1024]{1,0:T(8,128)(2,1)S(1)}, bf16[192,1024]{1,0:T(8,128)(2,1)S(1)}, u32[]{:S(2)}, u32[]{:S(2)}) collective-permute-start(bf16[192,1024]{1,0:T(8,128)(2,1)S(1)} %add_convert_fusion.8), channel_id=1, source_target_pairs={{0,2},{1,3},{2,0},{3,1},{4,6},{5,7},{6,4},{7,5},{8,10},{9,11},{10,... | collective-permute-start | bytes 1179656 | tf_op jit(solution)/shard_map/ppermute | solution.py:841
  246.4 20.0 %collective-permute-start.34 = (bf16[384,1024]{1,0:T(8,128)(2,1)S(1)}, bf16[384,1024]{1,0:T(8,128)(2,1)S(1)}, u32[]{:S(2)}, u32[]{:S(2)}) collective-permute-start(bf16[384,1024]{1,0:T(8,128)(2,1)S(1)} %get-tuple-element.229.g1_ref.refs_0_), channel_id=1, source_target_pairs={{0,2},{1,3},{2,0},{3,1},{4,6},{5,7},{6,4},{7,5},{8,10},{9,11},{10,... | collective-permute-start | bytes 2359304 | tf_op jit(solution)/shard_map/ppermute | solution.py:841
  271.9 20.8 %collective-permute-start.33 = (bf16[384,1024]{1,0:T(8,128)(2,1)}, bf16[384,1024]{1,0:T(8,128)(2,1)}, u32[]{:S(2)}, u32[]{:S(2)}) collective-permute-start(bf16[384,1024]{1,0:T(8,128)(2,1)} %get-tuple-element.232), channel_id=1, source_target_pairs={{0,1},{1,0},{2,3},{3,2},{4,5},{5,4},{6,7},{7,6},{8,9},{9,8},{10,11... | collective-permute-start | bytes 2359304 | tf_op jit(solution)/shard_map/ppermute | solution.py:841
  289.6 200.6 %reduce-scatter.7.cloned.1.call-start = ((), (), s32[]{:S(2)}) async-start(), calls=%async_computation.5 | async-start | bytes 1769472 | tf_op jit(solution)/shard_map/reduce_scatter | solution.py:893
  305.9 20.0 %collective-permute-start.40 = (bf16[384,1024]{1,0:T(8,128)(2,1)S(1)}, bf16[384,1024]{1,0:T(8,128)(2,1)S(1)}, u32[]{:S(2)}, u32[]{:S(2)}) collective-permute-start(bf16[384,1024]{1,0:T(8,128)(2,1)S(1)} %get-tuple-element.251.x1_ref.refs_0_), channel_id=1, source_target_pairs={{0,2},{1,3},{2,0},{3,1},{4,6},{5,7},{6,4},{7,5},{8,10},{9,11},{10,... | collective-permute-start | bytes 2359304 | tf_op jit(solution)/shard_map/ppermute | solution.py:841
  346.9 21.2 %collective-permute-start.43 = (bf16[384,1024]{1,0:T(8,128)(2,1)S(1)}, bf16[384,1024]{1,0:T(8,128)(2,1)S(1)}, u32[]{:S(2)}, u32[]{:S(2)}) collective-permute-start(bf16[384,1024]{1,0:T(8,128)(2,1)S(1)} %get-tuple-element.259), channel_id=1, source_target_pairs={{0,1},{1,0},{2,3},{3,2},{4,5},{5,4},{6,7},{7,6},{8,9},{9,8},{10,11... | collective-permute-start | bytes 2359304 | tf_op jit(solution)/shard_map/ppermute | solution.py:841
  348.0 26.4 %collective-permute-start.45 = (bf16[192,1024]{1,0:T(8,128)(2,1)}, bf16[192,1024]{1,0:T(8,128)(2,1)}, u32[]{:S(2)}, u32[]{:S(2)}) collective-permute-start(bf16[192,1024]{1,0:T(8,128)(2,1)} %add_convert_fusion.5), channel_id=1, source_target_pairs={{0,2},{1,3},{2,0},{3,1},{4,6},{5,7},{6,4},{7,5},{8,10},{9,11},{10,... | collective-permute-start | bytes 1179656 | tf_op jit(solution)/shard_map/ppermute | solution.py:841
  378.4 20.0 %collective-permute-start.48 = (bf16[384,1024]{1,0:T(8,128)(2,1)S(1)}, bf16[384,1024]{1,0:T(8,128)(2,1)S(1)}, u32[]{:S(2)}, u32[]{:S(2)}) collective-permute-start(bf16[384,1024]{1,0:T(8,128)(2,1)S(1)} %get-tuple-element.268.x1_ref.refs_0_), channel_id=1, source_target_pairs={{0,2},{1,3},{2,0},{3,1},{4,6},{5,7},{6,4},{7,5},{8,10},{9,11},{10,... | collective-permute-start | bytes 2359304 | tf_op jit(solution)/shard_map/ppermute | solution.py:841
  398.4 224.7 %reduce-scatter.11.cloned.1.call-start = ((), (), s32[]{:S(2)}) async-start(), calls=%async_computation.7 | async-start | bytes 2359296 | tf_op jit(solution)/shard_map/reduce_scatter | solution.py:893
  458.8 21.1 %collective-permute-start.51 = (bf16[384,1024]{1,0:T(8,128)(2,1)}, bf16[384,1024]{1,0:T(8,128)(2,1)S(1)}, u32[]{:S(2)}, u32[]{:S(2)}) collective-permute-start(bf16[384,1024]{1,0:T(8,128)(2,1)} %get-tuple-element.277), channel_id=1, source_target_pairs={{0,1},{1,0},{2,3},{3,2},{4,5},{5,4},{6,7},{7,6},{8,9},{9,8},{10,11... | collective-permute-start | bytes 2359304 | tf_op jit(solution)/shard_map/ppermute | solution.py:841
  459.9 24.9 %collective-permute-start.53 = (bf16[192,1024]{1,0:T(8,128)(2,1)}, bf16[192,1024]{1,0:T(8,128)(2,1)S(1)}, u32[]{:S(2)}, u32[]{:S(2)}) collective-permute-start(bf16[192,1024]{1,0:T(8,128)(2,1)} %add_convert_fusion.3), channel_id=1, source_target_pairs={{0,2},{1,3},{2,0},{3,1},{4,6},{5,7},{6,4},{7,5},{8,10},{9,11},{10,... | collective-permute-start | bytes 1179656 | tf_op jit(solution)/shard_map/ppermute | solution.py:841
  488.1 20.2 %collective-permute-start.58 = (bf16[384,1024]{1,0:T(8,128)(2,1)}, bf16[384,1024]{1,0:T(8,128)(2,1)S(1)}, u32[]{:S(2)}, u32[]{:S(2)}) collective-permute-start(bf16[384,1024]{1,0:T(8,128)(2,1)} %get-tuple-element.288.g1_ref.refs_0_), channel_id=1, source_target_pairs={{0,2},{1,3},{2,0},{3,1},{4,6},{5,7},{6,4},{7,5},{8,10},{9,11},{10,... | collective-permute-start | bytes 2359304 | tf_op jit(solution)/shard_map/ppermute | solution.py:841
  489.9 145.5 %reduce-scatter.9.cloned.1.call-start = ((), (), s32[]{:S(2)}) async-start(), calls=%async_computation.6 | async-start | bytes 2359296 | tf_op jit(solution)/shard_map/reduce_scatter | solution.py:893
  514.1 37.5 %collective-permute-start.57 = (bf16[384,1024]{1,0:T(8,128)(2,1)}, bf16[384,1024]{1,0:T(8,128)(2,1)}, u32[]{:S(2)}, u32[]{:S(2)}) collective-permute-start(bf16[384,1024]{1,0:T(8,128)(2,1)} %copy-done.48), channel_id=1, source_target_pairs={{0,1},{1,0},{2,3},{3,2},{4,5},{5,4},{6,7},{7,6},{8,9},{9,8},{10,11... | collective-permute-start | bytes 2359304 | tf_op jit(solution)/shard_map/ppermute | solution.py:841
  531.7 25.1 %collective-permute-start.61 = (bf16[192,1024]{1,0:T(8,128)(2,1)}, bf16[192,1024]{1,0:T(8,128)(2,1)}, u32[]{:S(2)}, u32[]{:S(2)}) collective-permute-start(bf16[192,1024]{1,0:T(8,128)(2,1)} %add_convert_fusion.1), channel_id=1, source_target_pairs={{0,2},{1,3},{2,0},{3,1},{4,6},{5,7},{6,4},{7,5},{8,10},{9,11},{10,... | collective-permute-start | bytes 1179656 | tf_op jit(solution)/shard_map/ppermute | solution.py:841
  574.2 18.4 %collective-permute-start.72 = (bf16[2,2,128,512]{3,2,0,1:T(8,128)(2,1)}, bf16[2,2,128,512]{3,2,0,1:T(8,128)(2,1)}, u32[]{:S(2)}, u32[]{:S(2)}) collective-permute-start(bf16[2,2,128,512]{3,2,0,1:T(8,128)(2,1)} %bitcast.66), channel_id=1, source_target_pairs={{0,4},{4,0},{8,12},{12,8},{16,20},{20,16},{24,28},{28,24},{1,5},{5... | collective-permute-start | bytes 1572872 | tf_op jit(solution)/shard_map/ppermute | solution.py:841
  (220 other events, 1551.4 us)
Sparse Core Ops, SparseCore 0:
  289.7 89.5 reduce-scatter.4
  398.5 66.6 reduce-scatter.6
  490.0 67.9 reduce-scatter.10
  562.2 73.1 reduce-scatter.8

commit v3 on v2

--- a/solution.py
+++ b/solution.py
@@ -43,7 +43,7 @@
     weight_grads=(5, 40), attend=(24, 40), attend_back=(43, 48),
     conv_forward=(11, 40), conv_backward=(17, 48),
 )
-COST_SCALE = 1.0
+COST_SCALE = 0.1
 
 
 def call(body, name, out_shape, cost=1.0, **options):
@@ -255,17 +255,32 @@
     return specs, plain
 
 
+def row_blocks(rows, at, block):
+    step = rows // 2 if rows > 256 else rows
+
+    def one(i, carry):
+        here = pl.multiple_of(i * step, step)
+        block(pl.ds(here, step), pl.ds(here + at, step))
+        return carry
+
+    lax.fori_loop(0, rows // step, one, 0)
+
+
 def ff_rows(x1, x2, w_in, w_out):
     specs, plain = pieces_of([x1, x2])
     rows, width = specs[0].block_shape
 
     def body(x1_ref, x2_ref, w_in_ref, w_out_ref, a_ref, z_ref, u1_ref, u2_ref):
         for x_ref, u_ref, at in ((x1_ref, u1_ref, 0), (x2_ref, u2_ref, rows)):
-            a = dot(x_ref[...], w_in_ref[...], 1, 0)
-            z = (a * sigmoid(a)).astype(BF16)
-            a_ref[at : at + rows, :] = a.astype(BF16)
-            z_ref[at : at + rows, :] = z
-            u_ref[...] = dot(z, w_out_ref[...], 1, 0).astype(BF16)
+
+            def block(here, there):
+                a = dot(x_ref[here, :], w_in_ref[...], 1, 0)
+                z = (a * sigmoid(a)).astype(BF16)
+                a_ref[there, :] = a.astype(BF16)
+                z_ref[there, :] = z
+                u_ref[here, :] = dot(z, w_out_ref[...], 1, 0).astype(BF16)
+
+            row_blocks(rows, at, block)
 
     wide = (2 * rows, w_in.shape[1])
     return call(
@@ -281,12 +296,16 @@
 
     def body(g1_ref, g2_ref, a_ref, w_out_ref, w_in_ref, ea_ref, p1_ref, p2_ref):
         for g_ref, p_ref, at in ((g1_ref, p1_ref, 0), (g2_ref, p2_ref, rows)):
-            ez = dot(g_ref[...], w_out_ref[...], 1, 1)
-            a = a_ref[at : at + rows, :].astype(F32)
-            s = sigmoid(a)
-            ea = (ez * s * (1.0 + a * (1.0 - s))).astype(BF16)
-            ea_ref[at : at + rows, :] = ea
-            p_ref[...] = dot(ea, w_in_ref[...], 1, 1).astype(BF16)
+
+            def block(here, there):
+                ez = dot(g_ref[here, :], w_out_ref[...], 1, 1)
+                a = a_ref[there, :].astype(F32)
+                s = sigmoid(a)
+                ea = (ez * s * (1.0 + a * (1.0 - s))).astype(BF16)
+                ea_ref[there, :] = ea
+                p_ref[here, :] = dot(ea, w_in_ref[...], 1, 1).astype(BF16)
+
+            row_blocks(rows, at, block)
 
     return call(
         body, "ff_back_rows", [shaped(a.shape, BF16)] + [shaped((rows, width), BF16)] * 2,
@@ -321,7 +340,7 @@
     )(*plain, weight)
 
 
-def weight_grads(products, pieces=1):
+def weight_grads(products):
     entries, spans, at, column = [], [], 0, 0
     for left, right in products:
         entries += left + right
@@ -331,23 +350,26 @@
         column += first.shape[1]
     specs, plain = pieces_of(entries)
     height = specs[0].block_shape[1]
-    cut = column // pieces
+    tile = 2 * TILE
 
     def body(*refs):
-        out_refs = refs[at:]
-        for first, middle, last, column in spans:
-            left = jnp.concatenate([ref[...] for ref in refs[first:middle]], 0)
-            right = jnp.concatenate([ref[...] for ref in refs[middle:last]], 0)
-            value = dot(left, right, 0, 0).astype(BF16)
-            if pieces == 1:
-                out_refs[0][:, column : column + right.shape[1]] = value
-            else:
-                for i, out_ref in enumerate(out_refs):
-                    out_ref[...] = value[:, i * cut : (i + 1) * cut]
+        out_ref = refs[-1]
+
+        def band(i, carry):
+            here = pl.ds(pl.multiple_of(i * tile, tile), tile)
+            for first, middle, last, column in spans:
+                left = jnp.concatenate([ref[:, here] for ref in refs[first:middle]], 0)
+                right = jnp.concatenate([ref[...] for ref in refs[middle:last]], 0)
+                out_ref[here, column : column + right.shape[1]] = dot(left, right, 0, 0).astype(
+                    BF16
+                )
+            return carry
+
+        lax.fori_loop(0, height // tile, band, 0)
 
     return call(
-        body, "weight_grads", [shaped((height, cut), BF16)] * pieces, grid=(1,),
-        in_specs=specs, out_specs=[fixed(height, cut)] * pieces,
+        body, "weight_grads", shaped((height, column), BF16), grid=(1,),
+        in_specs=specs, out_specs=fixed(height, column),
     )(*plain)
 
 
@@ -854,50 +876,43 @@
     blocks.append(swap(blocks[2], 1))
 
 
-def scatter(own, beside, far):
+def scatter(own, beside, far, sent=None):
     arriving = []
     for across, diagonal in far:
         outgoing = (across.astype(F32) + swap(diagonal, 1).astype(F32)).astype(BF16)
         arriving.append(swap(outgoing, 2))
+        if sent is not None:
+            sent.append(outgoing)
     return [own, swap(beside, 1), arriving]
 
 
-def sum_bits(values, axis):
-    bit = 1
+def sum_bits(values, axis, bit=1):
     while bit < lax.axis_size(axis):
         values = values + swap(values, bit, axis)
         bit *= 2
     return values
 
 
-def settle_halving(grad, first_bits):
+def halve_all(grad, gate):
     count = lax.axis_size("dp")
     bits = count.bit_length() - 1
-    here = lax.axis_index("dp")
-    values = grad.astype(BF16).reshape((2,) * bits + (grad.shape[0] // count, grad.shape[1]))
-    left = list(range(bits - 1, -1, -1))
-    order = [b for b in first_bits if b < bits] + [b for b in range(bits) if b not in first_bits]
-    for bit in order:
-        dim = left.index(bit)
-        keep = (here >> bit) & 1
+    values = grad.reshape((2,) * bits + (grad.shape[0] // count, grad.shape[1]))
+    for bit in range(bits):
+        dim = bits - 1 - bit
+        keep = (lax.axis_index("dp") >> bit) & 1
         sent = lax.dynamic_index_in_dim(values, 1 - keep, dim, keepdims=False)
         kept = lax.dynamic_index_in_dim(values, keep, dim, keepdims=False)
-        values = kept.astype(F32) + swap(sent, 1 << bit, "dp").astype(F32)
-        left.pop(dim)
-        if left:
+        arrived = swap(sent, 1 << bit, "dp")
+        if bit == 0:
+            arrived, _ = tie(arrived, gate)
+        values = kept.astype(F32) + arrived.astype(F32)
+        if bit < bits - 1:
             values = values.astype(BF16)
     return values
 
 
 def settle(grads):
     return lax.psum_scatter(grads, "dp", scatter_dimension=0, tiled=True).astype(F32)
-
-
-PIECES = 2
-
-
-def settle_split(grads):
-    return jnp.concatenate([settle_halving(grad, (0, 1, 2)) for grad in grads], 1)
 
 
 def halves(array):
@@ -920,7 +935,8 @@
         ff_back_rows(g1, g2, a, w_out, w_in)
         for g1, g2, a in zip(halves(blocks[2]), halves(blocks[3]), hidden[1:])
     ]
-    return scatter(near[1], near[2], [f[1:] for f in far]), [near[0]] + [f[0] for f in far]
+    parts = scatter(near[1], near[2], [f[1:] for f in far], outgoing := [])
+    return parts, [near[0]] + [f[0] for f in far], outgoing
 
 
 def zigzag(blocks):
@@ -1035,9 +1051,9 @@
     grads, output, e4, sums = turn(three, parts, gain_five, padded(cotangent), 0.5, 0.5)
     grad_five = total(sums)
     grads = gather(grads)
-    parts, inner = feed_back(grads, state_four, second_in, second_out)
+    parts, inner, _ = feed_back(grads, state_four, second_in, second_out)
     parts, grad_w = delayed(
-        parts, weight_grads([(zigzag(grads), state_four[1]), (zigzag(h_four), inner)])[0]
+        parts, weight_grads([(zigzag(grads), state_four[1]), (zigzag(h_four), inner)])
     )
     settled_four = settle(grad_w)
     grads, e3, sums = join_back(e4, three, parts, gain_four, 1.0)
@@ -1047,45 +1063,52 @@
         spread(grads, w_back, 1, F32), glu, kernel, plan, gated, mixed
     )
     parts, grad_w = delayed(
-        collect(dglu, glu_matrix, 1), weight_grads([(grads, [act]), (h_three, [dglu])])[0]
+        collect(dglu, glu_matrix, 1), weight_grads([(grads, [act]), (h_three, [dglu])])
     )
     settled_three = settle(grad_w)
     grads, e2, sums = join_back(e3, two, parts, gain_three, 1.0)
     grad_three = total(sums)
     grads = gather(grads)
     pulled = spread(grads, w_output, 1, BF16)
-    dqkv, table_sums = attend_back(pulled, qkv, bias, plan, out, lse)
-    dqkv, settled_four = tie(dqkv, settled_four)
+    (first, second), settled_four = tie(pulled, settled_four)
+    dqkv, table_sums = attend_back((first, second), qkv, bias, plan, out, lse)
     parts, grad_w = delayed(
-        collect(dqkv, w_qkv, 1), weight_grads([(grads, [out]), (h_two, [dqkv])])[0]
-    )
+        collect(dqkv, w_qkv, 1), weight_grads([(grads, [out]), (h_two, [dqkv])])
+    )
+    parts, settled_three = delayed(parts, settled_three)
     settled_two = settle(grad_w)
     grads, e1, sums = join_back(e2, one, parts, gain_two, 0.5)
     grad_two = total(sums)
     grads = gather(grads)
-    grads[0], settled_three = tie(grads[0], settled_three)
-    parts, inner = feed_back(grads, state_one, first_in, first_out)
-    grad_w, = weight_grads([(zigzag(grads), state_one[1])])
-    parts, grad_first_in = delayed(parts, weight_grads([(zigzag(h_one), inner)], PIECES))
-    parts, grad_w = delayed(parts, grad_w)
+    parts, inner, outgoing = feed_back(grads, state_one, first_in, first_out)
+    grad_w = weight_grads([(zigzag(grads), state_one[1])])
     grad_first_out = settle(grad_w)
-    small, grad_first_in = tie(
-        (table_sums, grad_kernel, grad_two, grad_three, grad_four, grad_five), grad_first_in
+    own, beside, (near_rows, far_rows) = parts
+    near_rows, settled_two = tie(near_rows, settled_two)
+    parts, grad_first_in = delayed(
+        [own, beside, [near_rows, far_rows]], weight_grads([(zigzag(h_one), inner)])
+    )
+    e0, sums = join_back(e1, start, parts, gain_one, 0.0)
+    grad_first_in = halve_all(grad_first_in, sums[-1])
+    small, sums = tie(
+        (table_sums, grad_kernel, grad_two, grad_three, grad_four, grad_five), sums
     )
     table_sums, grad_kernel, grad_two, grad_three, grad_four, grad_five = small
-    grad_first_in = settle_split(grad_first_in)
-    e0, sums = join_back(e1, start, parts, gain_one, 0.0)
     grad_one = total(sums)
     grad_table = lax.dot_general(
         table_sums.reshape(heads, -1), onehot, (((1,), (1,)), ((), ())),
         precision=lax.Precision.HIGHEST, preferred_element_type=F32,
     )
-    gains = sum_bits(jnp.concatenate([grad_two, grad_three, grad_four, grad_five]), "tensor")
-    small = jnp.concatenate([gains, grad_table.reshape(-1), grad_kernel.reshape(-1)])
-    small = sum_bits(small, "dp")
-    grad_one = sum_bits(sum_bits(grad_one, "tensor"), "dp")
-    grad_gains = [grad_one] + [small[i * width : (i + 1) * width] for i in range(4)]
-    rest = small[4 * width :]
+    small = jnp.concatenate(
+        [grad_one, grad_two, grad_three, grad_four, grad_five]
+        + [grad_table.reshape(-1), grad_kernel.reshape(-1)]
+    )
+    gains = sum_bits(small[: 5 * width], "tensor")
+    small = jnp.concatenate([gains, small[5 * width :]])
+    small = sum_bits(small, "dp", 2)
+    small = small + swap(small, 1, "dp")
+    grad_gains = [small[i * width : (i + 1) * width] for i in range(5)]
+    rest = small[5 * width :]
     grad_table = rest[: grad_table.size].reshape(grad_table.shape)
     grad_kernel = rest[grad_table.size :].reshape(grad_kernel.shape)
     part, own = w_query.shape[1], w_output.shape[0]

time: 652 us -> 629 us (0.965)
  starting transfers between devices: 61.8 us -> 48.9 us
  Pallas kernels: 217 us -> 207 us
    ppermute x80 -> x72, starting transfers between devices: 61.5 us -> 48.7 us  [swap(): return lax.ppermute(values, axis, [(i, i ^ bit) for i in range(count)])]
    reduce_scatter x4, waiting for transfers between devices: 9.67 us -> 0.01 us  [settle(): lax.psum_scatter(grads, 'dp', scatter_dimension=0, tiled=True).astype(F32)]
    ppermute x80 -> x72, waiting for transfers between devices: 246 us -> 252 us  [swap(): return lax.ppermute(values, axis, [(i, i ^ bit) for i in range(count)])]
    unnamed x330 -> x364, local copies, waits for them, and re-layouts: 59.6 us -> 56.9 us
  transfers between devices with their start and end apart: 84 -> 76, of which waited for: 43 -> 43; matrix products, arithmetic and copies ran while one was open for 6% -> 7% of each run, Pallas kernels for 26% -> 26%
where the time goes in v3:
time: 629 us; the launch traced here: 619 us
  waiting for transfers between devices  252 us (40%)
  Pallas kernels  207 us (33%)
  local copies, waits for them, and re-layouts  67.3 us (11%)
  starting transfers between devices  48.9 us (8%)
  other arithmetic  25 us (4%)
  between operations  16.4 us (3%)
    ppermute x72, waiting for transfers between devices, swap(): return lax.ppermute(values, axis, [(i, i ^ bit) for i in range(count)])  252 us
    unnamed x364, local copies, waits for them, and re-layouts  56.9 us
    ppermute x72, starting transfers between devices, swap(): return lax.ppermute(values, axis, [(i, i ^ bit) for i in range(count)])  48.7 us
    pallas_call x1, Pallas kernels, attend_back(): call(functools.partial(attend_back_body, tiles=tiles, pairs=pairs, scale=...  40.2 us
    pallas_call x16, Pallas kernels, by_chunks(): call(run, name, shapes, grid=(1,), in_specs=specs, out_specs=outs, input_...  30.7 us
    pallas_call x5, Pallas kernels, weight_grads(): call(body, 'weight_grads', shaped((height, column), BF16), grid=(1,), in_...  28.2 us
    pallas_call x6, Pallas kernels, ff_back_rows(): call(body, 'ff_back_rows', [shaped(a.shape, BF16)] + [shaped((rows, width...  26 us
    pallas_call x1, Pallas kernels, attend(): call(functools.partial(attend_body, tiles=tiles, pairs=pairs, scale=plan[...  21.1 us
  transfers between devices with their start and end apart: 76, of which 43 were waited for; matrix products, arithmetic and copies ran while one was open for 7% of the time, Pallas kernels for 26%

profile of v3, /device:TPU:0, one launch (start us, length us, event | category | flops | bytes accessed | tf_op | source)
XLA Modules:
  0.0 619.0 jit_solution(16736335663881579542)
XLA Ops:
  23.1 9.8 %collective-permute-done.2.x1_ref.refs_2_.refs_4_ = bf16[384,1024]{1,0:T(8,128)(2,1)S(1)} collective-permute-done((bf16[384,1024]{1,0:T(8,128)(2,1)S(1)}, bf16[384,1024]{1,0:T(8,128)(2,1)S(1)}, u32[]{:S(2)}, u32[]{:S(2)}) %collective-permute-start.2) | collective-permute-done | bytes 786464 | tf_op jit(solution)/shard_map/ppermute | solution.py:863
  43.1 9.0 %collective-permute-done.5.p3_ref = bf16[192,1024]{1,0:T(8,128)(2,1)S(1)} collective-permute-done((bf16[192,1024]{1,0:T(8,128)(2,1)S(1)}, bf16[192,1024]{1,0:T(8,128)(2,1)S(1)}, u32[]{:S(2)}, u32[]{:S(2)}) %collective-permute-start.5) | collective-permute-done | bytes 393248 | tf_op jit(solution)/shard_map/ppermute | solution.py:863
  71.4 9.8 %collective-permute-done.8.x1_ref.refs_7_ = bf16[384,1024]{1,0:T(8,128)(2,1)S(1)} collective-permute-done((bf16[384,1024]{1,0:T(8,128)(2,1)S(1)}, bf16[384,1024]{1,0:T(8,128)(2,1)S(1)}, u32[]{:S(2)}, u32[]{:S(2)}) %collective-permute-start.8) | collective-permute-done | bytes 786464 | tf_op jit(solution)/shard_map/ppermute | solution.py:863
  86.7 21.1 %attend.1 = (bf16[1536,256]{1,0:T(8,128)(2,1)S(1)}, f32[12,4,128]{2,1,0:T(4,128)S(1)}, bf16[1536,768]{1,0:T(8,128)(2,1)S(1)}) custom-call(s32[12]{0:T(128)S(1)} %add.169.place_ref, s32[12]{0:T(128)S(1)} %get-tuple-element.400.start_ref, s32[12]{0:T(128)S(1)} %get-tuple-element.401.count_ref, s32[144]{0:T(256)S(1)} %copy-done.159, ...), custom_call_target="tpu_custom_call" | custom-call | flops 2400000000 | bytes 8400000 | tf_op jit(solution)/shard_map/attend/pallas_call | solution.py:477
  113.0 9.5 %collective-permute-done.13.p3_ref = bf16[192,1024]{1,0:T(8,128)(2,1)S(1)} collective-permute-done((bf16[192,1024]{1,0:T(8,128)(2,1)S(1)}, bf16[192,1024]{1,0:T(8,128)(2,1)S(1)}, u32[]{:S(2)}, u32[]{:S(2)}) %collective-permute-start.13) | collective-permute-done | bytes 393248 | tf_op jit(solution)/shard_map/ppermute | solution.py:863
  123.8 6.7 %collective-permute-done.15.refs_3_ = bf16[192,1024]{1,0:T(8,128)(2,1)S(1)} collective-permute-done((bf16[192,1024]{1,0:T(8,128)(2,1)S(1)}, bf16[192,1024]{1,0:T(8,128)(2,1)S(1)}, u32[]{:S(2)}, u32[]{:S(2)}) %collective-permute-start.15) | collective-permute-done | bytes 393248 | tf_op jit(solution)/shard_map/ppermute | solution.py:863
  135.2 16.7 %collective-permute-done.16.x1_ref.refs_7_ = bf16[384,1024]{1,0:T(8,128)(2,1)S(1)} collective-permute-done((bf16[384,1024]{1,0:T(8,128)(2,1)S(1)}, bf16[384,1024]{1,0:T(8,128)(2,1)S(1)}, u32[]{:S(2)}, u32[]{:S(2)}) %collective-permute-start.16) | collective-permute-done | bytes 786464 | tf_op jit(solution)/shard_map/ppermute | solution.py:863
  155.5 6.4 %conv_forward.1 = (bf16[1536,256]{1,0:T(8,128)(2,1)S(1)}, f32[1536,256]{1,0:T(8,128)S(1)}, f32[1536,256]{1,0:T(8,128)S(1)}, f32[1536,512]{1,0:T(8,128)S(1)}) custom-call(s32[4]{0:T(128)S(1)} %get-tuple-element.415.order_ref, s32[12]{0:T(128)S(1)} %get-tuple-element.395.low_ref, s32[12]{0:T(128)S(1)} %get-tuple-element.394.high_ref, ...), custom_call_target="tpu_custom_call" | custom-call | flops 1100000000 | bytes 3850000 | tf_op jit(solution)/shard_map/conv_forward/pallas_call | solution.py:714
  169.6 9.7 %collective-permute-done.21.p3_ref = bf16[192,1024]{1,0:T(8,128)(2,1)S(1)} collective-permute-done((bf16[192,1024]{1,0:T(8,128)(2,1)S(1)}, bf16[192,1024]{1,0:T(8,128)(2,1)S(1)}, u32[]{:S(2)}, u32[]{:S(2)}) %collective-permute-start.21) | collective-permute-done | bytes 393248 | tf_op jit(solution)/shard_map/ppermute | solution.py:863
  180.6 6.3 %collective-permute-done.23.refs_3_ = bf16[192,1024]{1,0:T(8,128)(2,1)S(1)} collective-permute-done((bf16[192,1024]{1,0:T(8,128)(2,1)S(1)}, bf16[192,1024]{1,0:T(8,128)(2,1)S(1)}, u32[]{:S(2)}, u32[]{:S(2)}) %collective-permute-start.23) | collective-permute-done | bytes 393248 | tf_op jit(solution)/shard_map/ppermute | solution.py:863
  195.4 12.9 %collective-permute-done.26.x1_ref.refs_11_.refs_13_ = bf16[384,1024]{1,0:T(8,128)(2,1)S(1)} collective-permute-done((bf16[384,1024]{1,0:T(8,128)(2,1)S(1)}, bf16[384,1024]{1,0:T(8,128)(2,1)S(1)}, u32[]{:S(2)}, u32[]{:S(2)}) %collective-permute-start.26) | collective-permute-done | bytes 786464 | tf_op jit(solution)/shard_map/ppermute | solution.py:863
  218.4 8.9 %collective-permute-done.29.p3_ref = bf16[192,1024]{1,0:T(8,128)(2,1)S(1)} collective-permute-done((bf16[192,1024]{1,0:T(8,128)(2,1)S(1)}, bf16[192,1024]{1,0:T(8,128)(2,1)S(1)}, u32[]{:S(2)}, u32[]{:S(2)}) %collective-permute-start.29) | collective-permute-done | bytes 393248 | tf_op jit(solution)/shard_map/ppermute | solution.py:863
  240.3 6.4 %ff_back_rows.6 = (bf16[768,1024]{1,0:T(8,128)(2,1)S(1)}, bf16[384,1024]{1,0:T(8,128)(2,1)S(1)}, bf16[384,1024]{1,0:T(8,128)(2,1)S(1)}) custom-call(bf16[384,1024]{1,0:T(8,128)(2,1)S(1)} %get-tuple-element.228.g1_ref.refs_0_, bf16[384,1024]{1,0:T(8,128)(2,1)S(1)} %collective-permute-done.32.g2_ref.refs_1_, bf16[768,1024]{1,0:T(8,128)(2,1)S(1)} %get-tuple-element.229.a_ref, ...), custom_call_target="tpu_custom_call" | custom-call | flops 400000000 | bytes 1400000 | tf_op jit(solution)/shard_map/ff_back_rows/pallas_call | solution.py:310
  247.7 10.3 %collective-permute-done.34.g1_ref.refs_2_.refs_4_ = bf16[384,1024]{1,0:T(8,128)(2,1)S(1)} collective-permute-done((bf16[384,1024]{1,0:T(8,128)(2,1)S(1)}, bf16[384,1024]{1,0:T(8,128)(2,1)S(1)}, u32[]{:S(2)}, u32[]{:S(2)}) %collective-permute-start.34) | collective-permute-done | bytes 786464 | tf_op jit(solution)/shard_map/ppermute | solution.py:863
  271.5 9.5 %weight_grads.5 = bf16[1024,2048]{1,0:T(8,128)(2,1)} custom-call(bf16[384,1024]{1,0:T(8,128)(2,1)S(1)} %get-tuple-element.228.g1_ref.refs_0_, bf16[384,1024]{1,0:T(8,128)(2,1)S(1)} %collective-permute-done.32.g2_ref.refs_1_, bf16[384,1024]{1,0:T(8,128)(2,1)S(1)} %collective-permute-done.34.g1_ref.refs_2_.refs_4_, ...), custom_call_target="tpu_custom_call" | custom-call | flops 500000000 | bytes 1750000 | tf_op jit(solution)/shard_map/weight_grads/pallas_call | solution.py:370
  300.2 17.0 %collective-permute-done.40.x1_ref.refs_2_ = bf16[384,1024]{1,0:T(8,128)(2,1)S(1)} collective-permute-done((bf16[384,1024]{1,0:T(8,128)(2,1)S(1)}, bf16[384,1024]{1,0:T(8,128)(2,1)S(1)}, u32[]{:S(2)}, u32[]{:S(2)}) %collective-permute-start.40) | collective-permute-done | bytes 786464 | tf_op jit(solution)/shard_map/ppermute | solution.py:863
  320.1 14.9 %conv_backward.1 = (bf16[1536,512]{1,0:T(8,128)(2,1)S(1)}, f32[31,256]{1,0:T(8,128)S(1)}) custom-call(s32[4]{0:T(128)S(1)} %copy-done.150, s32[12]{0:T(128)S(1)} %copy-done.148, s32[12]{0:T(128)S(1)} %get-tuple-element.394.high_ref, f32[768,256]{1,0:T(8,128)S(1)} %project.12.refs_0_, f32[768,256]{1,0:T(8,128)S(1)} %project.13.refs_1_, ...), custom_call_target="tpu_custom_call" | custom-call | flops 1700000000 | bytes 5950000 | tf_op jit(solution)/shard_map/conv_backward/pallas_call | solution.py:830
  367.0 16.1 %collective-permute-done.48.x1_ref.refs_2_ = bf16[384,1024]{1,0:T(8,128)(2,1)S(1)} collective-permute-done((bf16[384,1024]{1,0:T(8,128)(2,1)S(1)}, bf16[384,1024]{1,0:T(8,128)(2,1)S(1)}, u32[]{:S(2)}, u32[]{:S(2)}) %collective-permute-start.48) | collective-permute-done | bytes 786464 | tf_op jit(solution)/shard_map/ppermute | solution.py:863
  394.6 40.2 %attend_back.1 = (bf16[1536,768]{1,0:T(8,128)(2,1)S(1)}, f32[4,9,256]{2,1,0:T(8,128)S(1)}) custom-call(s32[12]{0:T(128)S(1)} %copy-done.152, s32[12]{0:T(128)S(1)} %copy-done.154, s32[12]{0:T(128)S(1)} %copy-done.156, s32[144]{0:T(256)S(1)} %copy-done.160, bf16[768,256]{1,0:T(8,128)(2,1)S(1)} %project.14.refs_0_, bf16[768,256]{1,0:T(8,128)(2,1)S(1)} %copy-done.118, ...), custom_call_target="tpu_custom_call" | custom-call | flops 4300000256 | bytes 15050000 | tf_op jit(solution)/shard_map/attend_back/pallas_call | solution.py:615
  473.0 7.4 %ff_back_rows.9 = (bf16[768,1024]{1,0:T(8,128)(2,1)S(1)}, bf16[384,1024]{1,0:T(8,128)(2,1)S(1)}, bf16[384,1024]{1,0:T(8,128)(2,1)}) custom-call(bf16[384,1024]{1,0:T(8,128)(2,1)S(1)} %get-tuple-element.288.g1_ref.refs_0_, bf16[384,1024]{1,0:T(8,128)(2,1)S(1)} %collective-permute-done.56.g2_ref.refs_1_, bf16[768,1024]{1,0:T(8,128)(2,1)S(1)} %copy-done.79, ...), custom_call_target="tpu_custom_call" | custom-call | flops 400000000 | bytes 1400000 | tf_op jit(solution)/shard_map/ff_back_rows/pallas_call | solution.py:310
  480.4 10.2 %collective-permute-done.58.g1_ref.refs_2_.refs_4_ = bf16[384,1024]{1,0:T(8,128)(2,1)S(1)} collective-permute-done((bf16[384,1024]{1,0:T(8,128)(2,1)S(1)}, bf16[384,1024]{1,0:T(8,128)(2,1)S(1)}, u32[]{:S(2)}, u32[]{:S(2)}) %collective-permute-start.58) | collective-permute-done | bytes 786464 | tf_op jit(solution)/shard_map/ppermute | solution.py:863
  559.5 16.0 %collective-permute-done.69 = bf16[2,2,128,1024]{3,2,0,1:T(8,128)(2,1)S(1)} collective-permute-done((bf16[2,2,128,1024]{3,2,0,1:T(8,128)(2,1)}, bf16[2,2,128,1024]{3,2,0,1:T(8,128)(2,1)S(1)}, u32[]{:S(2)}, u32[]{:S(2)}) %collective-permute-start.69) | collective-permute-done | bytes 1048608 | tf_op jit(solution)/shard_map/ppermute | solution.py:863
  583.9 13.7 %collective-permute-done.70 = bf16[2,128,1024]{2,1,0:T(8,128)(2,1)S(1)} collective-permute-done((bf16[2,128,1024]{2,1,0:T(8,128)(2,1)S(1)}, bf16[2,128,1024]{2,1,0:T(8,128)(2,1)S(1)}, u32[]{:S(2)}, u32[]{:S(2)}) %collective-permute-start.70) | collective-permute-done | bytes 524320 | tf_op jit(solution)/shard_map/ppermute | solution.py:863
  604.5 6.6 %collective-permute-done.71 = bf16[128,1024]{1,0:T(8,128)(2,1)S(1)} collective-permute-done((bf16[128,1024]{1,0:T(8,128)(2,1)S(1)}, bf16[128,1024]{1,0:T(8,128)(2,1)S(1)}, u32[]{:S(2)}, u32[]{:S(2)}) %collective-permute-start.71) | collective-permute-done | bytes 262176 | tf_op jit(solution)/shard_map/ppermute | solution.py:863
  (644 shorter events, 307.2 us)
Async XLA Ops:
  7.2 381.4 %reduce-scatter.5.cloned.1.call-start = ((), (), s32[]{:S(2)}) async-start(), calls=%async_computation.4 | async-start | bytes 4718592 | tf_op jit(solution)/shard_map/reduce_scatter | solution.py:915
  12.1 20.7 %collective-permute-start.2 = (bf16[384,1024]{1,0:T(8,128)(2,1)S(1)}, bf16[384,1024]{1,0:T(8,128)(2,1)S(1)}, u32[]{:S(2)}, u32[]{:S(2)}) collective-permute-start(bf16[384,1024]{1,0:T(8,128)(2,1)S(1)} %enter.1.x1_ref.refs_0_), channel_id=1, source_target_pairs={{0,2},{1,3},{2,0},{3,1},{4,6},{5,7},{6,4},{7,5},{8,10},{9,11},{10,... | collective-permute-start | bytes 2359304 | tf_op jit(solution)/shard_map/ppermute | solution.py:863
  42.0 17.9 %collective-permute-start.7 = (bf16[192,1024]{1,0:T(8,128)(2,1)S(1)}, bf16[192,1024]{1,0:T(8,128)(2,1)S(1)}, u32[]{:S(2)}, u32[]{:S(2)}) collective-permute-start(bf16[192,1024]{1,0:T(8,128)(2,1)S(1)} %add_convert_fusion.14), channel_id=1, source_target_pairs={{0,2},{1,3},{2,0},{3,1},{4,6},{5,7},{6,4},{7,5},{8,10},{9,11},{10,... | collective-permute-start | bytes 1179656 | tf_op jit(solution)/shard_map/ppermute | solution.py:863
  62.2 19.0 %collective-permute-start.8 = (bf16[384,1024]{1,0:T(8,128)(2,1)S(1)}, bf16[384,1024]{1,0:T(8,128)(2,1)S(1)}, u32[]{:S(2)}, u32[]{:S(2)}) collective-permute-start(bf16[384,1024]{1,0:T(8,128)(2,1)S(1)} %get-tuple-element.188.x1_ref.refs_5_), channel_id=1, source_target_pairs={{0,2},{1,3},{2,0},{3,1},{4,6},{5,7},{6,4},{7,5},{8,10},{9,11},{10,... | collective-permute-start | bytes 2359304 | tf_op jit(solution)/shard_map/ppermute | solution.py:863
  112.5 18.1 %collective-permute-start.15 = (bf16[192,1024]{1,0:T(8,128)(2,1)S(1)}, bf16[192,1024]{1,0:T(8,128)(2,1)S(1)}, u32[]{:S(2)}, u32[]{:S(2)}) collective-permute-start(bf16[192,1024]{1,0:T(8,128)(2,1)S(1)} %add_convert_fusion.12), channel_id=1, source_target_pairs={{0,2},{1,3},{2,0},{3,1},{4,6},{5,7},{6,4},{7,5},{8,10},{9,11},{10,... | collective-permute-start | bytes 1179656 | tf_op jit(solution)/shard_map/ppermute | solution.py:863
  131.9 20.0 %collective-permute-start.16 = (bf16[384,1024]{1,0:T(8,128)(2,1)S(1)}, bf16[384,1024]{1,0:T(8,128)(2,1)S(1)}, u32[]{:S(2)}, u32[]{:S(2)}) collective-permute-start(bf16[384,1024]{1,0:T(8,128)(2,1)S(1)} %get-tuple-element.201.x1_ref.refs_5_), channel_id=1, source_target_pairs={{0,2},{1,3},{2,0},{3,1},{4,6},{5,7},{6,4},{7,5},{8,10},{9,11},{10,... | collective-permute-start | bytes 2359304 | tf_op jit(solution)/shard_map/ppermute | solution.py:863
  169.2 17.7 %collective-permute-start.23 = (bf16[192,1024]{1,0:T(8,128)(2,1)S(1)}, bf16[192,1024]{1,0:T(8,128)(2,1)S(1)}, u32[]{:S(2)}, u32[]{:S(2)}) collective-permute-start(bf16[192,1024]{1,0:T(8,128)(2,1)S(1)} %add_convert_fusion.10), channel_id=1, source_target_pairs={{0,2},{1,3},{2,0},{3,1},{4,6},{5,7},{6,4},{7,5},{8,10},{9,11},{10,... | collective-permute-start | bytes 1179656 | tf_op jit(solution)/shard_map/ppermute | solution.py:863
  188.3 20.0 %collective-permute-start.26 = (bf16[384,1024]{1,0:T(8,128)(2,1)S(1)}, bf16[384,1024]{1,0:T(8,128)(2,1)S(1)}, u32[]{:S(2)}, u32[]{:S(2)}) collective-permute-start(bf16[384,1024]{1,0:T(8,128)(2,1)S(1)} %get-tuple-element.214.x1_ref.refs_9_), channel_id=1, source_target_pairs={{0,2},{1,3},{2,0},{3,1},{4,6},{5,7},{6,4},{7,5},{8,10},{9,11},{10,... | collective-permute-start | bytes 2359304 | tf_op jit(solution)/shard_map/ppermute | solution.py:863
  217.3 17.9 %collective-permute-start.31 = (bf16[192,1024]{1,0:T(8,128)(2,1)S(1)}, bf16[192,1024]{1,0:T(8,128)(2,1)S(1)}, u32[]{:S(2)}, u32[]{:S(2)}) collective-permute-start(bf16[192,1024]{1,0:T(8,128)(2,1)S(1)} %add_convert_fusion.8), channel_id=1, source_target_pairs={{0,2},{1,3},{2,0},{3,1},{4,6},{5,7},{6,4},{7,5},{8,10},{9,11},{10,... | collective-permute-start | bytes 1179656 | tf_op jit(solution)/shard_map/ppermute | solution.py:863
  238.1 20.0 %collective-permute-start.34 = (bf16[384,1024]{1,0:T(8,128)(2,1)S(1)}, bf16[384,1024]{1,0:T(8,128)(2,1)S(1)}, u32[]{:S(2)}, u32[]{:S(2)}) collective-permute-start(bf16[384,1024]{1,0:T(8,128)(2,1)S(1)} %get-tuple-element.228.g1_ref.refs_0_), channel_id=1, source_target_pairs={{0,2},{1,3},{2,0},{3,1},{4,6},{5,7},{6,4},{7,5},{8,10},{9,11},{10,... | collective-permute-start | bytes 2359304 | tf_op jit(solution)/shard_map/ppermute | solution.py:863
  266.0 15.0 %collective-permute-start.39 = (bf16[192,1024]{1,0:T(8,128)(2,1)}, bf16[192,1024]{1,0:T(8,128)(2,1)}, u32[]{:S(2)}, u32[]{:S(2)}) collective-permute-start(bf16[192,1024]{1,0:T(8,128)(2,1)} %add_convert_fusion.6), channel_id=1, source_target_pairs={{0,2},{1,3},{2,0},{3,1},{4,6},{5,7},{6,4},{7,5},{8,10},{9,11},{10,... | collective-permute-start | bytes 1179656 | tf_op jit(solution)/shard_map/ppermute | solution.py:863
  281.1 175.9 %reduce-scatter.7.cloned.1.call-start = ((), (), s32[]{:S(2)}) async-start(), calls=%async_computation.5 | async-start | bytes 1769472 | tf_op jit(solution)/shard_map/reduce_scatter | solution.py:915
  297.2 20.0 %collective-permute-start.40 = (bf16[384,1024]{1,0:T(8,128)(2,1)S(1)}, bf16[384,1024]{1,0:T(8,128)(2,1)S(1)}, u32[]{:S(2)}, u32[]{:S(2)}) collective-permute-start(bf16[384,1024]{1,0:T(8,128)(2,1)S(1)} %get-tuple-element.250.x1_ref.refs_0_), channel_id=1, source_target_pairs={{0,2},{1,3},{2,0},{3,1},{4,6},{5,7},{6,4},{7,5},{8,10},{9,11},{10,... | collective-permute-start | bytes 2359304 | tf_op jit(solution)/shard_map/ppermute | solution.py:863
  341.6 18.8 %collective-permute-start.45 = (bf16[192,1024]{1,0:T(8,128)(2,1)}, bf16[192,1024]{1,0:T(8,128)(2,1)S(1)}, u32[]{:S(2)}, u32[]{:S(2)}) collective-permute-start(bf16[192,1024]{1,0:T(8,128)(2,1)} %add_convert_fusion.5), channel_id=1, source_target_pairs={{0,2},{1,3},{2,0},{3,1},{4,6},{5,7},{6,4},{7,5},{8,10},{9,11},{10,... | collective-permute-start | bytes 1179656 | tf_op jit(solution)/shard_map/ppermute | solution.py:863
  352.7 177.4 %reduce-scatter.9.cloned.1.call-start = ((), (), s32[]{:S(2)}) async-start(), calls=%async_computation.6 | async-start | bytes 2359296 | tf_op jit(solution)/shard_map/reduce_scatter | solution.py:915
  363.1 20.0 %collective-permute-start.48 = (bf16[384,1024]{1,0:T(8,128)(2,1)S(1)}, bf16[384,1024]{1,0:T(8,128)(2,1)S(1)}, u32[]{:S(2)}, u32[]{:S(2)}) collective-permute-start(bf16[384,1024]{1,0:T(8,128)(2,1)S(1)} %get-tuple-element.267.x1_ref.refs_0_), channel_id=1, source_target_pairs={{0,2},{1,3},{2,0},{3,1},{4,6},{5,7},{6,4},{7,5},{8,10},{9,11},{10,... | collective-permute-start | bytes 2359304 | tf_op jit(solution)/shard_map/ppermute | solution.py:863
  450.3 152.2 %reduce-scatter.11.cloned.1.call-start = ((), (), s32[]{:S(2)}) async-start(), calls=%async_computation.7 | async-start | bytes 2359296 | tf_op jit(solution)/shard_map/reduce_scatter | solution.py:915
  470.7 20.0 %collective-permute-start.58 = (bf16[384,1024]{1,0:T(8,128)(2,1)S(1)}, bf16[384,1024]{1,0:T(8,128)(2,1)S(1)}, u32[]{:S(2)}, u32[]{:S(2)}) collective-permute-start(bf16[384,1024]{1,0:T(8,128)(2,1)S(1)} %get-tuple-element.288.g1_ref.refs_0_), channel_id=1, source_target_pairs={{0,2},{1,3},{2,0},{3,1},{4,6},{5,7},{6,4},{7,5},{8,10},{9,11},{10,... | collective-permute-start | bytes 2359304 | tf_op jit(solution)/shard_map/ppermute | solution.py:863
  506.1 25.8 %collective-permute-start.57 = (bf16[384,1024]{1,0:T(8,128)(2,1)}, bf16[384,1024]{1,0:T(8,128)(2,1)}, u32[]{:S(2)}, u32[]{:S(2)}) collective-permute-start(bf16[384,1024]{1,0:T(8,128)(2,1)} %get-tuple-element.291), channel_id=1, source_target_pairs={{0,1},{1,0},{2,3},{3,2},{4,5},{5,4},{6,7},{7,6},{8,9},{9,8},{10,11... | collective-permute-start | bytes 2359304 | tf_op jit(solution)/shard_map/ppermute | solution.py:863
  507.2 24.8 %collective-permute-start.63 = (bf16[192,1024]{1,0:T(8,128)(2,1)}, bf16[192,1024]{1,0:T(8,128)(2,1)}, u32[]{:S(2)}, u32[]{:S(2)}) collective-permute-start(bf16[192,1024]{1,0:T(8,128)(2,1)} %add_convert_fusion), channel_id=1, source_target_pairs={{0,2},{1,3},{2,0},{3,1},{4,6},{5,7},{6,4},{7,5},{8,10},{9,11},{10,... | collective-permute-start | bytes 1179656 | tf_op jit(solution)/shard_map/ppermute | solution.py:863
  510.3 26.9 %collective-permute-start.61 = (bf16[192,1024]{1,0:T(8,128)(2,1)}, bf16[192,1024]{1,0:T(8,128)(2,1)S(1)}, u32[]{:S(2)}, u32[]{:S(2)}) collective-permute-start(bf16[192,1024]{1,0:T(8,128)(2,1)} %add_convert_fusion.1), channel_id=1, source_target_pairs={{0,2},{1,3},{2,0},{3,1},{4,6},{5,7},{6,4},{7,5},{8,10},{9,11},{10,... | collective-permute-start | bytes 1179656 | tf_op jit(solution)/shard_map/ppermute | solution.py:863
  543.9 31.6 %collective-permute-start.69 = (bf16[2,2,128,1024]{3,2,0,1:T(8,128)(2,1)}, bf16[2,2,128,1024]{3,2,0,1:T(8,128)(2,1)S(1)}, u32[]{:S(2)}, u32[]{:S(2)}) collective-permute-start(bf16[2,2,128,1024]{3,2,0,1:T(8,128)(2,1)} %bitcast.48), channel_id=1, source_target_pairs={{0,4},{4,0},{8,12},{12,8},{16,20},{20,16},{24,28},{28,24},{1,5},{5... | collective-permute-start | bytes 3145736 | tf_op jit(solution)/shard_map/ppermute | solution.py:863
  556.9 20.9 %collective-permute-start.67 = (f32[14084]{0:T(1024)S(1)}, f32[14084]{0:T(1024)S(1)}, u32[]{:S(2)}, u32[]{:S(2)}) collective-permute-start(f32[14084]{0:T(1024)S(1)} %add.196), channel_id=1, source_target_pairs={{0,16},{4,20},{8,24},{12,28},{16,0},{20,4},{24,8},{28,12},{1,17},{... | collective-permute-start | bytes 169016 | tf_op jit(solution)/shard_map/ppermute | solution.py:863
  576.0 21.6 %collective-permute-start.70 = (bf16[2,128,1024]{2,1,0:T(8,128)(2,1)S(1)}, bf16[2,128,1024]{2,1,0:T(8,128)(2,1)S(1)}, u32[]{:S(2)}, u32[]{:S(2)}) collective-permute-start(bf16[2,128,1024]{2,1,0:T(8,128)(2,1)S(1)} %dynamic-slice_bitcast_fusion), channel_id=1, source_target_pairs={{0,8},{4,12},{8,0},{12,4},{16,24},{20,28},{24,16},{28,20},{1,9},{5... | collective-permute-start | bytes 1572872 | tf_op jit(solution)/shard_map/ppermute | solution.py:863
  (229 other events, 1763.9 us)
Sparse Core Ops, SparseCore 0:
  281.2 88.4 reduce-scatter.4
  373.5 64.7 reduce-scatter.6
  450.4 67.9 reduce-scatter.8
  521.8 74.6 reduce-scatter.10

commit v4 on v3

--- a/solution.py
+++ b/solution.py
@@ -38,10 +38,10 @@
 
 
 BUDGET = dict(
-    distance_bias=(3, 12), enter=(1, 8), join=(2, 8), turn=(3, 12), join_back=(3, 12),
-    ff_rows=(4, 28), ff_back_rows=(4, 28), project=(2, 20), expand=(2, 16),
-    weight_grads=(5, 40), attend=(24, 40), attend_back=(43, 48),
-    conv_forward=(11, 40), conv_backward=(17, 48),
+    distance_bias=(3, 12), enter=(1, 4), join=(2, 4), turn=(3, 6), join_back=(3, 5),
+    ff_rows=(4, 14), ff_back_rows=(4, 14), project=(2, 10), expand=(2, 8),
+    weight_grads=(5, 20), attend=(24, 24), attend_back=(43, 30),
+    conv_forward=(11, 20), conv_backward=(9, 28), taps_backward=(8, 12),
 )
 COST_SCALE = 0.1
 
@@ -745,9 +745,9 @@
 ):
     pieces, refs = refs[:2], refs[2:]
     (
-        glu_ref, taps_ref, lab_ref, gated_ref, mixed_ref,
-        dglu_ref, dtaps_ref,
-        grad_ref, window_ref, source_ref, slope_ref, dgate_ref, sums_ref,
+        glu_ref, taps_ref, lab_ref, mixed_ref,
+        dglu_ref, slope_ref,
+        grad_ref, window_ref, dgate_ref,
     ) = refs
     size = glu_ref.shape[0] // blocks
     assemble(grad_ref, pieces)
@@ -771,11 +771,7 @@
         slope_ref[lane, EDGE : EDGE + rows, :] = slope_ref[lane, EDGE : EDGE + rows, :] * (
             gate * (1.0 + mixed * (1.0 - gate))
         )
-        source_ref[lane, :EDGE, :] = jnp.zeros((EDGE, TILE), F32)
-        source_ref[lane, EDGE : EDGE + rows, :] = gated_ref[:, lane * TILE : (lane + 1) * TILE]
-        source_ref[lane, EDGE + rows :, :] = jnp.zeros((EDGE, TILE), F32)
         dgate_ref[lane, rows:, :] = jnp.zeros((dgate_ref.shape[1] - rows, TILE), F32)
-    sums_ref[...] = jnp.zeros_like(sums_ref)
 
     def chunk(index, carry):
         base = pl.multiple_of(index * TILE, TILE)
@@ -783,21 +779,15 @@
         center = labels[EDGE : EDGE + TILE]
         for lane in range(lanes):
             slopes = slope_ref[lane, pl.ds(base, span), :]
-            sources = source_ref[lane, pl.ds(base, span), :]
 
             def segment(label, total):
-                window_ref[0] = jnp.where(labels == label, slopes, 0.0)
-                window_ref[1] = jnp.where(labels == label, sources, 0.0)
-                inner = window_ref[0, EDGE : EDGE + TILE, :]
+                window_ref[...] = jnp.where(labels == label, slopes, 0.0)
                 acc = jnp.zeros((TILE, TILE), F32)
                 for tap in range(taps):
                     first = EDGE - tap + half
-                    acc = acc + window_ref[0, first : first + TILE, :] * taps_ref[
+                    acc = acc + window_ref[first : first + TILE, :] * taps_ref[
                         tap : tap + 1, lane * TILE : (lane + 1) * TILE
                     ]
-                    first = EDGE + tap - half
-                    part = fold(inner * window_ref[1, first : first + TILE, :])
-                    sums_ref[lane, tap] += jnp.sum(part, axis=0)
                 return jnp.where(center == label, acc, total)
 
             dgate_ref[lane, pl.ds(base, TILE), :] = lax.fori_loop(
@@ -806,8 +796,6 @@
         return carry
 
     lax.fori_loop(0, chunks, chunk, 0)
-    for lane in range(lanes):
-        dtaps_ref[:, lane * TILE : (lane + 1) * TILE] = jnp.sum(sums_ref[lane], axis=1)
     valid = lax.broadcasted_iota(jnp.int32, (size, TILE), 0) < frames
     for block in range(blocks):
         here = pl.ds(pl.multiple_of(order_ref[block] * size, TILE), size)
@@ -822,40 +810,97 @@
             dglu_ref[here, follow] = (rows_in * value * gate * (1.0 - gate)).astype(BF16)
 
 
-def conv_backward(pieces, glu, taps, plan, gated, mixed):
+def conv_backward(pieces, glu, taps, plan, mixed):
     channels = glu.shape[1] // 2
     blocks, frames, chunks = 4, plan["frames"], plan["chunks"]
     rows = chunks * TILE
     lanes = channels // TILE
+    slope = (lanes, rows + 2 * EDGE, TILE)
     return call(
         functools.partial(
             conv_back_body, blocks=blocks, frames=frames, chunks=chunks,
             lanes=lanes, taps=taps.shape[0],
         ),
         "conv_backward",
-        [shaped(glu.shape, BF16), shaped(taps.shape, F32)],
+        [shaped(glu.shape, BF16), shaped(slope, F32)],
         grid_spec=pltpu.PrefetchScalarGridSpec(
             num_scalar_prefetch=3,
             grid=(1,),
             in_specs=[fixed(*piece.shape) for piece in pieces]
             + [
                 fixed(*glu.shape), fixed(*taps.shape), fixed(*plan["flat_lab"].shape),
-                fixed(rows, channels), fixed(rows, channels),
+                fixed(rows, channels),
             ],
-            out_specs=[fixed(*glu.shape), fixed(*taps.shape)],
+            out_specs=[fixed(*glu.shape), fixed(*slope)],
             scratch_shapes=[
                 pltpu.VMEM((glu.shape[0], channels), F32),
-                pltpu.VMEM((2, TILE + 2 * EDGE, TILE), F32),
-                pltpu.VMEM((lanes, rows + 2 * EDGE, TILE), F32),
-                pltpu.VMEM((lanes, rows + 2 * EDGE, TILE), F32),
+                pltpu.VMEM((TILE + 2 * EDGE, TILE), F32),
                 pltpu.VMEM((lanes, rows + EDGE, TILE), F32),
-                pltpu.VMEM((lanes, taps.shape[0], 8, TILE), F32),
             ],
         ),
-    )(
-        plan["order"], plan["low"], plan["high"],
-        *pieces, glu, taps, plan["flat_lab"], gated, mixed,
-    )
+    )(plan["order"], plan["low"], plan["high"], *pieces, glu, taps, plan["flat_lab"], mixed)
+
+
+def taps_body(
+    low_ref, high_ref, slope_ref, gated_ref, lab_ref, dtaps_ref, source_ref, window_ref, sums_ref,
+    *, chunks, lanes, taps,
+):
+    half = taps // 2
+    span = TILE + 2 * EDGE
+    rows = chunks * TILE
+    for lane in range(lanes):
+        source_ref[lane, :EDGE, :] = jnp.zeros((EDGE, TILE), F32)
+        source_ref[lane, EDGE : EDGE + rows, :] = gated_ref[:, lane * TILE : (lane + 1) * TILE]
+        source_ref[lane, EDGE + rows :, :] = jnp.zeros((EDGE, TILE), F32)
+    sums_ref[...] = jnp.zeros_like(sums_ref)
+
+    def chunk(index, carry):
+        base = pl.multiple_of(index * TILE, TILE)
+        labels = lab_ref[pl.ds(base, span), :]
+        center = labels[EDGE : EDGE + TILE]
+        for lane in range(lanes):
+            slopes = slope_ref[lane, pl.ds(base + EDGE, TILE), :]
+            sources = source_ref[lane, pl.ds(base, span), :]
+
+            def segment(label, kept):
+                window_ref[...] = jnp.where(labels == label, sources, 0.0)
+                inner = jnp.where(center == label, slopes, 0.0)
+                for tap in range(taps):
+                    first = EDGE + tap - half
+                    part = fold(inner * window_ref[first : first + TILE, :])
+                    sums_ref[lane, tap] += jnp.sum(part, axis=0)
+                return kept
+
+            lax.fori_loop(low_ref[index], high_ref[index] + 1, segment, 0)
+        return carry
+
+    lax.fori_loop(0, chunks, chunk, 0)
+    for lane in range(lanes):
+        dtaps_ref[:, lane * TILE : (lane + 1) * TILE] = jnp.sum(sums_ref[lane], axis=1)
+
+
+def taps_backward(slope, gated, plan, taps):
+    lanes, padded, _ = slope.shape
+    chunks = plan["chunks"]
+    shape = (taps, lanes * TILE)
+    return call(
+        functools.partial(taps_body, chunks=chunks, lanes=lanes, taps=taps),
+        "taps_backward",
+        shaped(shape, F32),
+        grid_spec=pltpu.PrefetchScalarGridSpec(
+            num_scalar_prefetch=2,
+            grid=(1,),
+            in_specs=[
+                fixed(*slope.shape), fixed(*gated.shape), fixed(*plan["flat_lab"].shape),
+            ],
+            out_specs=fixed(*shape),
+            scratch_shapes=[
+                pltpu.VMEM((lanes, padded, TILE), F32),
+                pltpu.VMEM((TILE + 2 * EDGE, TILE), F32),
+                pltpu.VMEM((lanes, taps, 8, TILE), F32),
+            ],
+        ),
+    )(plan["low"], plan["high"], slope, gated, plan["flat_lab"])
 
 
 def swap(values, bit, axis="tensor"):
@@ -904,15 +949,15 @@
         kept = lax.dynamic_index_in_dim(values, keep, dim, keepdims=False)
         arrived = swap(sent, 1 << bit, "dp")
         if bit == 0:
-            arrived, _ = tie(arrived, gate)
+            arrived, gate = tie(arrived, gate)
         values = kept.astype(F32) + arrived.astype(F32)
         if bit < bits - 1:
             values = values.astype(BF16)
-    return values
+    return values, gate
 
 
 def settle(grads):
-    return lax.psum_scatter(grads, "dp", scatter_dimension=0, tiled=True).astype(F32)
+    return lax.psum_scatter(grads, "dp", scatter_dimension=0, tiled=True)
 
 
 def halves(array):
@@ -1059,9 +1104,7 @@
     grads, e3, sums = join_back(e4, three, parts, gain_four, 1.0)
     grad_four = total(sums)
     grads = gather(grads)
-    dglu, grad_kernel = conv_backward(
-        spread(grads, w_back, 1, F32), glu, kernel, plan, gated, mixed
-    )
+    dglu, slope = conv_backward(spread(grads, w_back, 1, F32), glu, kernel, plan, mixed)
     parts, grad_w = delayed(
         collect(dglu, glu_matrix, 1), weight_grads([(grads, [act]), (h_three, [dglu])])
     )
@@ -1069,6 +1112,8 @@
     grads, e2, sums = join_back(e3, two, parts, gain_three, 1.0)
     grad_three = total(sums)
     grads = gather(grads)
+    grad_kernel = taps_backward(slope, gated, plan, kernel.shape[0])
+    grads[2], grad_kernel = tie(grads[2], grad_kernel)
     pulled = spread(grads, w_output, 1, BF16)
     (first, second), settled_four = tie(pulled, settled_four)
     dqkv, table_sums = attend_back((first, second), qkv, bias, plan, out, lse)
@@ -1085,11 +1130,12 @@
     grad_first_out = settle(grad_w)
     own, beside, (near_rows, far_rows) = parts
     near_rows, settled_two = tie(near_rows, settled_two)
-    parts, grad_first_in = delayed(
+    (_, _, (near_rows, _)), grad_first_in = delayed(
         [own, beside, [near_rows, far_rows]], weight_grads([(zigzag(h_one), inner)])
     )
+    grad_first_in, far_rows = halve_all(grad_first_in, far_rows)
+    parts = [own, beside, [near_rows, far_rows]]
     e0, sums = join_back(e1, start, parts, gain_one, 0.0)
-    grad_first_in = halve_all(grad_first_in, sums[-1])
     small, sums = tie(
         (table_sums, grad_kernel, grad_two, grad_three, grad_four, grad_five), sums
     )
@@ -1112,6 +1158,9 @@
     grad_table = rest[: grad_table.size].reshape(grad_table.shape)
     grad_kernel = rest[grad_table.size :].reshape(grad_kernel.shape)
     part, own = w_query.shape[1], w_output.shape[0]
+    settled_two, settled_three, settled_four, grad_first_out = (
+        x.astype(F32) for x in (settled_two, settled_three, settled_four, grad_first_out)
+    )
     return (
         jnp.concatenate(output, 0)[:frames].reshape(inputs.shape),
         e0[:frames].reshape(inputs.shape),

time: 629 us -> 623 us (level)
  local copies, waits for them, and re-layouts: 67.3 us -> 86.7 us
  Pallas kernels: 207 us -> 194 us
  other arithmetic: 25 us -> 18.2 us
    ppermute x72, waiting for transfers between devices: 252 us -> 219 us  [swap(): return lax.ppermute(values, axis, [(i, i ^ bit) for i in range(count)])]
    reduce_scatter x4, waiting for transfers between devices: 0.01 us -> 29.4 us  [settle(): return lax.psum_scatter(grads, 'dp', scatter_dimension=0, tiled=True)]
    unnamed x364 -> x424, local copies, waits for them, and re-layouts: 56.9 us -> 74.5 us
    pallas_call x1, Pallas kernels: 14.9 us -> 7.21 us  [conv_backward(): call(functools.partial(conv_back_body, blocks=blocks, frames=frames, chun...]
    pallas_call x1, Pallas kernels: 40.2 us -> 32.6 us  [attend_back(): call(functools.partial(attend_back_body, tiles=tiles, pairs=pairs, scale=...]
  transfers between devices with their start and end apart: 76 -> 76, of which waited for: 43 -> 46; matrix products, arithmetic and copies ran while one was open for 7% -> 6% of each run, Pallas kernels for 26% -> 25%
where the time goes in v4:
time: 623 us; the launch traced here: 614 us
  waiting for transfers between devices  248 us (40%)
  Pallas kernels  194 us (31%)
  local copies, waits for them, and re-layouts  86.7 us (14%)
  starting transfers between devices  47.9 us (8%)
  other arithmetic  18.2 us (3%)
  between operations  16.7 us (3%)
    ppermute x72, waiting for transfers between devices, swap(): return lax.ppermute(values, axis, [(i, i ^ bit) for i in range(count)])  219 us
    unnamed x424, local copies, waits for them, and re-layouts  74.5 us
    ppermute x72, starting transfers between devices, swap(): return lax.ppermute(values, axis, [(i, i ^ bit) for i in range(count)])  47.7 us
    pallas_call x1, Pallas kernels, attend_back(): call(functools.partial(attend_back_body, tiles=tiles, pairs=pairs, scale=...  32.6 us
    pallas_call x16, Pallas kernels, by_chunks(): call(run, name, shapes, grid=(1,), in_specs=specs, out_specs=outs, input_...  32.2 us
    reduce_scatter x4, waiting for transfers between devices, settle(): return lax.psum_scatter(grads, 'dp', scatter_dimension=0, tiled=True)  29.4 us
    pallas_call x6, Pallas kernels, ff_back_rows(): call(body, 'ff_back_rows', [shaped(a.shape, BF16)] + [shaped((rows, width...  26.8 us
    pallas_call x5, Pallas kernels, weight_grads(): call(body, 'weight_grads', shaped((height, column), BF16), grid=(1,), in_...  25.3 us
  transfers between devices with their start and end apart: 76, of which 46 were waited for; matrix products, arithmetic and copies ran while one was open for 6% of the time, Pallas kernels for 25%

profile of v4, /device:TPU:0, one launch (start us, length us, event | category | flops | bytes accessed | tf_op | source)
XLA Modules:
  0.0 613.7 jit_solution(4944206141466055952)
XLA Ops:
  23.1 9.8 %collective-permute-done.2.x1_ref.refs_2_.refs_4_ = bf16[384,1024]{1,0:T(8,128)(2,1)S(1)} collective-permute-done((bf16[384,1024]{1,0:T(8,128)(2,1)S(1)}, bf16[384,1024]{1,0:T(8,128)(2,1)S(1)}, u32[]{:S(2)}, u32[]{:S(2)}) %collective-permute-start.2) | collective-permute-done | bytes 786464 | tf_op jit(solution)/shard_map/ppermute | solution.py:908
  44.8 8.9 %collective-permute-done.5.p3_ref = bf16[192,1024]{1,0:T(8,128)(2,1)S(1)} collective-permute-done((bf16[192,1024]{1,0:T(8,128)(2,1)S(1)}, bf16[192,1024]{1,0:T(8,128)(2,1)S(1)}, u32[]{:S(2)}, u32[]{:S(2)}) %collective-permute-start.5) | collective-permute-done | bytes 393248 | tf_op jit(solution)/shard_map/ppermute | solution.py:908
  74.6 9.4 %collective-permute-done.8.x1_ref.refs_7_ = bf16[384,1024]{1,0:T(8,128)(2,1)} collective-permute-done((bf16[384,1024]{1,0:T(8,128)(2,1)}, bf16[384,1024]{1,0:T(8,128)(2,1)}, u32[]{:S(2)}, u32[]{:S(2)}) %collective-permute-start.8) | collective-permute-done | bytes 786464 | tf_op jit(solution)/shard_map/ppermute | solution.py:908
  92.5 17.4 %attend.1 = (bf16[1536,256]{1,0:T(8,128)(2,1)S(1)}, f32[12,4,128]{2,1,0:T(4,128)S(1)}, bf16[1536,768]{1,0:T(8,128)(2,1)S(1)}) custom-call(s32[12]{0:T(128)S(1)} %add.169.place_ref, s32[12]{0:T(128)S(1)} %get-tuple-element.406.start_ref, s32[12]{0:T(128)S(1)} %get-tuple-element.407.count_ref, s32[144]{0:T(256)S(1)} %copy-done.184, ...), custom_call_target="tpu_custom_call" | custom-call | flops 2400000000 | bytes 8400000 | tf_op jit(solution)/shard_map/attend/pallas_call | solution.py:477
  117.6 9.5 %collective-permute-done.13.p3_ref = bf16[192,1024]{1,0:T(8,128)(2,1)S(1)} collective-permute-done((bf16[192,1024]{1,0:T(8,128)(2,1)S(1)}, bf16[192,1024]{1,0:T(8,128)(2,1)S(1)}, u32[]{:S(2)}, u32[]{:S(2)}) %collective-permute-start.13) | collective-permute-done | bytes 393248 | tf_op jit(solution)/shard_map/ppermute | solution.py:908
  128.3 6.7 %collective-permute-done.15.refs_3_ = bf16[192,1024]{1,0:T(8,128)(2,1)S(1)} collective-permute-done((bf16[192,1024]{1,0:T(8,128)(2,1)S(1)}, bf16[192,1024]{1,0:T(8,128)(2,1)S(1)}, u32[]{:S(2)}, u32[]{:S(2)}) %collective-permute-start.15) | collective-permute-done | bytes 393248 | tf_op jit(solution)/shard_map/ppermute | solution.py:908
  139.7 16.7 %collective-permute-done.16.x1_ref.refs_7_ = bf16[384,1024]{1,0:T(8,128)(2,1)S(1)} collective-permute-done((bf16[384,1024]{1,0:T(8,128)(2,1)S(1)}, bf16[384,1024]{1,0:T(8,128)(2,1)S(1)}, u32[]{:S(2)}, u32[]{:S(2)}) %collective-permute-start.16) | collective-permute-done | bytes 786464 | tf_op jit(solution)/shard_map/ppermute | solution.py:908
  160.0 6.2 %conv_forward.1 = (bf16[1536,256]{1,0:T(8,128)(2,1)S(1)}, f32[1536,256]{1,0:T(8,128)S(1)}, f32[1536,256]{1,0:T(8,128)S(1)}, f32[1536,512]{1,0:T(8,128)S(1)}) custom-call(s32[4]{0:T(128)S(1)} %get-tuple-element.418.order_ref, s32[12]{0:T(128)S(1)} %get-tuple-element.401.low_ref, s32[12]{0:T(128)S(1)} %get-tuple-element.400.high_ref, ...), custom_call_target="tpu_custom_call" | custom-call | flops 1100000000 | bytes 3850000 | tf_op jit(solution)/shard_map/conv_forward/pallas_call | solution.py:714
  174.0 9.7 %collective-permute-done.21.p3_ref = bf16[192,1024]{1,0:T(8,128)(2,1)S(1)} collective-permute-done((bf16[192,1024]{1,0:T(8,128)(2,1)S(1)}, bf16[192,1024]{1,0:T(8,128)(2,1)S(1)}, u32[]{:S(2)}, u32[]{:S(2)}) %collective-permute-start.21) | collective-permute-done | bytes 393248 | tf_op jit(solution)/shard_map/ppermute | solution.py:908
  185.0 6.3 %collective-permute-done.23.refs_3_ = bf16[192,1024]{1,0:T(8,128)(2,1)S(1)} collective-permute-done((bf16[192,1024]{1,0:T(8,128)(2,1)S(1)}, bf16[192,1024]{1,0:T(8,128)(2,1)S(1)}, u32[]{:S(2)}, u32[]{:S(2)}) %collective-permute-start.23) | collective-permute-done | bytes 393248 | tf_op jit(solution)/shard_map/ppermute | solution.py:908
  199.7 12.9 %collective-permute-done.26.x1_ref.refs_11_.refs_13_ = bf16[384,1024]{1,0:T(8,128)(2,1)S(1)} collective-permute-done((bf16[384,1024]{1,0:T(8,128)(2,1)S(1)}, bf16[384,1024]{1,0:T(8,128)(2,1)S(1)}, u32[]{:S(2)}, u32[]{:S(2)}) %collective-permute-start.26) | collective-permute-done | bytes 786464 | tf_op jit(solution)/shard_map/ppermute | solution.py:908
  222.8 8.9 %collective-permute-done.29.p3_ref = bf16[192,1024]{1,0:T(8,128)(2,1)S(1)} collective-permute-done((bf16[192,1024]{1,0:T(8,128)(2,1)S(1)}, bf16[192,1024]{1,0:T(8,128)(2,1)S(1)}, u32[]{:S(2)}, u32[]{:S(2)}) %collective-permute-start.29) | collective-permute-done | bytes 393248 | tf_op jit(solution)/shard_map/ppermute | solution.py:908
  243.9 6.5 %ff_back_rows.6 = (bf16[768,1024]{1,0:T(8,128)(2,1)S(1)}, bf16[384,1024]{1,0:T(8,128)(2,1)S(1)}, bf16[384,1024]{1,0:T(8,128)(2,1)S(1)}) custom-call(bf16[384,1024]{1,0:T(8,128)(2,1)S(1)} %get-tuple-element.231.g1_ref.refs_0_, bf16[384,1024]{1,0:T(8,128)(2,1)S(1)} %collective-permute-done.32.g2_ref.refs_1_, bf16[768,1024]{1,0:T(8,128)(2,1)S(1)} %get-tuple-element.232.a_ref, ...), custom_call_target="tpu_custom_call" | custom-call | flops 400000000 | bytes 1400000 | tf_op jit(solution)/shard_map/ff_back_rows/pallas_call | solution.py:310
  251.3 10.3 %collective-permute-done.34.g1_ref.refs_2_.refs_4_ = bf16[384,1024]{1,0:T(8,128)(2,1)S(1)} collective-permute-done((bf16[384,1024]{1,0:T(8,128)(2,1)S(1)}, bf16[384,1024]{1,0:T(8,128)(2,1)S(1)}, u32[]{:S(2)}, u32[]{:S(2)}) %collective-permute-start.34) | collective-permute-done | bytes 786464 | tf_op jit(solution)/shard_map/ppermute | solution.py:908
  275.2 7.6 %weight_grads.5 = bf16[1024,2048]{1,0:T(8,128)(2,1)S(1)} custom-call(bf16[384,1024]{1,0:T(8,128)(2,1)S(1)} %get-tuple-element.231.g1_ref.refs_0_, bf16[384,1024]{1,0:T(8,128)(2,1)S(1)} %collective-permute-done.32.g2_ref.refs_1_, bf16[384,1024]{1,0:T(8,128)(2,1)S(1)} %collective-permute-done.34.g1_ref.refs_2_.refs_4_, ...), custom_call_target="tpu_custom_call" | custom-call | flops 500000000 | bytes 1750000 | tf_op jit(solution)/shard_map/weight_grads/pallas_call | solution.py:370
  304.5 17.0 %collective-permute-done.40.x1_ref.refs_2_ = bf16[384,1024]{1,0:T(8,128)(2,1)S(1)} collective-permute-done((bf16[384,1024]{1,0:T(8,128)(2,1)S(1)}, bf16[384,1024]{1,0:T(8,128)(2,1)S(1)}, u32[]{:S(2)}, u32[]{:S(2)}) %collective-permute-start.40) | collective-permute-done | bytes 786464 | tf_op jit(solution)/shard_map/ppermute | solution.py:908
  324.5 7.2 %conv_backward.1 = (bf16[1536,512]{1,0:T(8,128)(2,1)S(1)}, f32[2,1568,128]{2,1,0:T(8,128)S(1)}) custom-call(s32[4]{0:T(128)S(1)} %copy-done.174, s32[12]{0:T(128)S(1)} %copy-done.172, s32[12]{0:T(128)S(1)} %get-tuple-element.400.high_ref, f32[768,256]{1,0:T(8,128)S(1)} %project.12.refs_0_, f32[768,256]{1,0:T(8,128)S(1)} %project.13.refs_1_, ...), custom_call_target="tpu_custom_call" | custom-call | flops 900000000 | bytes 3150000 | tf_op jit(solution)/shard_map/conv_backward/pallas_call | solution.py:819
  366.8 12.8 %collective-permute-done.48.x1_ref.refs_2_ = bf16[384,1024]{1,0:T(8,128)(2,1)S(1)} collective-permute-done((bf16[384,1024]{1,0:T(8,128)(2,1)S(1)}, bf16[384,1024]{1,0:T(8,128)(2,1)S(1)}, u32[]{:S(2)}, u32[]{:S(2)}) %collective-permute-start.48) | collective-permute-done | bytes 786464 | tf_op jit(solution)/shard_map/ppermute | solution.py:908
  392.2 32.6 %attend_back.1 = (bf16[1536,768]{1,0:T(8,128)(2,1)S(1)}, f32[4,9,256]{2,1,0:T(8,128)S(1)}) custom-call(s32[12]{0:T(128)S(1)} %copy-done.176, s32[12]{0:T(128)S(1)} %copy-done.178, s32[12]{0:T(128)S(1)} %copy-done.180, s32[144]{0:T(256)S(1)} %copy-done.185, bf16[768,256]{1,0:T(8,128)(2,1)S(1)} %project.14.refs_0_, bf16[768,256]{1,0:T(8,128)(2,1)S(1)} %copy-done.132, ...), custom_call_target="tpu_custom_call" | custom-call | flops 4300000256 | bytes 15050000 | tf_op jit(solution)/shard_map/attend_back/pallas_call | solution.py:615
  463.4 6.5 %ff_back_rows.9 = (bf16[768,1024]{1,0:T(8,128)(2,1)S(1)}, bf16[384,1024]{1,0:T(8,128)(2,1)S(1)}, bf16[384,1024]{1,0:T(8,128)(2,1)S(1)}) custom-call(bf16[384,1024]{1,0:T(8,128)(2,1)S(1)} %get-tuple-element.293.g1_ref.refs_0_, bf16[384,1024]{1,0:T(8,128)(2,1)S(1)} %collective-permute-done.56.g2_ref.refs_1_, bf16[768,1024]{1,0:T(8,128)(2,1)S(1)} %copy-done.94, ...), custom_call_target="tpu_custom_call" | custom-call | flops 400000000 | bytes 1400000 | tf_op jit(solution)/shard_map/ff_back_rows/pallas_call | solution.py:310
  471.2 8.5 %collective-permute-done.58.g1_ref.refs_2_.refs_4_ = bf16[384,1024]{1,0:T(8,128)(2,1)S(1)} collective-permute-done((bf16[384,1024]{1,0:T(8,128)(2,1)S(1)}, bf16[384,1024]{1,0:T(8,128)(2,1)S(1)}, u32[]{:S(2)}, u32[]{:S(2)}) %collective-permute-start.58) | collective-permute-done | bytes 786464 | tf_op jit(solution)/shard_map/ppermute | solution.py:908
  507.6 15.5 %reduce-scatter.9.cloned.1.call-done = bf16[128,1024]{1,0:T(8,128)(2,1)} async-done(((bf16[1024,1024]{1,0:T(8,128)(2,1)}), bf16[128,1024]{1,0:T(8,128)(2,1)}) %reduce-scatter.9.cloned.1.call-update) | async-done | bytes 262160 | tf_op jit(solution)/shard_map/reduce_scatter | solution.py:960
  544.2 11.1 %collective-permute-done.62 = bf16[2,2,128,1024]{3,2,0,1:T(8,128)(2,1)} collective-permute-done((bf16[2,2,128,1024]{3,2,0,1:T(8,128)(2,1)}, bf16[2,2,128,1024]{3,2,0,1:T(8,128)(2,1)}, u32[]{:S(2)}, u32[]{:S(2)}) %collective-permute-start.62) | collective-permute-done | bytes 1048608 | tf_op jit(solution)/shard_map/ppermute | solution.py:908
  591.7 12.2 %reduce-scatter.11.cloned.1.call-done = bf16[128,1024]{1,0:T(8,128)(2,1)} async-done(((bf16[1024,1024]{1,0:T(8,128)(2,1)}), bf16[128,1024]{1,0:T(8,128)(2,1)}) %reduce-scatter.11.cloned.1.call-update) | async-done | bytes 262160 | tf_op jit(solution)/shard_map/reduce_scatter | solution.py:960
  (706 shorter events, 326.8 us)
Async XLA Ops:
  7.2 376.7 %reduce-scatter.5.cloned.1.call-start = ((), (), s32[]{:S(2)}) async-start(), calls=%async_computation.4 | async-start | bytes 4718592 | tf_op jit(solution)/shard_map/reduce_scatter | solution.py:960
  12.1 20.7 %collective-permute-start.2 = (bf16[384,1024]{1,0:T(8,128)(2,1)S(1)}, bf16[384,1024]{1,0:T(8,128)(2,1)S(1)}, u32[]{:S(2)}, u32[]{:S(2)}) collective-permute-start(bf16[384,1024]{1,0:T(8,128)(2,1)S(1)} %enter.1.x1_ref.refs_0_), channel_id=1, source_target_pairs={{0,2},{1,3},{2,0},{3,1},{4,6},{5,7},{6,4},{7,5},{8,10},{9,11},{10,... | collective-permute-start | bytes 2359304 | tf_op jit(solution)/shard_map/ppermute | solution.py:908
  43.8 17.9 %collective-permute-start.7 = (bf16[192,1024]{1,0:T(8,128)(2,1)S(1)}, bf16[192,1024]{1,0:T(8,128)(2,1)S(1)}, u32[]{:S(2)}, u32[]{:S(2)}) collective-permute-start(bf16[192,1024]{1,0:T(8,128)(2,1)S(1)} %add_convert_fusion.14), channel_id=1, source_target_pairs={{0,2},{1,3},{2,0},{3,1},{4,6},{5,7},{6,4},{7,5},{8,10},{9,11},{10,... | collective-permute-start | bytes 1179656 | tf_op jit(solution)/shard_map/ppermute | solution.py:908
  64.6 19.4 %collective-permute-start.8 = (bf16[384,1024]{1,0:T(8,128)(2,1)}, bf16[384,1024]{1,0:T(8,128)(2,1)}, u32[]{:S(2)}, u32[]{:S(2)}) collective-permute-start(bf16[384,1024]{1,0:T(8,128)(2,1)} %get-tuple-element.191.x1_ref.refs_5_), channel_id=1, source_target_pairs={{0,2},{1,3},{2,0},{3,1},{4,6},{5,7},{6,4},{7,5},{8,10},{9,11},{10,... | collective-permute-start | bytes 2359304 | tf_op jit(solution)/shard_map/ppermute | solution.py:908
  117.0 18.1 %collective-permute-start.15 = (bf16[192,1024]{1,0:T(8,128)(2,1)S(1)}, bf16[192,1024]{1,0:T(8,128)(2,1)S(1)}, u32[]{:S(2)}, u32[]{:S(2)}) collective-permute-start(bf16[192,1024]{1,0:T(8,128)(2,1)S(1)} %add_convert_fusion.12), channel_id=1, source_target_pairs={{0,2},{1,3},{2,0},{3,1},{4,6},{5,7},{6,4},{7,5},{8,10},{9,11},{10,... | collective-permute-start | bytes 1179656 | tf_op jit(solution)/shard_map/ppermute | solution.py:908
  136.5 20.0 %collective-permute-start.16 = (bf16[384,1024]{1,0:T(8,128)(2,1)S(1)}, bf16[384,1024]{1,0:T(8,128)(2,1)S(1)}, u32[]{:S(2)}, u32[]{:S(2)}) collective-permute-start(bf16[384,1024]{1,0:T(8,128)(2,1)S(1)} %get-tuple-element.204.x1_ref.refs_5_), channel_id=1, source_target_pairs={{0,2},{1,3},{2,0},{3,1},{4,6},{5,7},{6,4},{7,5},{8,10},{9,11},{10,... | collective-permute-start | bytes 2359304 | tf_op jit(solution)/shard_map/ppermute | solution.py:908
  173.6 17.7 %collective-permute-start.23 = (bf16[192,1024]{1,0:T(8,128)(2,1)S(1)}, bf16[192,1024]{1,0:T(8,128)(2,1)S(1)}, u32[]{:S(2)}, u32[]{:S(2)}) collective-permute-start(bf16[192,1024]{1,0:T(8,128)(2,1)S(1)} %add_convert_fusion.10), channel_id=1, source_target_pairs={{0,2},{1,3},{2,0},{3,1},{4,6},{5,7},{6,4},{7,5},{8,10},{9,11},{10,... | collective-permute-start | bytes 1179656 | tf_op jit(solution)/shard_map/ppermute | solution.py:908
  192.7 20.0 %collective-permute-start.26 = (bf16[384,1024]{1,0:T(8,128)(2,1)S(1)}, bf16[384,1024]{1,0:T(8,128)(2,1)S(1)}, u32[]{:S(2)}, u32[]{:S(2)}) collective-permute-start(bf16[384,1024]{1,0:T(8,128)(2,1)S(1)} %get-tuple-element.217.x1_ref.refs_9_), channel_id=1, source_target_pairs={{0,2},{1,3},{2,0},{3,1},{4,6},{5,7},{6,4},{7,5},{8,10},{9,11},{10,... | collective-permute-start | bytes 2359304 | tf_op jit(solution)/shard_map/ppermute | solution.py:908
  221.7 18.0 %collective-permute-start.31 = (bf16[192,1024]{1,0:T(8,128)(2,1)S(1)}, bf16[192,1024]{1,0:T(8,128)(2,1)S(1)}, u32[]{:S(2)}, u32[]{:S(2)}) collective-permute-start(bf16[192,1024]{1,0:T(8,128)(2,1)S(1)} %add_convert_fusion.8), channel_id=1, source_target_pairs={{0,2},{1,3},{2,0},{3,1},{4,6},{5,7},{6,4},{7,5},{8,10},{9,11},{10,... | collective-permute-start | bytes 1179656 | tf_op jit(solution)/shard_map/ppermute | solution.py:908
  241.7 20.0 %collective-permute-start.34 = (bf16[384,1024]{1,0:T(8,128)(2,1)S(1)}, bf16[384,1024]{1,0:T(8,128)(2,1)S(1)}, u32[]{:S(2)}, u32[]{:S(2)}) collective-permute-start(bf16[384,1024]{1,0:T(8,128)(2,1)S(1)} %get-tuple-element.231.g1_ref.refs_0_), channel_id=1, source_target_pairs={{0,2},{1,3},{2,0},{3,1},{4,6},{5,7},{6,4},{7,5},{8,10},{9,11},{10,... | collective-permute-start | bytes 2359304 | tf_op jit(solution)/shard_map/ppermute | solution.py:908
  269.7 15.2 %collective-permute-start.39 = (bf16[192,1024]{1,0:T(8,128)(2,1)}, bf16[192,1024]{1,0:T(8,128)(2,1)}, u32[]{:S(2)}, u32[]{:S(2)}) collective-permute-start(bf16[192,1024]{1,0:T(8,128)(2,1)} %add_convert_fusion.6), channel_id=1, source_target_pairs={{0,2},{1,3},{2,0},{3,1},{4,6},{5,7},{6,4},{7,5},{8,10},{9,11},{10,... | collective-permute-start | bytes 1179656 | tf_op jit(solution)/shard_map/ppermute | solution.py:908
  284.9 163.0 %reduce-scatter.7.cloned.1.call-start = ((), (), s32[]{:S(2)}) async-start(), calls=%async_computation.5 | async-start | bytes 1769472 | tf_op jit(solution)/shard_map/reduce_scatter | solution.py:960
  301.6 20.0 %collective-permute-start.40 = (bf16[384,1024]{1,0:T(8,128)(2,1)S(1)}, bf16[384,1024]{1,0:T(8,128)(2,1)S(1)}, u32[]{:S(2)}, u32[]{:S(2)}) collective-permute-start(bf16[384,1024]{1,0:T(8,128)(2,1)S(1)} %get-tuple-element.253.x1_ref.refs_0_), channel_id=1, source_target_pairs={{0,2},{1,3},{2,0},{3,1},{4,6},{5,7},{6,4},{7,5},{8,10},{9,11},{10,... | collective-permute-start | bytes 2359304 | tf_op jit(solution)/shard_map/ppermute | solution.py:908
  339.4 19.1 %collective-permute-start.45 = (bf16[192,1024]{1,0:T(8,128)(2,1)}, bf16[192,1024]{1,0:T(8,128)(2,1)S(1)}, u32[]{:S(2)}, u32[]{:S(2)}) collective-permute-start(bf16[192,1024]{1,0:T(8,128)(2,1)} %add_convert_fusion.5), channel_id=1, source_target_pairs={{0,2},{1,3},{2,0},{3,1},{4,6},{5,7},{6,4},{7,5},{8,10},{9,11},{10,... | collective-permute-start | bytes 1179656 | tf_op jit(solution)/shard_map/ppermute | solution.py:908
  350.4 172.7 %reduce-scatter.9.cloned.1.call-start = ((), (), s32[]{:S(2)}) async-start(), calls=%async_computation.6 | async-start | bytes 2359296 | tf_op jit(solution)/shard_map/reduce_scatter | solution.py:960
  360.9 18.7 %collective-permute-start.48 = (bf16[384,1024]{1,0:T(8,128)(2,1)S(1)}, bf16[384,1024]{1,0:T(8,128)(2,1)S(1)}, u32[]{:S(2)}, u32[]{:S(2)}) collective-permute-start(bf16[384,1024]{1,0:T(8,128)(2,1)S(1)} %get-tuple-element.269.x1_ref.refs_0_), channel_id=1, source_target_pairs={{0,2},{1,3},{2,0},{3,1},{4,6},{5,7},{6,4},{7,5},{8,10},{9,11},{10,... | collective-permute-start | bytes 2359304 | tf_op jit(solution)/shard_map/ppermute | solution.py:908
  361.2 18.4 %collective-permute-start.49 = (bf16[384,1024]{1,0:T(8,128)(2,1)S(1)}, bf16[384,1024]{1,0:T(8,128)(2,1)S(1)}, u32[]{:S(2)}, u32[]{:S(2)}) collective-permute-start(bf16[384,1024]{1,0:T(8,128)(2,1)S(1)} %get-tuple-element.269.x1_ref.refs_0_), channel_id=1, source_target_pairs={{0,1},{1,0},{2,3},{3,2},{4,5},{5,4},{6,7},{7,6},{8,9},{9,8},{10,11... | collective-permute-start | bytes 2359304 | tf_op jit(solution)/shard_map/ppermute | solution.py:908
  440.1 163.7 %reduce-scatter.11.cloned.1.call-start = ((), (), s32[]{:S(2)}) async-start(), calls=%async_computation.7 | async-start | bytes 2359296 | tf_op jit(solution)/shard_map/reduce_scatter | solution.py:960
  459.7 20.0 %collective-permute-start.58 = (bf16[384,1024]{1,0:T(8,128)(2,1)S(1)}, bf16[384,1024]{1,0:T(8,128)(2,1)S(1)}, u32[]{:S(2)}, u32[]{:S(2)}) collective-permute-start(bf16[384,1024]{1,0:T(8,128)(2,1)S(1)} %get-tuple-element.293.g1_ref.refs_0_), channel_id=1, source_target_pairs={{0,2},{1,3},{2,0},{3,1},{4,6},{5,7},{6,4},{7,5},{8,10},{9,11},{10,... | collective-permute-start | bytes 2359304 | tf_op jit(solution)/shard_map/ppermute | solution.py:908
  495.1 42.1 %collective-permute-start.57 = (bf16[384,1024]{1,0:T(8,128)(2,1)}, bf16[384,1024]{1,0:T(8,128)(2,1)}, u32[]{:S(2)}, u32[]{:S(2)}) collective-permute-start(bf16[384,1024]{1,0:T(8,128)(2,1)} %copy-done.181), channel_id=1, source_target_pairs={{0,1},{1,0},{2,3},{3,2},{4,5},{5,4},{6,7},{7,6},{8,9},{9,8},{10,11... | collective-permute-start | bytes 2359304 | tf_op jit(solution)/shard_map/ppermute | solution.py:908
  503.0 28.7 %collective-permute-start.63 = (bf16[192,1024]{1,0:T(8,128)(2,1)}, bf16[192,1024]{1,0:T(8,128)(2,1)}, u32[]{:S(2)}, u32[]{:S(2)}) collective-permute-start(bf16[192,1024]{1,0:T(8,128)(2,1)} %get-tuple-element.310), channel_id=1, source_target_pairs={{0,1},{1,0},{2,3},{3,2},{4,5},{5,4},{6,7},{7,6},{8,9},{9,8},{10,11... | collective-permute-start | bytes 1179656 | tf_op jit(solution)/shard_map/ppermute | solution.py:908
  525.6 29.8 %collective-permute-start.62 = (bf16[2,2,128,1024]{3,2,0,1:T(8,128)(2,1)}, bf16[2,2,128,1024]{3,2,0,1:T(8,128)(2,1)}, u32[]{:S(2)}, u32[]{:S(2)}) collective-permute-start(bf16[2,2,128,1024]{3,2,0,1:T(8,128)(2,1)} %bitcast.48), channel_id=1, source_target_pairs={{0,4},{4,0},{8,12},{12,8},{16,20},{20,16},{24,28},{28,24},{1,5},{5... | collective-permute-start | bytes 3145736 | tf_op jit(solution)/shard_map/ppermute | solution.py:908
  566.0 18.5 %collective-permute-start.70 = (bf16[2,128,1024]{2,1,0:T(8,128)(2,1)}, bf16[2,128,1024]{2,1,0:T(8,128)(2,1)}, u32[]{:S(2)}, u32[]{:S(2)}) collective-permute-start(bf16[2,128,1024]{2,1,0:T(8,128)(2,1)} %dynamic-slice_bitcast_fusion), channel_id=1, source_target_pairs={{0,8},{4,12},{8,0},{12,4},{16,24},{20,28},{24,16},{28,20},{1,9},{5... | collective-permute-start | bytes 1572872 | tf_op jit(solution)/shard_map/ppermute | solution.py:908
  585.8 20.1 %collective-permute-start.71 = (bf16[128,1024]{1,0:T(8,128)(2,1)S(1)}, bf16[128,1024]{1,0:T(8,128)(2,1)S(1)}, u32[]{:S(2)}, u32[]{:S(2)}) collective-permute-start(bf16[128,1024]{1,0:T(8,128)(2,1)S(1)} %dynamic-slice_bitcast_fusion.1), channel_id=1, source_target_pairs={{0,16},{4,20},{8,24},{12,28},{16,0},{20,4},{24,8},{28,12},{1,17},{... | collective-permute-start | bytes 786440 | tf_op jit(solution)/shard_map/ppermute | solution.py:908
  (258 other events, 1705.9 us)
Sparse Core Ops, SparseCore 0:
  285.0 94.3 reduce-scatter.4
  383.2 64.6 reduce-scatter.6
  451.4 71.6 reduce-scatter.8
  526.5 77.2 reduce-scatter.10

commit v5 on v4

--- a/solution.py
+++ b/solution.py
@@ -54,7 +54,7 @@
         out_shape=out_shape,
         compiler_params=pltpu.CompilerParams(vmem_limit_bytes=limit * 2**20),
         cost_estimate=pl.CostEstimate(
-            flops=int(time * 1e9), bytes_accessed=int(time * 3.5e6), transcendentals=0
+            flops=1024, bytes_accessed=int(time * 3.5e6), transcendentals=0
         ),
         name=name,
         **options,
@@ -947,9 +947,9 @@
         keep = (lax.axis_index("dp") >> bit) & 1
         sent = lax.dynamic_index_in_dim(values, 1 - keep, dim, keepdims=False)
         kept = lax.dynamic_index_in_dim(values, keep, dim, keepdims=False)
+        if bit == 1:
+            sent, gate = tie(sent, gate)
         arrived = swap(sent, 1 << bit, "dp")
-        if bit == 0:
-            arrived, gate = tie(arrived, gate)
         values = kept.astype(F32) + arrived.astype(F32)
         if bit < bits - 1:
             values = values.astype(BF16)

time: 623 us -> 617 us (level)
  waiting for transfers between devices: 248 us -> 234 us
  Pallas kernels: 194 us -> 203 us
    reduce_scatter x4, waiting for transfers between devices: 29.4 us -> 8.35 us  [settle(): return lax.psum_scatter(grads, 'dp', scatter_dimension=0, tiled=True)]
    ppermute x72, waiting for transfers between devices: 219 us -> 226 us  [swap(): return lax.ppermute(values, axis, [(i, i ^ bit) for i in range(count)])]
    unnamed x424 -> x428, local copies, waits for them, and re-layouts: 74.5 us -> 73.6 us
  transfers between devices with their start and end apart: 76 -> 76, of which waited for: 46 -> 49; matrix products, arithmetic and copies ran while one was open for 6% -> 6% of each run, Pallas kernels for 25% -> 26%
where the time goes in v5:
time: 617 us; the launch traced here: 605 us
  waiting for transfers between devices  234 us (38%)
  Pallas kernels  203 us (33%)
  local copies, waits for them, and re-layouts  85.5 us (14%)
  starting transfers between devices  47 us (8%)
  between operations  16.8 us (3%)
  other arithmetic  16 us (3%)
    ppermute x72, waiting for transfers between devices, swap(): return lax.ppermute(values, axis, [(i, i ^ bit) for i in range(count)])  226 us
    unnamed x428, local copies, waits for them, and re-layouts  73.6 us
    ppermute x72, starting transfers between devices, swap(): return lax.ppermute(values, axis, [(i, i ^ bit) for i in range(count)])  46.8 us
    pallas_call x1, Pallas kernels, attend_back(): call(functools.partial(attend_back_body, tiles=tiles, pairs=pairs, scale=...  38.4 us
    pallas_call x16, Pallas kernels, by_chunks(): call(run, name, shapes, grid=(1,), in_specs=specs, out_specs=outs, input_...  31 us
    pallas_call x6, Pallas kernels, ff_back_rows(): call(body, 'ff_back_rows', [shaped(a.shape, BF16)] + [shaped((rows, width...  25.9 us
    pallas_call x5, Pallas kernels, weight_grads(): call(body, 'weight_grads', shaped((height, column), BF16), grid=(1,), in_...  25.3 us
    pallas_call x1, Pallas kernels, attend(): call(functools.partial(attend_body, tiles=tiles, pairs=pairs, scale=plan[...  21.6 us
  transfers between devices with their start and end apart: 76, of which 49 were waited for; matrix products, arithmetic and copies ran while one was open for 6% of the time, Pallas kernels for 26%

profile of v5, /device:TPU:0, one launch (start us, length us, event | category | flops | bytes accessed | tf_op | source)
XLA Modules:
  0.0 605.0 jit_solution(7016390348105600939)
XLA Ops:
  23.1 9.8 %collective-permute-done.2.x1_ref.refs_2_.refs_4_ = bf16[384,1024]{1,0:T(8,128)(2,1)S(1)} collective-permute-done((bf16[384,1024]{1,0:T(8,128)(2,1)S(1)}, bf16[384,1024]{1,0:T(8,128)(2,1)S(1)}, u32[]{:S(2)}, u32[]{:S(2)}) %collective-permute-start.2) | collective-permute-done | bytes 786464 | tf_op jit(solution)/shard_map/ppermute | solution.py:908
  44.8 9.0 %collective-permute-done.5.p3_ref = bf16[192,1024]{1,0:T(8,128)(2,1)S(1)} collective-permute-done((bf16[192,1024]{1,0:T(8,128)(2,1)S(1)}, bf16[192,1024]{1,0:T(8,128)(2,1)S(1)}, u32[]{:S(2)}, u32[]{:S(2)}) %collective-permute-start.5) | collective-permute-done | bytes 393248 | tf_op jit(solution)/shard_map/ppermute | solution.py:908
  76.9 7.0 %collective-permute-done.8.x1_ref.refs_7_ = bf16[384,1024]{1,0:T(8,128)(2,1)} collective-permute-done((bf16[384,1024]{1,0:T(8,128)(2,1)}, bf16[384,1024]{1,0:T(8,128)(2,1)}, u32[]{:S(2)}, u32[]{:S(2)}) %collective-permute-start.8) | collective-permute-done | bytes 786464 | tf_op jit(solution)/shard_map/ppermute | solution.py:908
  89.6 21.6 %attend.1 = (bf16[1536,256]{1,0:T(8,128)(2,1)S(1)}, f32[12,4,128]{2,1,0:T(4,128)S(1)}, bf16[1536,768]{1,0:T(8,128)(2,1)S(1)}) custom-call(s32[12]{0:T(128)S(1)} %add.169.place_ref, s32[12]{0:T(128)S(1)} %get-tuple-element.406.start_ref, s32[12]{0:T(128)S(1)} %get-tuple-element.407.count_ref, s32[144]{0:T(256)S(1)} %copy-done.183, ...), custom_call_target="tpu_custom_call" | custom-call | flops 1024 | bytes 8400000 | tf_op jit(solution)/shard_map/attend/pallas_call | solution.py:477
  116.2 9.7 %collective-permute-done.13.p3_ref = bf16[192,1024]{1,0:T(8,128)(2,1)S(1)} collective-permute-done((bf16[192,1024]{1,0:T(8,128)(2,1)S(1)}, bf16[192,1024]{1,0:T(8,128)(2,1)S(1)}, u32[]{:S(2)}, u32[]{:S(2)}) %collective-permute-start.13) | collective-permute-done | bytes 393248 | tf_op jit(solution)/shard_map/ppermute | solution.py:908
  127.2 6.3 %collective-permute-done.15.refs_3_ = bf16[192,1024]{1,0:T(8,128)(2,1)S(1)} collective-permute-done((bf16[192,1024]{1,0:T(8,128)(2,1)S(1)}, bf16[192,1024]{1,0:T(8,128)(2,1)S(1)}, u32[]{:S(2)}, u32[]{:S(2)}) %collective-permute-start.15) | collective-permute-done | bytes 393248 | tf_op jit(solution)/shard_map/ppermute | solution.py:908
  138.2 16.7 %collective-permute-done.16.x1_ref.refs_7_ = bf16[384,1024]{1,0:T(8,128)(2,1)S(1)} collective-permute-done((bf16[384,1024]{1,0:T(8,128)(2,1)S(1)}, bf16[384,1024]{1,0:T(8,128)(2,1)S(1)}, u32[]{:S(2)}, u32[]{:S(2)}) %collective-permute-start.16) | collective-permute-done | bytes 786464 | tf_op jit(solution)/shard_map/ppermute | solution.py:908
  158.5 6.2 %conv_forward.1 = (bf16[1536,256]{1,0:T(8,128)(2,1)S(1)}, f32[1536,256]{1,0:T(8,128)S(1)}, f32[1536,256]{1,0:T(8,128)S(1)}, f32[1536,512]{1,0:T(8,128)S(1)}) custom-call(s32[4]{0:T(128)S(1)} %get-tuple-element.418.order_ref, s32[12]{0:T(128)S(1)} %get-tuple-element.401.low_ref, s32[12]{0:T(128)S(1)} %get-tuple-element.400.high_ref, ...), custom_call_target="tpu_custom_call" | custom-call | flops 1024 | bytes 3850000 | tf_op jit(solution)/shard_map/conv_forward/pallas_call | solution.py:714
  172.4 9.7 %collective-permute-done.21.p3_ref = bf16[192,1024]{1,0:T(8,128)(2,1)S(1)} collective-permute-done((bf16[192,1024]{1,0:T(8,128)(2,1)S(1)}, bf16[192,1024]{1,0:T(8,128)(2,1)S(1)}, u32[]{:S(2)}, u32[]{:S(2)}) %collective-permute-start.21) | collective-permute-done | bytes 393248 | tf_op jit(solution)/shard_map/ppermute | solution.py:908
  183.4 6.3 %collective-permute-done.23.refs_3_ = bf16[192,1024]{1,0:T(8,128)(2,1)S(1)} collective-permute-done((bf16[192,1024]{1,0:T(8,128)(2,1)S(1)}, bf16[192,1024]{1,0:T(8,128)(2,1)S(1)}, u32[]{:S(2)}, u32[]{:S(2)}) %collective-permute-start.23) | collective-permute-done | bytes 393248 | tf_op jit(solution)/shard_map/ppermute | solution.py:908
  198.1 12.9 %collective-permute-done.26.x1_ref.refs_11_.refs_13_ = bf16[384,1024]{1,0:T(8,128)(2,1)S(1)} collective-permute-done((bf16[384,1024]{1,0:T(8,128)(2,1)S(1)}, bf16[384,1024]{1,0:T(8,128)(2,1)S(1)}, u32[]{:S(2)}, u32[]{:S(2)}) %collective-permute-start.26) | collective-permute-done | bytes 786464 | tf_op jit(solution)/shard_map/ppermute | solution.py:908
  221.2 8.9 %collective-permute-done.29.p3_ref = bf16[192,1024]{1,0:T(8,128)(2,1)S(1)} collective-permute-done((bf16[192,1024]{1,0:T(8,128)(2,1)S(1)}, bf16[192,1024]{1,0:T(8,128)(2,1)S(1)}, u32[]{:S(2)}, u32[]{:S(2)}) %collective-permute-start.29) | collective-permute-done | bytes 393248 | tf_op jit(solution)/shard_map/ppermute | solution.py:908
  242.3 6.4 %ff_back_rows.6 = (bf16[768,1024]{1,0:T(8,128)(2,1)S(1)}, bf16[384,1024]{1,0:T(8,128)(2,1)S(1)}, bf16[384,1024]{1,0:T(8,128)(2,1)S(1)}) custom-call(bf16[384,1024]{1,0:T(8,128)(2,1)S(1)} %get-tuple-element.231.g1_ref.refs_0_, bf16[384,1024]{1,0:T(8,128)(2,1)S(1)} %collective-permute-done.32.g2_ref.refs_1_, bf16[768,1024]{1,0:T(8,128)(2,1)S(1)} %get-tuple-element.232.a_ref, ...), custom_call_target="tpu_custom_call" | custom-call | flops 1024 | bytes 1400000 | tf_op jit(solution)/shard_map/ff_back_rows/pallas_call | solution.py:310
  248.8 11.2 %collective-permute-done.34.g1_ref.refs_2_.refs_4_ = bf16[384,1024]{1,0:T(8,128)(2,1)S(1)} collective-permute-done((bf16[384,1024]{1,0:T(8,128)(2,1)S(1)}, bf16[384,1024]{1,0:T(8,128)(2,1)S(1)}, u32[]{:S(2)}, u32[]{:S(2)}) %collective-permute-start.34) | collective-permute-done | bytes 786464 | tf_op jit(solution)/shard_map/ppermute | solution.py:908
  273.5 7.6 %weight_grads.5 = bf16[1024,2048]{1,0:T(8,128)(2,1)S(1)} custom-call(bf16[384,1024]{1,0:T(8,128)(2,1)S(1)} %get-tuple-element.231.g1_ref.refs_0_, bf16[384,1024]{1,0:T(8,128)(2,1)S(1)} %collective-permute-done.32.g2_ref.refs_1_, bf16[384,1024]{1,0:T(8,128)(2,1)S(1)} %collective-permute-done.34.g1_ref.refs_2_.refs_4_, ...), custom_call_target="tpu_custom_call" | custom-call | flops 1024 | bytes 1750000 | tf_op jit(solution)/shard_map/weight_grads/pallas_call | solution.py:370
  302.8 17.0 %collective-permute-done.40.x1_ref.refs_2_ = bf16[384,1024]{1,0:T(8,128)(2,1)S(1)} collective-permute-done((bf16[384,1024]{1,0:T(8,128)(2,1)S(1)}, bf16[384,1024]{1,0:T(8,128)(2,1)S(1)}, u32[]{:S(2)}, u32[]{:S(2)}) %collective-permute-start.40) | collective-permute-done | bytes 786464 | tf_op jit(solution)/shard_map/ppermute | solution.py:908
  322.8 7.0 %conv_backward.1 = (bf16[1536,512]{1,0:T(8,128)(2,1)S(1)}, f32[2,1568,128]{2,1,0:T(8,128)S(1)}) custom-call(s32[4]{0:T(128)S(1)} %copy-done.186, s32[12]{0:T(128)S(1)} %copy-done.176, s32[12]{0:T(128)S(1)} %get-tuple-element.400.high_ref, f32[768,256]{1,0:T(8,128)S(1)} %project.12.refs_0_, f32[768,256]{1,0:T(8,128)S(1)} %project.13.refs_1_, ...), custom_call_target="tpu_custom_call" | custom-call | flops 1024 | bytes 3150000 | tf_op jit(solution)/shard_map/conv_backward/pallas_call | solution.py:819
  366.6 12.8 %collective-permute-done.48.x1_ref.refs_2_ = bf16[384,1024]{1,0:T(8,128)(2,1)S(1)} collective-permute-done((bf16[384,1024]{1,0:T(8,128)(2,1)S(1)}, bf16[384,1024]{1,0:T(8,128)(2,1)S(1)}, u32[]{:S(2)}, u32[]{:S(2)}) %collective-permute-start.48) | collective-permute-done | bytes 786464 | tf_op jit(solution)/shard_map/ppermute | solution.py:908
  392.1 38.4 %attend_back.1 = (bf16[1536,768]{1,0:T(8,128)(2,1)S(1)}, f32[4,9,256]{2,1,0:T(8,128)S(1)}) custom-call(s32[12]{0:T(128)S(1)} %copy-done.178, s32[12]{0:T(128)S(1)} %copy-done.180, s32[12]{0:T(128)S(1)} %copy-done.182, s32[144]{0:T(256)S(1)} %copy-done.184, bf16[768,256]{1,0:T(8,128)(2,1)S(1)} %project.14.refs_0_, bf16[768,256]{1,0:T(8,128)(2,1)S(1)} %copy-done.100, ...), custom_call_target="tpu_custom_call" | custom-call | flops 1024 | bytes 15050000 | tf_op jit(solution)/shard_map/attend_back/pallas_call | solution.py:615
  470.1 7.3 %ff_back_rows.9 = (bf16[768,1024]{1,0:T(8,128)(2,1)S(1)}, bf16[384,1024]{1,0:T(8,128)(2,1)S(1)}, bf16[384,1024]{1,0:T(8,128)(2,1)}) custom-call(bf16[384,1024]{1,0:T(8,128)(2,1)S(1)} %get-tuple-element.293.g1_ref.refs_0_, bf16[384,1024]{1,0:T(8,128)(2,1)S(1)} %collective-permute-done.56.g2_ref.refs_1_, bf16[768,1024]{1,0:T(8,128)(2,1)S(1)} %copy-done.104, ...), custom_call_target="tpu_custom_call" | custom-call | flops 1024 | bytes 1400000 | tf_op jit(solution)/shard_map/ff_back_rows/pallas_call | solution.py:310
  478.6 7.7 %collective-permute-done.58.g1_ref.refs_2_.refs_4_ = bf16[384,1024]{1,0:T(8,128)(2,1)S(1)} collective-permute-done((bf16[384,1024]{1,0:T(8,128)(2,1)S(1)}, bf16[384,1024]{1,0:T(8,128)(2,1)S(1)}, u32[]{:S(2)}, u32[]{:S(2)}) %collective-permute-start.58) | collective-permute-done | bytes 786464 | tf_op jit(solution)/shard_map/ppermute | solution.py:908
  533.2 13.5 %collective-permute-done.62 = bf16[2,2,128,1024]{3,2,0,1:T(8,128)(2,1)} collective-permute-done((bf16[2,2,128,1024]{3,2,0,1:T(8,128)(2,1)}, bf16[2,2,128,1024]{3,2,0,1:T(8,128)(2,1)}, u32[]{:S(2)}, u32[]{:S(2)}) %collective-permute-start.62) | collective-permute-done | bytes 1048608 | tf_op jit(solution)/shard_map/ppermute | solution.py:908
  565.4 10.2 %collective-permute-done.68 = f32[14084]{0:T(1024)S(1)} collective-permute-done((f32[14084]{0:T(1024)S(1)}, f32[14084]{0:T(1024)S(1)}, u32[]{:S(2)}, u32[]{:S(2)}) %collective-permute-start.68) | collective-permute-done | bytes 56368 | tf_op jit(solution)/shard_map/ppermute | solution.py:908
  586.6 7.4 %reduce-scatter.11.cloned.1.call-done = bf16[128,1024]{1,0:T(8,128)(2,1)} async-done(((bf16[1024,1024]{1,0:T(8,128)(2,1)}), bf16[128,1024]{1,0:T(8,128)(2,1)}) %reduce-scatter.11.cloned.1.call-update) | async-done | bytes 262160 | tf_op jit(solution)/shard_map/reduce_scatter | solution.py:960
  (710 shorter events, 317.7 us)
Async XLA Ops:
  7.2 376.7 %reduce-scatter.5.cloned.1.call-start = ((), (), s32[]{:S(2)}) async-start(), calls=%async_computation.4 | async-start | bytes 4718592 | tf_op jit(solution)/shard_map/reduce_scatter | solution.py:960
  12.1 20.7 %collective-permute-start.2 = (bf16[384,1024]{1,0:T(8,128)(2,1)S(1)}, bf16[384,1024]{1,0:T(8,128)(2,1)S(1)}, u32[]{:S(2)}, u32[]{:S(2)}) collective-permute-start(bf16[384,1024]{1,0:T(8,128)(2,1)S(1)} %enter.1.x1_ref.refs_0_), channel_id=1, source_target_pairs={{0,2},{1,3},{2,0},{3,1},{4,6},{5,7},{6,4},{7,5},{8,10},{9,11},{10,... | collective-permute-start | bytes 2359304 | tf_op jit(solution)/shard_map/ppermute | solution.py:908
  43.7 17.9 %collective-permute-start.7 = (bf16[192,1024]{1,0:T(8,128)(2,1)S(1)}, bf16[192,1024]{1,0:T(8,128)(2,1)S(1)}, u32[]{:S(2)}, u32[]{:S(2)}) collective-permute-start(bf16[192,1024]{1,0:T(8,128)(2,1)S(1)} %add_convert_fusion.14), channel_id=1, source_target_pairs={{0,2},{1,3},{2,0},{3,1},{4,6},{5,7},{6,4},{7,5},{8,10},{9,11},{10,... | collective-permute-start | bytes 1179656 | tf_op jit(solution)/shard_map/ppermute | solution.py:908
  64.6 19.3 %collective-permute-start.8 = (bf16[384,1024]{1,0:T(8,128)(2,1)}, bf16[384,1024]{1,0:T(8,128)(2,1)}, u32[]{:S(2)}, u32[]{:S(2)}) collective-permute-start(bf16[384,1024]{1,0:T(8,128)(2,1)} %get-tuple-element.191.x1_ref.refs_5_), channel_id=1, source_target_pairs={{0,2},{1,3},{2,0},{3,1},{4,6},{5,7},{6,4},{7,5},{8,10},{9,11},{10,... | collective-permute-start | bytes 2359304 | tf_op jit(solution)/shard_map/ppermute | solution.py:908
  113.9 12.0 %collective-permute-start.13 = (bf16[192,1024]{1,0:T(8,128)(2,1)S(1)}, bf16[192,1024]{1,0:T(8,128)(2,1)S(1)}, u32[]{:S(2)}, u32[]{:S(2)}) collective-permute-start(bf16[192,1024]{1,0:T(8,128)(2,1)S(1)} %add_convert_fusion.13), channel_id=1, source_target_pairs={{0,2},{1,3},{2,0},{3,1},{4,6},{5,7},{6,4},{7,5},{8,10},{9,11},{10,... | collective-permute-start | bytes 1179656 | tf_op jit(solution)/shard_map/ppermute | solution.py:908
  115.8 17.7 %collective-permute-start.15 = (bf16[192,1024]{1,0:T(8,128)(2,1)S(1)}, bf16[192,1024]{1,0:T(8,128)(2,1)S(1)}, u32[]{:S(2)}, u32[]{:S(2)}) collective-permute-start(bf16[192,1024]{1,0:T(8,128)(2,1)S(1)} %add_convert_fusion.12), channel_id=1, source_target_pairs={{0,2},{1,3},{2,0},{3,1},{4,6},{5,7},{6,4},{7,5},{8,10},{9,11},{10,... | collective-permute-start | bytes 1179656 | tf_op jit(solution)/shard_map/ppermute | solution.py:908
  134.9 20.0 %collective-permute-start.16 = (bf16[384,1024]{1,0:T(8,128)(2,1)S(1)}, bf16[384,1024]{1,0:T(8,128)(2,1)S(1)}, u32[]{:S(2)}, u32[]{:S(2)}) collective-permute-start(bf16[384,1024]{1,0:T(8,128)(2,1)S(1)} %get-tuple-element.204.x1_ref.refs_5_), channel_id=1, source_target_pairs={{0,2},{1,3},{2,0},{3,1},{4,6},{5,7},{6,4},{7,5},{8,10},{9,11},{10,... | collective-permute-start | bytes 2359304 | tf_op jit(solution)/shard_map/ppermute | solution.py:908
  172.0 17.7 %collective-permute-start.23 = (bf16[192,1024]{1,0:T(8,128)(2,1)S(1)}, bf16[192,1024]{1,0:T(8,128)(2,1)S(1)}, u32[]{:S(2)}, u32[]{:S(2)}) collective-permute-start(bf16[192,1024]{1,0:T(8,128)(2,1)S(1)} %add_convert_fusion.10), channel_id=1, source_target_pairs={{0,2},{1,3},{2,0},{3,1},{4,6},{5,7},{6,4},{7,5},{8,10},{9,11},{10,... | collective-permute-start | bytes 1179656 | tf_op jit(solution)/shard_map/ppermute | solution.py:908
  191.1 20.0 %collective-permute-start.26 = (bf16[384,1024]{1,0:T(8,128)(2,1)S(1)}, bf16[384,1024]{1,0:T(8,128)(2,1)S(1)}, u32[]{:S(2)}, u32[]{:S(2)}) collective-permute-start(bf16[384,1024]{1,0:T(8,128)(2,1)S(1)} %get-tuple-element.217.x1_ref.refs_9_), channel_id=1, source_target_pairs={{0,2},{1,3},{2,0},{3,1},{4,6},{5,7},{6,4},{7,5},{8,10},{9,11},{10,... | collective-permute-start | bytes 2359304 | tf_op jit(solution)/shard_map/ppermute | solution.py:908
  220.1 17.9 %collective-permute-start.31 = (bf16[192,1024]{1,0:T(8,128)(2,1)S(1)}, bf16[192,1024]{1,0:T(8,128)(2,1)S(1)}, u32[]{:S(2)}, u32[]{:S(2)}) collective-permute-start(bf16[192,1024]{1,0:T(8,128)(2,1)S(1)} %add_convert_fusion.8), channel_id=1, source_target_pairs={{0,2},{1,3},{2,0},{3,1},{4,6},{5,7},{6,4},{7,5},{8,10},{9,11},{10,... | collective-permute-start | bytes 1179656 | tf_op jit(solution)/shard_map/ppermute | solution.py:908
  240.0 20.0 %collective-permute-start.34 = (bf16[384,1024]{1,0:T(8,128)(2,1)S(1)}, bf16[384,1024]{1,0:T(8,128)(2,1)S(1)}, u32[]{:S(2)}, u32[]{:S(2)}) collective-permute-start(bf16[384,1024]{1,0:T(8,128)(2,1)S(1)} %get-tuple-element.231.g1_ref.refs_0_), channel_id=1, source_target_pairs={{0,2},{1,3},{2,0},{3,1},{4,6},{5,7},{6,4},{7,5},{8,10},{9,11},{10,... | collective-permute-start | bytes 2359304 | tf_op jit(solution)/shard_map/ppermute | solution.py:908
  268.0 15.1 %collective-permute-start.39 = (bf16[192,1024]{1,0:T(8,128)(2,1)}, bf16[192,1024]{1,0:T(8,128)(2,1)}, u32[]{:S(2)}, u32[]{:S(2)}) collective-permute-start(bf16[192,1024]{1,0:T(8,128)(2,1)} %add_convert_fusion.6), channel_id=1, source_target_pairs={{0,2},{1,3},{2,0},{3,1},{4,6},{5,7},{6,4},{7,5},{8,10},{9,11},{10,... | collective-permute-start | bytes 1179656 | tf_op jit(solution)/shard_map/ppermute | solution.py:908
  283.1 170.1 %reduce-scatter.7.cloned.1.call-start = ((), (), s32[]{:S(2)}) async-start(), calls=%async_computation.5 | async-start | bytes 1769472 | tf_op jit(solution)/shard_map/reduce_scatter | solution.py:960
  299.8 20.0 %collective-permute-start.40 = (bf16[384,1024]{1,0:T(8,128)(2,1)S(1)}, bf16[384,1024]{1,0:T(8,128)(2,1)S(1)}, u32[]{:S(2)}, u32[]{:S(2)}) collective-permute-start(bf16[384,1024]{1,0:T(8,128)(2,1)S(1)} %get-tuple-element.253.x1_ref.refs_0_), channel_id=1, source_target_pairs={{0,2},{1,3},{2,0},{3,1},{4,6},{5,7},{6,4},{7,5},{8,10},{9,11},{10,... | collective-permute-start | bytes 2359304 | tf_op jit(solution)/shard_map/ppermute | solution.py:908
  345.1 169.4 %reduce-scatter.9.cloned.1.call-start = ((), (), s32[]{:S(2)}) async-start(), calls=%async_computation.6 | async-start | bytes 2359296 | tf_op jit(solution)/shard_map/reduce_scatter | solution.py:960
  359.4 20.0 %collective-permute-start.48 = (bf16[384,1024]{1,0:T(8,128)(2,1)S(1)}, bf16[384,1024]{1,0:T(8,128)(2,1)S(1)}, u32[]{:S(2)}, u32[]{:S(2)}) collective-permute-start(bf16[384,1024]{1,0:T(8,128)(2,1)S(1)} %get-tuple-element.269.x1_ref.refs_0_), channel_id=1, source_target_pairs={{0,2},{1,3},{2,0},{3,1},{4,6},{5,7},{6,4},{7,5},{8,10},{9,11},{10,... | collective-permute-start | bytes 2359304 | tf_op jit(solution)/shard_map/ppermute | solution.py:908
  445.8 148.1 %reduce-scatter.11.cloned.1.call-start = ((), (), s32[]{:S(2)}) async-start(), calls=%async_computation.7 | async-start | bytes 2359296 | tf_op jit(solution)/shard_map/reduce_scatter | solution.py:960
  466.4 20.0 %collective-permute-start.58 = (bf16[384,1024]{1,0:T(8,128)(2,1)S(1)}, bf16[384,1024]{1,0:T(8,128)(2,1)S(1)}, u32[]{:S(2)}, u32[]{:S(2)}) collective-permute-start(bf16[384,1024]{1,0:T(8,128)(2,1)S(1)} %get-tuple-element.293.g1_ref.refs_0_), channel_id=1, source_target_pairs={{0,2},{1,3},{2,0},{3,1},{4,6},{5,7},{6,4},{7,5},{8,10},{9,11},{10,... | collective-permute-start | bytes 2359304 | tf_op jit(solution)/shard_map/ppermute | solution.py:908
  495.2 18.4 %collective-permute-start.61 = (bf16[192,1024]{1,0:T(8,128)(2,1)}, bf16[192,1024]{1,0:T(8,128)(2,1)}, u32[]{:S(2)}, u32[]{:S(2)}) collective-permute-start(bf16[192,1024]{1,0:T(8,128)(2,1)} %add_convert_fusion.1), channel_id=1, source_target_pairs={{0,2},{1,3},{2,0},{3,1},{4,6},{5,7},{6,4},{7,5},{8,10},{9,11},{10,... | collective-permute-start | bytes 1179656 | tf_op jit(solution)/shard_map/ppermute | solution.py:908
  516.8 29.9 %collective-permute-start.62 = (bf16[2,2,128,1024]{3,2,0,1:T(8,128)(2,1)}, bf16[2,2,128,1024]{3,2,0,1:T(8,128)(2,1)}, u32[]{:S(2)}, u32[]{:S(2)}) collective-permute-start(bf16[2,2,128,1024]{3,2,0,1:T(8,128)(2,1)} %bitcast.48), channel_id=1, source_target_pairs={{0,4},{4,0},{8,12},{12,8},{16,20},{20,16},{24,28},{28,24},{1,5},{5... | collective-permute-start | bytes 3145736 | tf_op jit(solution)/shard_map/ppermute | solution.py:908
  525.6 23.8 %collective-permute-start.64 = (bf16[192,1024]{1,0:T(8,128)(2,1)S(1)}, bf16[192,1024]{1,0:T(8,128)(2,1)S(1)}, u32[]{:S(2)}, u32[]{:S(2)}) collective-permute-start(bf16[192,1024]{1,0:T(8,128)(2,1)S(1)} %add_convert_fusion), channel_id=1, source_target_pairs={{0,2},{1,3},{2,0},{3,1},{4,6},{5,7},{6,4},{7,5},{8,10},{9,11},{10,... | collective-permute-start | bytes 1179656 | tf_op jit(solution)/shard_map/ppermute | solution.py:908
  560.4 19.3 %collective-permute-start.70 = (bf16[2,128,1024]{2,1,0:T(8,128)(2,1)}, bf16[2,128,1024]{2,1,0:T(8,128)(2,1)}, u32[]{:S(2)}, u32[]{:S(2)}) collective-permute-start(bf16[2,128,1024]{2,1,0:T(8,128)(2,1)} %dynamic-slice_bitcast_fusion), channel_id=1, source_target_pairs={{0,8},{4,12},{8,0},{12,4},{16,24},{20,28},{24,16},{28,20},{1,9},{5... | collective-permute-start | bytes 1572872 | tf_op jit(solution)/shard_map/ppermute | solution.py:908
  562.8 12.8 %collective-permute-start.68 = (f32[14084]{0:T(1024)S(1)}, f32[14084]{0:T(1024)S(1)}, u32[]{:S(2)}, u32[]{:S(2)}) collective-permute-start(f32[14084]{0:T(1024)S(1)} %add.200), channel_id=1, source_target_pairs={{0,16},{4,20},{8,24},{12,28},{16,0},{20,4},{24,8},{28,12},{1,17},{... | collective-permute-start | bytes 169016 | tf_op jit(solution)/shard_map/ppermute | solution.py:908
  581.1 16.0 %collective-permute-start.71 = (bf16[128,1024]{1,0:T(8,128)(2,1)S(1)}, bf16[128,1024]{1,0:T(8,128)(2,1)S(1)}, u32[]{:S(2)}, u32[]{:S(2)}) collective-permute-start(bf16[128,1024]{1,0:T(8,128)(2,1)S(1)} %dynamic-slice_bitcast_fusion.1), channel_id=1, source_target_pairs={{0,16},{4,20},{8,24},{12,28},{16,0},{20,4},{24,8},{28,12},{1,17},{... | collective-permute-start | bytes 786440 | tf_op jit(solution)/shard_map/ppermute | solution.py:908
  (260 other events, 1723.8 us)
Sparse Core Ops, SparseCore 0:
  283.3 88.2 reduce-scatter.4
  375.4 64.6 reduce-scatter.6
  445.9 68.5 reduce-scatter.8
  517.9 76.0 reduce-scatter.10

commit v6 on v5

--- a/solution.py
+++ b/solution.py
@@ -660,8 +660,8 @@
     for block in range(blocks):
         here = pl.ds(pl.multiple_of(order_ref[block] * size, TILE), size)
         for lane in range(lanes):
-            value = glu_ref[here, lane * TILE : (lane + 1) * TILE]
-            gate = glu_ref[here, channels + lane * TILE : channels + (lane + 1) * TILE]
+            value = glu_ref[here, lane * TILE : (lane + 1) * TILE].astype(F32)
+            gate = glu_ref[here, channels + lane * TILE : channels + (lane + 1) * TILE].astype(F32)
             first = EDGE + block * frames
             pad_ref[lane, first : first + size, :] = value * sigmoid(gate)
     rest = EDGE + (blocks - 1) * frames + size
@@ -720,7 +720,7 @@
             shaped((total, channels), BF16),
             shaped((rows, channels), F32),
             shaped((rows, channels), F32),
-            shaped((total, 2 * channels), F32),
+            shaped((total, 2 * channels), BF16),
         ],
         grid_spec=pltpu.PrefetchScalarGridSpec(
             num_scalar_prefetch=3,
@@ -761,7 +761,7 @@
             first = EDGE + block * frames
             slope_ref[lane, first : first + size, :] = grad_ref[
                 here, lane * TILE : (lane + 1) * TILE
-            ]
+            ].astype(F32)
     rest = EDGE + (blocks - 1) * frames + size
     for lane in range(lanes):
         slope_ref[lane, :EDGE, :] = jnp.zeros((EDGE, TILE), F32)
@@ -804,8 +804,8 @@
             follow = slice(channels + lane * TILE, channels + (lane + 1) * TILE)
             rows_in = dgate_ref[lane, block * frames : block * frames + size, :]
             rows_in = jnp.where(valid, rows_in, 0.0)
-            value = glu_ref[here, lead]
-            gate = sigmoid(glu_ref[here, follow])
+            value = glu_ref[here, lead].astype(F32)
+            gate = sigmoid(glu_ref[here, follow].astype(F32))
             dglu_ref[here, lead] = (rows_in * gate).astype(BF16)
             dglu_ref[here, follow] = (rows_in * value * gate * (1.0 - gate)).astype(BF16)
 
@@ -833,7 +833,7 @@
             ],
             out_specs=[fixed(*glu.shape), fixed(*slope)],
             scratch_shapes=[
-                pltpu.VMEM((glu.shape[0], channels), F32),
+                pltpu.VMEM((glu.shape[0], channels), BF16),
                 pltpu.VMEM((TILE + 2 * EDGE, TILE), F32),
                 pltpu.VMEM((lanes, rows + EDGE, TILE), F32),
             ],
@@ -1088,7 +1088,7 @@
     out, lse, qkv = attend(spread(h_two, w_qkv, 0, BF16), bias, plan)
     h_three, two = join(one, collect(out, w_output, 0), gain_three, 1.0)
     h_three = gather(h_three)
-    act, gated, mixed, glu = conv_forward(spread(h_three, glu_matrix, 0, F32), kernel, plan)
+    act, gated, mixed, glu = conv_forward(spread(h_three, glu_matrix, 0, BF16), kernel, plan)
     h_four, three = join(two, collect(act, w_back, 0), gain_four, 1.0)
     h_four = gather(h_four)
     parts, state_four = feed_forward(h_four, second_in, second_out)
@@ -1104,7 +1104,7 @@
     grads, e3, sums = join_back(e4, three, parts, gain_four, 1.0)
     grad_four = total(sums)
     grads = gather(grads)
-    dglu, slope = conv_backward(spread(grads, w_back, 1, F32), glu, kernel, plan, mixed)
+    dglu, slope = conv_backward(spread(grads, w_back, 1, BF16), glu, kernel, plan, mixed)
     parts, grad_w = delayed(
         collect(dglu, glu_matrix, 1), weight_grads([(grads, [act]), (h_three, [dglu])])
     )

time: 617 us -> 617 us (level)
  waiting for transfers between devices: 234 us -> 244 us
  local copies, waits for them, and re-layouts: 85.5 us -> 76.4 us
    unnamed x428 -> x412, local copies, waits for them, and re-layouts: 73.6 us -> 63.5 us
    reduce_scatter x4, waiting for transfers between devices: 8.35 us -> 16.3 us  [settle(): return lax.psum_scatter(grads, 'dp', scatter_dimension=0, tiled=True)]
  transfers between devices with their start and end apart: 76 -> 76, of which waited for: 49 -> 48; matrix products, arithmetic and copies ran while one was open for 6% -> 6% of each run, Pallas kernels for 26% -> 26%
where the time goes in v6:
time: 617 us; the launch traced here: 607 us
  waiting for transfers between devices  244 us (40%)
  Pallas kernels  200 us (32%)
  local copies, waits for them, and re-layouts  76.4 us (12%)
  starting transfers between devices  52.3 us (8%)
  between operations  16.8 us (3%)
  other arithmetic  15 us (2%)
    ppermute x72, waiting for transfers between devices, swap(): return lax.ppermute(values, axis, [(i, i ^ bit) for i in range(count)])  227 us
    unnamed x412, local copies, waits for them, and re-layouts  63.5 us
    ppermute x72, starting transfers between devices, swap(): return lax.ppermute(values, axis, [(i, i ^ bit) for i in range(count)])  52.1 us
    pallas_call x1, Pallas kernels, attend_back(): call(functools.partial(attend_back_body, tiles=tiles, pairs=pairs, scale=...  37.7 us
    pallas_call x16, Pallas kernels, by_chunks(): call(run, name, shapes, grid=(1,), in_specs=specs, out_specs=outs, input_...  29.4 us
    pallas_call x5, Pallas kernels, weight_grads(): call(body, 'weight_grads', shaped((height, column), BF16), grid=(1,), in_...  26 us
    pallas_call x6, Pallas kernels, ff_back_rows(): call(body, 'ff_back_rows', [shaped(a.shape, BF16)] + [shaped((rows, width...  25.9 us
    pallas_call x1, Pallas kernels, attend(): call(functools.partial(attend_body, tiles=tiles, pairs=pairs, scale=plan[...  21 us
  transfers between devices with their start and end apart: 76, of which 48 were waited for; matrix products, arithmetic and copies ran while one was open for 6% of the time, Pallas kernels for 26%

profile of v6, /device:TPU:0, one launch (start us, length us, event | category | flops | bytes accessed | tf_op | source)
XLA Modules:
  0.0 606.7 jit_solution(4788776103942633668)
XLA Ops:
  23.1 9.8 %collective-permute-done.2.x1_ref.refs_2_.refs_4_ = bf16[384,1024]{1,0:T(8,128)(2,1)S(1)} collective-permute-done((bf16[384,1024]{1,0:T(8,128)(2,1)S(1)}, bf16[384,1024]{1,0:T(8,128)(2,1)S(1)}, u32[]{:S(2)}, u32[]{:S(2)}) %collective-permute-start.2) | collective-permute-done | bytes 786464 | tf_op jit(solution)/shard_map/ppermute | solution.py:908
  44.8 8.9 %collective-permute-done.5.p3_ref = bf16[192,1024]{1,0:T(8,128)(2,1)S(1)} collective-permute-done((bf16[192,1024]{1,0:T(8,128)(2,1)S(1)}, bf16[192,1024]{1,0:T(8,128)(2,1)S(1)}, u32[]{:S(2)}, u32[]{:S(2)}) %collective-permute-start.5) | collective-permute-done | bytes 393248 | tf_op jit(solution)/shard_map/ppermute | solution.py:908
  77.0 6.0 collective-permute-done.8.x1_ref.refs_7_
  87.0 21.0 %attend.1 = (bf16[1536,256]{1,0:T(8,128)(2,1)S(1)}, f32[12,4,128]{2,1,0:T(4,128)S(1)}, bf16[1536,768]{1,0:T(8,128)(2,1)S(1)}) custom-call(s32[12]{0:T(128)S(1)} %add.169.place_ref, s32[12]{0:T(128)S(1)} %get-tuple-element.406.start_ref, s32[12]{0:T(128)S(1)} %get-tuple-element.407.count_ref, s32[144]{0:T(256)S(1)} %copy-done.177, ...), custom_call_target="tpu_custom_call" | custom-call | flops 1024 | bytes 8400000 | tf_op jit(solution)/shard_map/attend/pallas_call | solution.py:477
  113.2 9.6 %collective-permute-done.13.p3_ref = bf16[192,1024]{1,0:T(8,128)(2,1)S(1)} collective-permute-done((bf16[192,1024]{1,0:T(8,128)(2,1)S(1)}, bf16[192,1024]{1,0:T(8,128)(2,1)S(1)}, u32[]{:S(2)}, u32[]{:S(2)}) %collective-permute-start.13) | collective-permute-done | bytes 393248 | tf_op jit(solution)/shard_map/ppermute | solution.py:908
  124.1 6.4 %collective-permute-done.15.refs_3_ = bf16[192,1024]{1,0:T(8,128)(2,1)S(1)} collective-permute-done((bf16[192,1024]{1,0:T(8,128)(2,1)S(1)}, bf16[192,1024]{1,0:T(8,128)(2,1)S(1)}, u32[]{:S(2)}, u32[]{:S(2)}) %collective-permute-start.15) | collective-permute-done | bytes 393248 | tf_op jit(solution)/shard_map/ppermute | solution.py:908
  135.2 16.7 %collective-permute-done.16.x1_ref.refs_7_ = bf16[384,1024]{1,0:T(8,128)(2,1)S(1)} collective-permute-done((bf16[384,1024]{1,0:T(8,128)(2,1)S(1)}, bf16[384,1024]{1,0:T(8,128)(2,1)S(1)}, u32[]{:S(2)}, u32[]{:S(2)}) %collective-permute-start.16) | collective-permute-done | bytes 786464 | tf_op jit(solution)/shard_map/ppermute | solution.py:908
  155.5 6.4 %conv_forward.1 = (bf16[1536,256]{1,0:T(8,128)(2,1)S(1)}, f32[1536,256]{1,0:T(8,128)S(1)}, f32[1536,256]{1,0:T(8,128)S(1)}, bf16[1536,512]{1,0:T(8,128)(2,1)S(1)}) custom-call(s32[4]{0:T(128)S(1)} %get-tuple-element.418.order_ref, s32[12]{0:T(128)S(1)} %get-tuple-element.401.low_ref, s32[12]{0:T(128)S(1)} %get-tuple-element.400.high_ref, ...), custom_call_target="tpu_custom_call" | custom-call | flops 1024 | bytes 3850000 | tf_op jit(solution)/shard_map/conv_forward/pallas_call | solution.py:714
  168.4 9.7 %collective-permute-done.21.p3_ref = bf16[192,1024]{1,0:T(8,128)(2,1)S(1)} collective-permute-done((bf16[192,1024]{1,0:T(8,128)(2,1)S(1)}, bf16[192,1024]{1,0:T(8,128)(2,1)S(1)}, u32[]{:S(2)}, u32[]{:S(2)}) %collective-permute-start.21) | collective-permute-done | bytes 393248 | tf_op jit(solution)/shard_map/ppermute | solution.py:908
  179.4 6.3 %collective-permute-done.23.refs_3_ = bf16[192,1024]{1,0:T(8,128)(2,1)S(1)} collective-permute-done((bf16[192,1024]{1,0:T(8,128)(2,1)S(1)}, bf16[192,1024]{1,0:T(8,128)(2,1)S(1)}, u32[]{:S(2)}, u32[]{:S(2)}) %collective-permute-start.23) | collective-permute-done | bytes 393248 | tf_op jit(solution)/shard_map/ppermute | solution.py:908
  194.1 12.9 %collective-permute-done.26.x1_ref.refs_11_.refs_13_ = bf16[384,1024]{1,0:T(8,128)(2,1)S(1)} collective-permute-done((bf16[384,1024]{1,0:T(8,128)(2,1)S(1)}, bf16[384,1024]{1,0:T(8,128)(2,1)S(1)}, u32[]{:S(2)}, u32[]{:S(2)}) %collective-permute-start.26) | collective-permute-done | bytes 786464 | tf_op jit(solution)/shard_map/ppermute | solution.py:908
  217.2 9.0 %collective-permute-done.29.p3_ref = bf16[192,1024]{1,0:T(8,128)(2,1)S(1)} collective-permute-done((bf16[192,1024]{1,0:T(8,128)(2,1)S(1)}, bf16[192,1024]{1,0:T(8,128)(2,1)S(1)}, u32[]{:S(2)}, u32[]{:S(2)}) %collective-permute-start.29) | collective-permute-done | bytes 393248 | tf_op jit(solution)/shard_map/ppermute | solution.py:908
  239.1 6.4 %ff_back_rows.6 = (bf16[768,1024]{1,0:T(8,128)(2,1)S(1)}, bf16[384,1024]{1,0:T(8,128)(2,1)S(1)}, bf16[384,1024]{1,0:T(8,128)(2,1)S(1)}) custom-call(bf16[384,1024]{1,0:T(8,128)(2,1)S(1)} %get-tuple-element.231.g1_ref.refs_0_, bf16[384,1024]{1,0:T(8,128)(2,1)S(1)} %collective-permute-done.32.g2_ref.refs_1_, bf16[768,1024]{1,0:T(8,128)(2,1)S(1)} %get-tuple-element.232.a_ref, ...), custom_call_target="tpu_custom_call" | custom-call | flops 1024 | bytes 1400000 | tf_op jit(solution)/shard_map/ff_back_rows/pallas_call | solution.py:310
  245.6 11.2 %collective-permute-done.34.g1_ref.refs_2_.refs_4_ = bf16[384,1024]{1,0:T(8,128)(2,1)S(1)} collective-permute-done((bf16[384,1024]{1,0:T(8,128)(2,1)S(1)}, bf16[384,1024]{1,0:T(8,128)(2,1)S(1)}, u32[]{:S(2)}, u32[]{:S(2)}) %collective-permute-start.34) | collective-permute-done | bytes 786464 | tf_op jit(solution)/shard_map/ppermute | solution.py:908
  270.3 7.6 %weight_grads.5 = bf16[1024,2048]{1,0:T(8,128)(2,1)S(1)} custom-call(bf16[384,1024]{1,0:T(8,128)(2,1)S(1)} %get-tuple-element.231.g1_ref.refs_0_, bf16[384,1024]{1,0:T(8,128)(2,1)S(1)} %collective-permute-done.32.g2_ref.refs_1_, bf16[384,1024]{1,0:T(8,128)(2,1)S(1)} %collective-permute-done.34.g1_ref.refs_2_.refs_4_, ...), custom_call_target="tpu_custom_call" | custom-call | flops 1024 | bytes 1750000 | tf_op jit(solution)/shard_map/weight_grads/pallas_call | solution.py:370
  298.9 17.0 %collective-permute-done.40.x1_ref.refs_2_ = bf16[384,1024]{1,0:T(8,128)(2,1)S(1)} collective-permute-done((bf16[384,1024]{1,0:T(8,128)(2,1)S(1)}, bf16[384,1024]{1,0:T(8,128)(2,1)S(1)}, u32[]{:S(2)}, u32[]{:S(2)}) %collective-permute-start.40) | collective-permute-done | bytes 786464 | tf_op jit(solution)/shard_map/ppermute | solution.py:908
  318.9 7.3 %conv_backward.1 = (bf16[1536,512]{1,0:T(8,128)(2,1)S(1)}, f32[2,1568,128]{2,1,0:T(8,128)S(1)}) custom-call(s32[4]{0:T(128)S(1)} %copy-done.180, s32[12]{0:T(128)S(1)} %copy-done.170, s32[12]{0:T(128)S(1)} %get-tuple-element.400.high_ref, bf16[768,256]{1,0:T(8,128)(2,1)S(1)} %project.12.refs_0_, bf16[768,256]{1,0:T(8,128)(2,1)S(1)} %project.13.refs_1_, ...), custom_call_target="tpu_custom_call" | custom-call | flops 1024 | bytes 3150000 | tf_op jit(solution)/shard_map/conv_backward/pallas_call | solution.py:819
  347.2 6.0 collective-permute-done.45.refs_4_
  363.2 12.6 %collective-permute-done.48.x1_ref.refs_2_ = bf16[384,1024]{1,0:T(8,128)(2,1)S(1)} collective-permute-done((bf16[384,1024]{1,0:T(8,128)(2,1)S(1)}, bf16[384,1024]{1,0:T(8,128)(2,1)S(1)}, u32[]{:S(2)}, u32[]{:S(2)}) %collective-permute-start.48) | collective-permute-done | bytes 786464 | tf_op jit(solution)/shard_map/ppermute | solution.py:908
  389.4 37.7 %attend_back.1 = (bf16[1536,768]{1,0:T(8,128)(2,1)S(1)}, f32[4,9,256]{2,1,0:T(8,128)S(1)}) custom-call(s32[12]{0:T(128)S(1)} %copy-done.172, s32[12]{0:T(128)S(1)} %copy-done.174, s32[12]{0:T(128)S(1)} %copy-done.176, s32[144]{0:T(256)S(1)} %copy-done.178, bf16[768,256]{1,0:T(8,128)(2,1)S(1)} %project.14.refs_0_, bf16[768,256]{1,0:T(8,128)(2,1)S(1)} %copy-done.92, ...), custom_call_target="tpu_custom_call" | custom-call | flops 1024 | bytes 15050000 | tf_op jit(solution)/shard_map/attend_back/pallas_call | solution.py:615
  466.9 7.3 %ff_back_rows.9 = (bf16[768,1024]{1,0:T(8,128)(2,1)S(1)}, bf16[384,1024]{1,0:T(8,128)(2,1)S(1)}, bf16[384,1024]{1,0:T(8,128)(2,1)}) custom-call(bf16[384,1024]{1,0:T(8,128)(2,1)S(1)} %get-tuple-element.293.g1_ref.refs_0_, bf16[384,1024]{1,0:T(8,128)(2,1)S(1)} %collective-permute-done.56.g2_ref.refs_1_, bf16[768,1024]{1,0:T(8,128)(2,1)S(1)} %copy-done.96, ...), custom_call_target="tpu_custom_call" | custom-call | flops 1024 | bytes 1400000 | tf_op jit(solution)/shard_map/ff_back_rows/pallas_call | solution.py:310
  474.3 10.3 %collective-permute-done.58.g1_ref.refs_2_.refs_4_ = bf16[384,1024]{1,0:T(8,128)(2,1)S(1)} collective-permute-done((bf16[384,1024]{1,0:T(8,128)(2,1)S(1)}, bf16[384,1024]{1,0:T(8,128)(2,1)S(1)}, u32[]{:S(2)}, u32[]{:S(2)}) %collective-permute-start.58) | collective-permute-done | bytes 786464 | tf_op jit(solution)/shard_map/ppermute | solution.py:908
  534.6 12.5 %collective-permute-done.62 = bf16[2,2,128,1024]{3,2,0,1:T(8,128)(2,1)} collective-permute-done((bf16[2,2,128,1024]{3,2,0,1:T(8,128)(2,1)}, bf16[2,2,128,1024]{3,2,0,1:T(8,128)(2,1)}, u32[]{:S(2)}, u32[]{:S(2)}) %collective-permute-start.62) | collective-permute-done | bytes 1048608 | tf_op jit(solution)/shard_map/ppermute | solution.py:908
  584.9 11.9 %reduce-scatter.11.cloned.1.call-done = bf16[128,1024]{1,0:T(8,128)(2,1)} async-done(((bf16[1024,1024]{1,0:T(8,128)(2,1)}), bf16[128,1024]{1,0:T(8,128)(2,1)}) %reduce-scatter.11.cloned.1.call-update) | async-done | bytes 262160 | tf_op jit(solution)/shard_map/reduce_scatter | solution.py:960
  (694 shorter events, 319.4 us)
Async XLA Ops:
  7.2 373.9 %reduce-scatter.5.cloned.1.call-start = ((), (), s32[]{:S(2)}) async-start(), calls=%async_computation.4 | async-start | bytes 4718592 | tf_op jit(solution)/shard_map/reduce_scatter | solution.py:960
  12.1 20.7 %collective-permute-start.2 = (bf16[384,1024]{1,0:T(8,128)(2,1)S(1)}, bf16[384,1024]{1,0:T(8,128)(2,1)S(1)}, u32[]{:S(2)}, u32[]{:S(2)}) collective-permute-start(bf16[384,1024]{1,0:T(8,128)(2,1)S(1)} %enter.1.x1_ref.refs_0_), channel_id=1, source_target_pairs={{0,2},{1,3},{2,0},{3,1},{4,6},{5,7},{6,4},{7,5},{8,10},{9,11},{10,... | collective-permute-start | bytes 2359304 | tf_op jit(solution)/shard_map/ppermute | solution.py:908
  43.7 17.9 %collective-permute-start.7 = (bf16[192,1024]{1,0:T(8,128)(2,1)S(1)}, bf16[192,1024]{1,0:T(8,128)(2,1)S(1)}, u32[]{:S(2)}, u32[]{:S(2)}) collective-permute-start(bf16[192,1024]{1,0:T(8,128)(2,1)S(1)} %add_convert_fusion.14), channel_id=1, source_target_pairs={{0,2},{1,3},{2,0},{3,1},{4,6},{5,7},{6,4},{7,5},{8,10},{9,11},{10,... | collective-permute-start | bytes 1179656 | tf_op jit(solution)/shard_map/ppermute | solution.py:908
  63.9 19.0 %collective-permute-start.8 = (bf16[384,1024]{1,0:T(8,128)(2,1)S(1)}, bf16[384,1024]{1,0:T(8,128)(2,1)S(1)}, u32[]{:S(2)}, u32[]{:S(2)}) collective-permute-start(bf16[384,1024]{1,0:T(8,128)(2,1)S(1)} %get-tuple-element.191.x1_ref.refs_5_), channel_id=1, source_target_pairs={{0,2},{1,3},{2,0},{3,1},{4,6},{5,7},{6,4},{7,5},{8,10},{9,11},{10,... | collective-permute-start | bytes 2359304 | tf_op jit(solution)/shard_map/ppermute | solution.py:908
  110.8 12.0 %collective-permute-start.13 = (bf16[192,1024]{1,0:T(8,128)(2,1)S(1)}, bf16[192,1024]{1,0:T(8,128)(2,1)S(1)}, u32[]{:S(2)}, u32[]{:S(2)}) collective-permute-start(bf16[192,1024]{1,0:T(8,128)(2,1)S(1)} %add_convert_fusion.13), channel_id=1, source_target_pairs={{0,2},{1,3},{2,0},{3,1},{4,6},{5,7},{6,4},{7,5},{8,10},{9,11},{10,... | collective-permute-start | bytes 1179656 | tf_op jit(solution)/shard_map/ppermute | solution.py:908
  112.8 17.7 %collective-permute-start.15 = (bf16[192,1024]{1,0:T(8,128)(2,1)S(1)}, bf16[192,1024]{1,0:T(8,128)(2,1)S(1)}, u32[]{:S(2)}, u32[]{:S(2)}) collective-permute-start(bf16[192,1024]{1,0:T(8,128)(2,1)S(1)} %add_convert_fusion.12), channel_id=1, source_target_pairs={{0,2},{1,3},{2,0},{3,1},{4,6},{5,7},{6,4},{7,5},{8,10},{9,11},{10,... | collective-permute-start | bytes 1179656 | tf_op jit(solution)/shard_map/ppermute | solution.py:908
  131.9 20.0 %collective-permute-start.16 = (bf16[384,1024]{1,0:T(8,128)(2,1)S(1)}, bf16[384,1024]{1,0:T(8,128)(2,1)S(1)}, u32[]{:S(2)}, u32[]{:S(2)}) collective-permute-start(bf16[384,1024]{1,0:T(8,128)(2,1)S(1)} %get-tuple-element.204.x1_ref.refs_5_), channel_id=1, source_target_pairs={{0,2},{1,3},{2,0},{3,1},{4,6},{5,7},{6,4},{7,5},{8,10},{9,11},{10,... | collective-permute-start | bytes 2359304 | tf_op jit(solution)/shard_map/ppermute | solution.py:908
  166.1 12.0 %collective-permute-start.21 = (bf16[192,1024]{1,0:T(8,128)(2,1)S(1)}, bf16[192,1024]{1,0:T(8,128)(2,1)S(1)}, u32[]{:S(2)}, u32[]{:S(2)}) collective-permute-start(bf16[192,1024]{1,0:T(8,128)(2,1)S(1)} %add_convert_fusion.11), channel_id=1, source_target_pairs={{0,2},{1,3},{2,0},{3,1},{4,6},{5,7},{6,4},{7,5},{8,10},{9,11},{10,... | collective-permute-start | bytes 1179656 | tf_op jit(solution)/shard_map/ppermute | solution.py:908
  168.0 17.7 %collective-permute-start.23 = (bf16[192,1024]{1,0:T(8,128)(2,1)S(1)}, bf16[192,1024]{1,0:T(8,128)(2,1)S(1)}, u32[]{:S(2)}, u32[]{:S(2)}) collective-permute-start(bf16[192,1024]{1,0:T(8,128)(2,1)S(1)} %add_convert_fusion.10), channel_id=1, source_target_pairs={{0,2},{1,3},{2,0},{3,1},{4,6},{5,7},{6,4},{7,5},{8,10},{9,11},{10,... | collective-permute-start | bytes 1179656 | tf_op jit(solution)/shard_map/ppermute | solution.py:908
  187.1 20.0 %collective-permute-start.26 = (bf16[384,1024]{1,0:T(8,128)(2,1)S(1)}, bf16[384,1024]{1,0:T(8,128)(2,1)S(1)}, u32[]{:S(2)}, u32[]{:S(2)}) collective-permute-start(bf16[384,1024]{1,0:T(8,128)(2,1)S(1)} %get-tuple-element.217.x1_ref.refs_9_), channel_id=1, source_target_pairs={{0,2},{1,3},{2,0},{3,1},{4,6},{5,7},{6,4},{7,5},{8,10},{9,11},{10,... | collective-permute-start | bytes 2359304 | tf_op jit(solution)/shard_map/ppermute | solution.py:908
  216.0 18.0 %collective-permute-start.31 = (bf16[192,1024]{1,0:T(8,128)(2,1)S(1)}, bf16[192,1024]{1,0:T(8,128)(2,1)S(1)}, u32[]{:S(2)}, u32[]{:S(2)}) collective-permute-start(bf16[192,1024]{1,0:T(8,128)(2,1)S(1)} %add_convert_fusion.8), channel_id=1, source_target_pairs={{0,2},{1,3},{2,0},{3,1},{4,6},{5,7},{6,4},{7,5},{8,10},{9,11},{10,... | collective-permute-start | bytes 1179656 | tf_op jit(solution)/shard_map/ppermute | solution.py:908
  236.8 20.0 %collective-permute-start.34 = (bf16[384,1024]{1,0:T(8,128)(2,1)S(1)}, bf16[384,1024]{1,0:T(8,128)(2,1)S(1)}, u32[]{:S(2)}, u32[]{:S(2)}) collective-permute-start(bf16[384,1024]{1,0:T(8,128)(2,1)S(1)} %get-tuple-element.231.g1_ref.refs_0_), channel_id=1, source_target_pairs={{0,2},{1,3},{2,0},{3,1},{4,6},{5,7},{6,4},{7,5},{8,10},{9,11},{10,... | collective-permute-start | bytes 2359304 | tf_op jit(solution)/shard_map/ppermute | solution.py:908
  264.8 15.0 %collective-permute-start.39 = (bf16[192,1024]{1,0:T(8,128)(2,1)}, bf16[192,1024]{1,0:T(8,128)(2,1)}, u32[]{:S(2)}, u32[]{:S(2)}) collective-permute-start(bf16[192,1024]{1,0:T(8,128)(2,1)} %add_convert_fusion.6), channel_id=1, source_target_pairs={{0,2},{1,3},{2,0},{3,1},{4,6},{5,7},{6,4},{7,5},{8,10},{9,11},{10,... | collective-permute-start | bytes 1179656 | tf_op jit(solution)/shard_map/ppermute | solution.py:908
  279.9 170.2 %reduce-scatter.7.cloned.1.call-start = ((), (), s32[]{:S(2)}) async-start(), calls=%async_computation.5 | async-start | bytes 1769472 | tf_op jit(solution)/shard_map/reduce_scatter | solution.py:960
  296.0 20.0 %collective-permute-start.40 = (bf16[384,1024]{1,0:T(8,128)(2,1)S(1)}, bf16[384,1024]{1,0:T(8,128)(2,1)S(1)}, u32[]{:S(2)}, u32[]{:S(2)}) collective-permute-start(bf16[384,1024]{1,0:T(8,128)(2,1)S(1)} %get-tuple-element.253.x1_ref.refs_0_), channel_id=1, source_target_pairs={{0,2},{1,3},{2,0},{3,1},{4,6},{5,7},{6,4},{7,5},{8,10},{9,11},{10,... | collective-permute-start | bytes 2359304 | tf_op jit(solution)/shard_map/ppermute | solution.py:908
  341.4 174.4 %reduce-scatter.9.cloned.1.call-start = ((), (), s32[]{:S(2)}) async-start(), calls=%async_computation.6 | async-start | bytes 2359296 | tf_op jit(solution)/shard_map/reduce_scatter | solution.py:960
  355.8 20.0 %collective-permute-start.48 = (bf16[384,1024]{1,0:T(8,128)(2,1)S(1)}, bf16[384,1024]{1,0:T(8,128)(2,1)S(1)}, u32[]{:S(2)}, u32[]{:S(2)}) collective-permute-start(bf16[384,1024]{1,0:T(8,128)(2,1)S(1)} %get-tuple-element.269.x1_ref.refs_0_), channel_id=1, source_target_pairs={{0,2},{1,3},{2,0},{3,1},{4,6},{5,7},{6,4},{7,5},{8,10},{9,11},{10,... | collective-permute-start | bytes 2359304 | tf_op jit(solution)/shard_map/ppermute | solution.py:908
  442.5 154.3 %reduce-scatter.11.cloned.1.call-start = ((), (), s32[]{:S(2)}) async-start(), calls=%async_computation.7 | async-start | bytes 2359296 | tf_op jit(solution)/shard_map/reduce_scatter | solution.py:960
  464.7 20.0 %collective-permute-start.58 = (bf16[384,1024]{1,0:T(8,128)(2,1)S(1)}, bf16[384,1024]{1,0:T(8,128)(2,1)S(1)}, u32[]{:S(2)}, u32[]{:S(2)}) collective-permute-start(bf16[384,1024]{1,0:T(8,128)(2,1)S(1)} %get-tuple-element.293.g1_ref.refs_0_), channel_id=1, source_target_pairs={{0,2},{1,3},{2,0},{3,1},{4,6},{5,7},{6,4},{7,5},{8,10},{9,11},{10,... | collective-permute-start | bytes 2359304 | tf_op jit(solution)/shard_map/ppermute | solution.py:908
  493.5 18.0 %collective-permute-start.61 = (bf16[192,1024]{1,0:T(8,128)(2,1)}, bf16[192,1024]{1,0:T(8,128)(2,1)}, u32[]{:S(2)}, u32[]{:S(2)}) collective-permute-start(bf16[192,1024]{1,0:T(8,128)(2,1)} %add_convert_fusion.1), channel_id=1, source_target_pairs={{0,2},{1,3},{2,0},{3,1},{4,6},{5,7},{6,4},{7,5},{8,10},{9,11},{10,... | collective-permute-start | bytes 1179656 | tf_op jit(solution)/shard_map/ppermute | solution.py:908
  518.1 29.0 %collective-permute-start.62 = (bf16[2,2,128,1024]{3,2,0,1:T(8,128)(2,1)}, bf16[2,2,128,1024]{3,2,0,1:T(8,128)(2,1)}, u32[]{:S(2)}, u32[]{:S(2)}) collective-permute-start(bf16[2,2,128,1024]{3,2,0,1:T(8,128)(2,1)} %bitcast.48), channel_id=1, source_target_pairs={{0,4},{4,0},{8,12},{12,8},{16,20},{20,16},{24,28},{28,24},{1,5},{5... | collective-permute-start | bytes 3145736 | tf_op jit(solution)/shard_map/ppermute | solution.py:908
  527.1 22.7 %collective-permute-start.64 = (bf16[192,1024]{1,0:T(8,128)(2,1)S(1)}, bf16[192,1024]{1,0:T(8,128)(2,1)S(1)}, u32[]{:S(2)}, u32[]{:S(2)}) collective-permute-start(bf16[192,1024]{1,0:T(8,128)(2,1)S(1)} %add_convert_fusion), channel_id=1, source_target_pairs={{0,2},{1,3},{2,0},{3,1},{4,6},{5,7},{6,4},{7,5},{8,10},{9,11},{10,... | collective-permute-start | bytes 1179656 | tf_op jit(solution)/shard_map/ppermute | solution.py:908
  560.8 18.2 %collective-permute-start.70 = (bf16[2,128,1024]{2,1,0:T(8,128)(2,1)S(1)}, bf16[2,128,1024]{2,1,0:T(8,128)(2,1)S(1)}, u32[]{:S(2)}, u32[]{:S(2)}) collective-permute-start(bf16[2,128,1024]{2,1,0:T(8,128)(2,1)S(1)} %copy-done.194), channel_id=1, source_target_pairs={{0,8},{4,12},{8,0},{12,4},{16,24},{20,28},{24,16},{28,20},{1,9},{5... | collective-permute-start | bytes 1572872 | tf_op jit(solution)/shard_map/ppermute | solution.py:908
  579.3 19.5 %collective-permute-start.71 = (bf16[128,1024]{1,0:T(8,128)(2,1)S(1)}, bf16[128,1024]{1,0:T(8,128)(2,1)S(1)}, u32[]{:S(2)}, u32[]{:S(2)}) collective-permute-start(bf16[128,1024]{1,0:T(8,128)(2,1)S(1)} %dynamic-slice_bitcast_fusion.1), channel_id=1, source_target_pairs={{0,16},{4,20},{8,24},{12,28},{16,0},{20,4},{24,8},{28,12},{1,17},{... | collective-permute-start | bytes 786440 | tf_op jit(solution)/shard_map/ppermute | solution.py:908
  (252 other events, 1744.6 us)
Sparse Core Ops, SparseCore 0:
  280.0 89.6 reduce-scatter.4
  373.5 64.7 reduce-scatter.6
  442.6 73.1 reduce-scatter.8
  519.2 77.5 reduce-scatter.10
